TPU v7x, 32 devices: a whole 2x2x4 slice. The times are simulated.
32 devices in a mesh: fsdp: 8 (over y, x, core), seq: 4 (over z).
Axes of the slice: x: 2, y: 2, z: 4, core: 2. Of those that a mesh axis runs over, the one named last changes fastest.
Arguments:
- layer_input: bfloat16 [16, 2048, 512], P('fsdp', 'seq'), may hold values from -6 to 6
- neighbour_ids: int32 [16, 2048, 4], P('fsdp', 'seq'), may hold values from 0 to 2047, as said below
- out_grad: bfloat16 [16, 2048, 512], P('fsdp', 'seq'), may hold values from -6 to 6
- attn_norm_gain: bfloat16 [512], P('fsdp'), may hold values from 0.099609375 to 1.8984375
- attn_norm_bias: bfloat16 [512], P('fsdp'), may hold values from -3 to 3
- attn_project: bfloat16 [512, 1536], P('fsdp'), may hold values from -0.25 to 0.25
- attn_merge: bfloat16 [512, 512], P('fsdp'), may hold values from -2 to 2
- position_bias: bfloat16 [256], P('fsdp'), may hold values from -4 to 4
- ffn_norm_gain: bfloat16 [512], P('fsdp'), may hold values from 0.099609375 to 1.8984375
- ffn_norm_bias: bfloat16 [512], P('fsdp'), may hold values from -3 to 3
- ffn_expand: bfloat16 [512, 2048], P('fsdp'), may hold values from -0.25 to 0.25
- expand_bias: bfloat16 [2048], P('fsdp'), may hold values from -3 to 3
- ffn_reduce: bfloat16 [2048, 512], P('fsdp'), may hold values from -0.125 to 0.125
- reduce_bias: bfloat16 [512], P('fsdp'), may hold values from -3 to 3
- near_query: bfloat16 [512, 512], P('fsdp'), may hold values from -0.25 to 0.25
- near_keys: bfloat16 [512, 1024], P('fsdp'), may hold values from -0.25 to 0.25
- near_merge: bfloat16 [512, 512], P('fsdp'), may hold values from -0.375 to 0.375
- gate_vector: bfloat16 [512], P('fsdp'), may hold values from -0.1875 to 0.1875
Outputs:
- layer_output: bfloat16 [16, 2048, 512], P('fsdp', 'seq')
- input_grad: float32 [16, 2048, 512], P('fsdp', 'seq')
- grad_attn_norm_gain: float32 [512], P('fsdp')
- grad_attn_norm_bias: float32 [512], P('fsdp')
- grad_attn_project: float32 [512, 1536], P('fsdp')
- grad_attn_merge: float32 [512, 512], P('fsdp')
- grad_position_bias: float32 [256], P('fsdp')
- grad_ffn_norm_gain: float32 [512], P('fsdp')
- grad_ffn_norm_bias: float32 [512], P('fsdp')
- grad_ffn_expand: float32 [512, 2048], P('fsdp')
- grad_expand_bias: float32 [2048], P('fsdp')
- grad_ffn_reduce: float32 [2048, 512], P('fsdp')
- grad_reduce_bias: float32 [512], P('fsdp')
- grad_near_query: float32 [512, 512], P('fsdp')
- grad_near_keys: float32 [512, 1024], P('fsdp')
- grad_near_merge: float32 [512, 512], P('fsdp')
- grad_gate_vector: float32 [512], P('fsdp')
Inputs may be any that keep to these rules, and one draw needn't show every extreme that they name: neighbour_ids[s, t, k] names a place of sequence s that is not later than t; the last token of a sequence names itself among its neighbours.
All inputs are finite; a program needn't handle non-finite values.
Results may differ from a plain program's by a relative error of at most 0.025.
Values may be sent and summed in bfloat16 or wider, within the bound.
No kernel may reach another device: no remote copies, remote signals or barrier semaphores. Data moves between devices by JAX's collectives and lax.ppermute only.
A program may use at most 320 MiB of HBM per device.

v0:
```python
import math

import jax
import jax.numpy as jnp
from jax import lax
from jax.sharding import PartitionSpec as P

D = 512
H = 8
HD = 64
K = 4
SEG = 512
NB = 32


EPS = 1e-05
HIGH = lax.Precision.HIGHEST
MASKED = -1000000000.0


def from_behind(block, axis, distance):
    devices = range(lax.axis_size(axis))
    route = [(i - distance, i) for i in devices if i - distance in devices]
    return lax.ppermute(block, axis, route)


def thresholds(seg_len, bucket_count):
    half_count = bucket_count // 2
    spread_ratio = 2.0 * seg_len / half_count
    exact_part = list(range(1, half_count))
    log_part = [
        int(half_count * spread_ratio ** ((bucket_index - half_count) / half_count))
        for bucket_index in range(half_count, bucket_count)
    ]
    return exact_part + log_part


def bucket_grid(row_start, row_count):
    query_pos = lax.broadcasted_iota(jnp.int32, (row_count, 2 * SEG), 0) + row_start
    key_pos = lax.broadcasted_iota(jnp.int32, (row_count, 2 * SEG), 1)
    distance = query_pos - key_pos + SEG
    bucket = jnp.zeros((row_count, 2 * SEG), jnp.int32)
    for threshold in thresholds(SEG, NB):
        bucket = bucket + (distance >= threshold).astype(jnp.int32)
    return (distance, bucket)


def bucket_onehot(block_index, block_rows):
    distance, bucket = bucket_grid(block_index * block_rows, block_rows)
    return (bucket[:, :, None] == lax.broadcasted_iota(jnp.int32, (1, 1, NB), 2)).astype(
        jnp.float32
    )


def make_bias(rel_table):
    block_rows = min(64, SEG)
    pieces = []
    for block_index in range(SEG // block_rows):
        onehot = bucket_onehot(block_index, block_rows)
        pieces.append(jnp.einsum("qkb,bh->hqk", onehot, rel_table, precision=HIGH))
    return jnp.concatenate(pieces, axis=1)


def bias_grad(grid):
    block_rows = min(64, SEG)
    table_grad = jnp.zeros((NB, H), jnp.float32)
    for block_index in range(SEG // block_rows):
        onehot = bucket_onehot(block_index, block_rows)
        part_grid = grid[:, block_index * block_rows : (block_index + 1) * block_rows]
        table_grad = table_grad + jnp.einsum("hqk,qkb->bh", part_grid, onehot, precision=HIGH)
    return table_grad


def gelu_slope(values):
    normal_cdf = 0.5 * (1.0 + jax.scipy.special.erf(values * (1.0 / math.sqrt(2.0))))
    return normal_cdf + values * jnp.exp(-0.5 * values * values) * (1.0 / math.sqrt(2.0 * math.pi))


def norm_forward(values, gain, shift):
    average = jnp.mean(values, axis=-1, keepdims=True)
    centred = values - average
    variance = jnp.mean(centred * centred, axis=-1, keepdims=True)
    rstd_value = lax.rsqrt(variance + EPS)
    hat_value = centred * rstd_value
    return (hat_value * gain + shift, hat_value, rstd_value)


def norm_backward(grad_result, hat_value, rstd_value, gain):
    scaled = grad_result * gain
    grad_input = rstd_value * (
        scaled
        - jnp.mean(scaled, axis=-1, keepdims=True)
        - hat_value * jnp.mean(scaled * hat_value, axis=-1, keepdims=True)
    )
    return (grad_input, jnp.sum(grad_result * hat_value, axis=0), jnp.sum(grad_result, axis=0))


def dot_plain(left, right):
    return jnp.dot(left, right, preferred_element_type=jnp.float32)


def dot_rows(left, right):
    return lax.dot_general(
        left, right, (((0,), (0,)), ((), ())), preferred_element_type=jnp.float32
    )


def dot_back(left, weight):
    return lax.dot_general(
        left, weight, (((1,), (1,)), ((), ())), preferred_element_type=jnp.float32
    )


def collect(shards):
    return (
        lax.all_gather(shards[0], "fsdp", axis=0, tiled=True),
        lax.all_gather(shards[1], "fsdp", axis=0, tiled=True),
        lax.all_gather(shards[2], "fsdp", axis=0, tiled=True),
        lax.all_gather(shards[3], "fsdp", axis=0, tiled=True),
        lax.all_gather(shards[4], "fsdp", axis=0, tiled=True),
        lax.all_gather(shards[5], "fsdp", axis=0, tiled=True),
        lax.all_gather(shards[6], "fsdp", axis=0, tiled=True),
        lax.all_gather(shards[7], "fsdp", axis=0, tiled=True),
        lax.all_gather(shards[8], "fsdp", axis=0, tiled=True),
        lax.all_gather(shards[9], "fsdp", axis=0, tiled=True),
        lax.all_gather(shards[10], "fsdp", axis=0, tiled=True),
        lax.all_gather(shards[11], "fsdp", axis=0, tiled=True),
        lax.all_gather(shards[12], "fsdp", axis=0, tiled=True),
        lax.all_gather(shards[13], "fsdp", axis=0, tiled=True),
        lax.all_gather(shards[14], "fsdp", axis=0, tiled=True),
    )


def on_device(
    layer_input,
    neighbour_ids,
    out_grad,
    attn_norm_gain,
    attn_norm_bias,
    attn_project,
    attn_merge,
    position_bias,
    ffn_norm_gain,
    ffn_norm_bias,
    ffn_expand,
    expand_bias,
    ffn_reduce,
    reduce_bias,
    near_query,
    near_keys,
    near_merge,
    gate_vector,
):
    shards = (
        attn_norm_gain,
        attn_norm_bias,
        attn_project,
        attn_merge,
        position_bias,
        ffn_norm_gain,
        ffn_norm_bias,
        ffn_expand,
        expand_bias,
        ffn_reduce,
        reduce_bias,
        near_query,
        near_keys,
        near_merge,
        gate_vector,
    )
    batch_count = layer_input.shape[0]
    seg_index = lax.axis_index("seq")
    seg_count = lax.axis_size("seq")
    seq_length = SEG * seg_count
    score_scale = HD ** (-0.5)
    flat_ids = neighbour_ids.reshape(batch_count, SEG * K)
    shard_piece = lax.all_gather(layer_input, "seq", axis=1, tiled=True)
    piece_rows = shard_piece.shape[1]
    inside = (flat_ids >= 0) & (flat_ids < piece_rows)
    taken_rows = jnp.take_along_axis(
        shard_piece, jnp.clip(flat_ids, 0, piece_rows - 1)[:, :, None], axis=1
    )
    neighbours = jnp.where(
        inside[:, :, None], taken_rows, jnp.zeros((batch_count, SEG * K, D), jnp.bfloat16)
    )
    distance, bucket = bucket_grid(0, SEG)
    key_pos = lax.broadcasted_iota(jnp.int32, (SEG, 2 * SEG), 1)
    allowed = jnp.where(key_pos < SEG, seg_index > 0, distance >= 0)[None]
    outputs = []
    input_grads = []
    neighbour_grads = []
    grad_totals = None
    grid_sum = jnp.zeros((H, SEG, 2 * SEG), jnp.float32)
    bias_grid = None
    for m in range(batch_count):
        gathered = collect(shards)
        (
            attn_gain,
            attn_shift,
            attn_proj_w,
            attn_merge_w,
            position_flat,
            ffn_gain,
            ffn_shift,
            ffn_expand_w,
            expand_bias_w,
            ffn_reduce_w,
            reduce_bias_w,
            near_query_w,
            near_keys_w,
            near_merge_w,
            gate_w,
        ) = gathered
        if bias_grid is None:
            bias_grid = make_bias(position_flat.reshape(NB, H).astype(jnp.float32))
        attn_gain_f = attn_gain.astype(jnp.float32)
        ffn_gain_f = ffn_gain.astype(jnp.float32)
        gate_float = gate_w.astype(jnp.float32)
        inputs = layer_input[m]
        normed, attn_hat, attn_rstd = norm_forward(
            inputs.astype(jnp.float32), attn_gain_f, attn_shift.astype(jnp.float32)
        )
        normed_low = normed.astype(jnp.bfloat16)
        joined_rows = dot_plain(normed_low, attn_proj_w).astype(jnp.bfloat16)
        previous = from_behind(normed_low, "seq", 1)
        memory = dot_plain(previous, attn_proj_w[:, D:]).astype(jnp.bfloat16)
        queries = joined_rows[:, :D].reshape(SEG, H, HD)
        key_all = jnp.concatenate([memory[:, :D], joined_rows[:, D : 2 * D]], axis=0).reshape(
            2 * SEG, H, HD
        )
        value_all = jnp.concatenate([memory[:, D:], joined_rows[:, 2 * D :]], axis=0).reshape(
            2 * SEG, H, HD
        )
        scores = (
            jnp.einsum("qhd,khd->hqk", queries, key_all, preferred_element_type=jnp.float32)
            * score_scale
            + bias_grid
        )
        scores = jnp.where(allowed, scores, MASKED)
        row_max = jnp.max(scores, axis=-1, keepdims=True)
        log_total = row_max + jnp.log(jnp.sum(jnp.exp(scores - row_max), axis=-1, keepdims=True))
        probs_low = jnp.exp(scores - log_total).astype(jnp.bfloat16)
        attended = (
            jnp.einsum("hqk,khd->qhd", probs_low, value_all, preferred_element_type=jnp.float32)
            .reshape(SEG, D)
            .astype(jnp.bfloat16)
        )
        after_attn = inputs.astype(jnp.float32) + dot_plain(attended, attn_merge_w)
        ffn_normed, ffn_hat, ffn_rstd = norm_forward(
            after_attn, ffn_gain_f, ffn_shift.astype(jnp.float32)
        )
        ffn_normed_low = ffn_normed.astype(jnp.bfloat16)
        pre_active = dot_plain(ffn_normed_low, ffn_expand_w) + expand_bias_w.astype(jnp.float32)
        active = jax.nn.gelu(pre_active, approximate=False).astype(jnp.bfloat16)
        after_ffn = after_attn + dot_plain(active, ffn_reduce_w) + reduce_bias_w.astype(jnp.float32)
        hidden_low = after_ffn.astype(jnp.bfloat16)
        near_queries = dot_plain(hidden_low, near_query_w).astype(jnp.bfloat16).reshape(SEG, H, HD)
        near_rows = neighbours[m]
        near_kv = dot_plain(near_rows, near_keys_w).astype(jnp.bfloat16).reshape(SEG, K, 2, H, HD)
        near_key = near_kv[:, :, 0]
        near_value = near_kv[:, :, 1]
        near_scores = (
            jnp.einsum("thd,tkhd->thk", near_queries, near_key, preferred_element_type=jnp.float32)
            * score_scale
        )
        near_probs = jax.nn.softmax(near_scores, axis=-1)
        near_mixed = jnp.einsum(
            "thk,tkhd->thd", near_probs, near_value.astype(jnp.float32), precision=HIGH
        )
        mixed_low = near_mixed.reshape(SEG, D).astype(jnp.bfloat16)
        near_out = dot_plain(mixed_low, near_merge_w)
        gate_value = jax.nn.sigmoid(jnp.sum(after_ffn * gate_float, axis=-1, keepdims=True))
        outputs.append(
            (gate_value * after_ffn + (1.0 - gate_value) * near_out).astype(jnp.bfloat16)
        )
        gathered = collect(shards)
        (
            attn_gain,
            attn_shift,
            attn_proj_w,
            attn_merge_w,
            position_flat,
            ffn_gain,
            ffn_shift,
            ffn_expand_w,
            expand_bias_w,
            ffn_reduce_w,
            reduce_bias_w,
            near_query_w,
            near_keys_w,
            near_merge_w,
            gate_w,
        ) = gathered
        grad_result = out_grad[m].astype(jnp.float32)
        gate_grad = (
            jnp.sum(grad_result * (after_ffn - near_out), axis=-1, keepdims=True)
            * gate_value
            * (1.0 - gate_value)
        )
        g_gate = jnp.sum(gate_grad * after_ffn, axis=0)
        grad_near_out = ((1.0 - gate_value) * grad_result).astype(jnp.bfloat16)
        g_near_merge = dot_rows(mixed_low, grad_near_out)
        grad_mixed = dot_back(grad_near_out, near_merge_w).astype(jnp.bfloat16).reshape(SEG, H, HD)
        grad_near_probs = jnp.einsum(
            "thd,tkhd->thk", grad_mixed, near_value, preferred_element_type=jnp.float32
        )
        grad_near_value = jnp.einsum(
            "thk,thd->tkhd", near_probs, grad_mixed.astype(jnp.float32), precision=HIGH
        )
        grad_near_scores = near_probs * (
            grad_near_probs - jnp.sum(near_probs * grad_near_probs, axis=-1, keepdims=True)
        )
        grad_near_query = (
            jnp.einsum(
                "thk,tkhd->thd", grad_near_scores, near_key.astype(jnp.float32), precision=HIGH
            )
            * score_scale
        )
        grad_near_key = (
            jnp.einsum(
                "thk,thd->tkhd", grad_near_scores, near_queries.astype(jnp.float32), precision=HIGH
            )
            * score_scale
        )
        near_q_grad = grad_near_query.reshape(SEG, D).astype(jnp.bfloat16)
        near_kv_grad = (
            jnp.concatenate(
                [grad_near_key.reshape(SEG, K, D), grad_near_value.reshape(SEG, K, D)], axis=-1
            )
            .reshape(SEG * K, 2 * D)
            .astype(jnp.bfloat16)
        )
        g_near_query = dot_rows(hidden_low, near_q_grad)
        g_near_keys = dot_rows(near_rows, near_kv_grad)
        neighbour_grads.append(dot_back(near_kv_grad, near_keys_w))
        grad_after_ffn = (
            gate_value * grad_result + gate_grad * gate_float + dot_back(near_q_grad, near_query_w)
        )
        ffn_out_grad = grad_after_ffn.astype(jnp.bfloat16)
        g_reduce_bias = jnp.sum(ffn_out_grad.astype(jnp.float32), axis=0)
        g_ffn_reduce = dot_rows(active, ffn_out_grad)
        pre_grad = (dot_back(ffn_out_grad, ffn_reduce_w) * gelu_slope(pre_active)).astype(
            jnp.bfloat16
        )
        g_expand_bias = jnp.sum(pre_grad.astype(jnp.float32), axis=0)
        g_ffn_expand = dot_rows(ffn_normed_low, pre_grad)
        norm_two_grad, g_ffn_gain, g_ffn_shift = norm_backward(
            dot_back(pre_grad, ffn_expand_w), ffn_hat, ffn_rstd, ffn_gain_f
        )
        grad_after_attn = grad_after_ffn + norm_two_grad
        merge_grad = grad_after_attn.astype(jnp.bfloat16)
        g_attn_merge = dot_rows(attended, merge_grad)
        grad_attended = dot_back(merge_grad, attn_merge_w).astype(jnp.bfloat16).reshape(SEG, H, HD)
        scores = (
            jnp.einsum("qhd,khd->hqk", queries, key_all, preferred_element_type=jnp.float32)
            * score_scale
            + bias_grid
        )
        attn_probs = jnp.exp(jnp.where(allowed, scores, MASKED) - log_total)
        grad_probs = jnp.einsum(
            "qhd,khd->hqk", grad_attended, value_all, preferred_element_type=jnp.float32
        )
        row_delta = jnp.sum(attn_probs * grad_probs, axis=-1, keepdims=True)
        grad_scores = (attn_probs * (grad_probs - row_delta)).astype(jnp.bfloat16)
        grid_sum = grid_sum + grad_scores.astype(jnp.float32)
        grad_queries = (
            jnp.einsum("hqk,khd->qhd", grad_scores, key_all, preferred_element_type=jnp.float32)
            * score_scale
        )
        grad_keys = (
            jnp.einsum("hqk,qhd->khd", grad_scores, queries, preferred_element_type=jnp.float32)
            * score_scale
        )
        grad_values = jnp.einsum(
            "hqk,qhd->khd",
            attn_probs.astype(jnp.bfloat16),
            grad_attended,
            preferred_element_type=jnp.float32,
        )
        memory_grad = jnp.concatenate(
            [grad_keys[:SEG].reshape(SEG, D), grad_values[:SEG].reshape(SEG, D)], axis=-1
        )
        returned = from_behind(memory_grad.astype(jnp.bfloat16), "seq", -1).astype(
            memory_grad.dtype
        )
        grad_joined = jnp.concatenate(
            [
                grad_queries.reshape(SEG, D),
                grad_keys[SEG:].reshape(SEG, D) + returned[:, :D],
                grad_values[SEG:].reshape(SEG, D) + returned[:, D:],
            ],
            axis=-1,
        ).astype(jnp.bfloat16)
        g_attn_project = dot_rows(normed_low, grad_joined)
        norm_one_grad, g_attn_gain, g_attn_shift = norm_backward(
            dot_back(grad_joined, attn_proj_w), attn_hat, attn_rstd, attn_gain_f
        )
        input_grads.append(grad_after_attn + norm_one_grad)
        fresh = [
            g_attn_gain,
            g_attn_shift,
            g_attn_project,
            g_attn_merge,
            None,
            g_ffn_gain,
            g_ffn_shift,
            g_ffn_expand,
            g_expand_bias,
            g_ffn_reduce,
            g_reduce_bias,
            g_near_query,
            g_near_keys,
            g_near_merge,
            g_gate,
        ]
        if grad_totals is None:
            grad_totals = fresh
        else:
            grad_totals = [
                None if older is None else older + newer for older, newer in zip(grad_totals, fresh)
            ]
    grad_totals[4] = bias_grad(grid_sum).reshape(NB * H)
    batch_index = lax.broadcasted_iota(jnp.int32, (batch_count, SEG * K), 0)
    spread_grad = (
        jnp.zeros((batch_count, seq_length, D), jnp.float32)
        .at[batch_index, flat_ids]
        .add(jnp.stack(neighbour_grads))
    )
    own_grad = lax.psum_scatter(
        spread_grad.astype(jnp.bfloat16), "seq", scatter_dimension=1, tiled=True
    ).astype(jnp.float32)
    input_grad = jnp.stack(input_grads) + own_grad
    owned = (
        lax.psum_scatter(
            grad_totals[0].astype(jnp.bfloat16), "fsdp", scatter_dimension=0, tiled=True
        ).astype(jnp.float32),
        lax.psum_scatter(
            grad_totals[1].astype(jnp.bfloat16), "fsdp", scatter_dimension=0, tiled=True
        ).astype(jnp.float32),
        lax.psum_scatter(
            grad_totals[2].astype(jnp.bfloat16), "fsdp", scatter_dimension=0, tiled=True
        ).astype(jnp.float32),
        lax.psum_scatter(
            grad_totals[3].astype(jnp.bfloat16), "fsdp", scatter_dimension=0, tiled=True
        ).astype(jnp.float32),
        lax.psum_scatter(
            grad_totals[4].astype(jnp.bfloat16), "fsdp", scatter_dimension=0, tiled=True
        ).astype(jnp.float32),
        lax.psum_scatter(
            grad_totals[5].astype(jnp.bfloat16), "fsdp", scatter_dimension=0, tiled=True
        ).astype(jnp.float32),
        lax.psum_scatter(
            grad_totals[6].astype(jnp.bfloat16), "fsdp", scatter_dimension=0, tiled=True
        ).astype(jnp.float32),
        lax.psum_scatter(
            grad_totals[7].astype(jnp.bfloat16), "fsdp", scatter_dimension=0, tiled=True
        ).astype(jnp.float32),
        lax.psum_scatter(
            grad_totals[8].astype(jnp.bfloat16), "fsdp", scatter_dimension=0, tiled=True
        ).astype(jnp.float32),
        lax.psum_scatter(
            grad_totals[9].astype(jnp.bfloat16), "fsdp", scatter_dimension=0, tiled=True
        ).astype(jnp.float32),
        lax.psum_scatter(
            grad_totals[10].astype(jnp.bfloat16), "fsdp", scatter_dimension=0, tiled=True
        ).astype(jnp.float32),
        lax.psum_scatter(
            grad_totals[11].astype(jnp.bfloat16), "fsdp", scatter_dimension=0, tiled=True
        ).astype(jnp.float32),
        lax.psum_scatter(
            grad_totals[12].astype(jnp.bfloat16), "fsdp", scatter_dimension=0, tiled=True
        ).astype(jnp.float32),
        lax.psum_scatter(
            grad_totals[13].astype(jnp.bfloat16), "fsdp", scatter_dimension=0, tiled=True
        ).astype(jnp.float32),
        lax.psum_scatter(
            grad_totals[14].astype(jnp.bfloat16), "fsdp", scatter_dimension=0, tiled=True
        ).astype(jnp.float32),
    )
    reduced = (
        lax.psum(owned[0].astype(jnp.bfloat16), "seq").astype(jnp.float32),
        lax.psum(owned[1].astype(jnp.bfloat16), "seq").astype(jnp.float32),
        lax.psum(owned[2].astype(jnp.bfloat16), "seq").astype(jnp.float32),
        lax.psum(owned[3].astype(jnp.bfloat16), "seq").astype(jnp.float32),
        lax.psum(owned[4].astype(jnp.bfloat16), "seq").astype(jnp.float32),
        lax.psum(owned[5].astype(jnp.bfloat16), "seq").astype(jnp.float32),
        lax.psum(owned[6].astype(jnp.bfloat16), "seq").astype(jnp.float32),
        lax.psum(owned[7].astype(jnp.bfloat16), "seq").astype(jnp.float32),
        lax.psum(owned[8].astype(jnp.bfloat16), "seq").astype(jnp.float32),
        lax.psum(owned[9].astype(jnp.bfloat16), "seq").astype(jnp.float32),
        lax.psum(owned[10].astype(jnp.bfloat16), "seq").astype(jnp.float32),
        lax.psum(owned[11].astype(jnp.bfloat16), "seq").astype(jnp.float32),
        lax.psum(owned[12].astype(jnp.bfloat16), "seq").astype(jnp.float32),
        lax.psum(owned[13].astype(jnp.bfloat16), "seq").astype(jnp.float32),
        lax.psum(owned[14].astype(jnp.bfloat16), "seq").astype(jnp.float32),
    )
    return (
        jnp.stack(outputs),
        input_grad,
        reduced[0],
        reduced[1],
        reduced[2],
        reduced[3],
        reduced[4],
        reduced[5],
        reduced[6],
        reduced[7],
        reduced[8],
        reduced[9],
        reduced[10],
        reduced[11],
        reduced[12],
        reduced[13],
        reduced[14],
    )


def solution(mesh):
    in_specs = (
        P("fsdp", "seq", None),
        P("fsdp", "seq", None),
        P("fsdp", "seq", None),
        P("fsdp"),
        P("fsdp"),
        P("fsdp", None),
        P("fsdp", None),
        P("fsdp"),
        P("fsdp"),
        P("fsdp"),
        P("fsdp", None),
        P("fsdp"),
        P("fsdp", None),
        P("fsdp"),
        P("fsdp", None),
        P("fsdp", None),
        P("fsdp", None),
        P("fsdp"),
    )
    out_specs = (
        P("fsdp", "seq", None),
        P("fsdp", "seq", None),
        P("fsdp"),
        P("fsdp"),
        P("fsdp", None),
        P("fsdp", None),
        P("fsdp"),
        P("fsdp"),
        P("fsdp"),
        P("fsdp", None),
        P("fsdp"),
        P("fsdp", None),
        P("fsdp"),
        P("fsdp", None),
        P("fsdp", None),
        P("fsdp", None),
        P("fsdp"),
    )
    return jax.shard_map(
        on_device, mesh=mesh, in_specs=in_specs, out_specs=out_specs, check_vma=False
    )
```

profile of v0, /device:TPU:0, one launch (start us, length us, event | category | flops | bytes accessed | tf_op | source)
XLA Modules:
  0.0 1011.6 jit_solution(5874684592545951952)
XLA Ops:
  18.6 15.5 %all-reduce.16 = (bf16[512]{0:T(512)(128)(2,1)S(1)}, bf16[512]{0:T(512)(128)(2,1)S(1)}, bf16[256]{0:T(256)(128)(2,1)S(1)}, bf16[512]{0:T(512)(128)(2,1)S(1)}, bf...) all-reduce(bf16[512]{0:T(512)(128)(2,1)S(1)} %dynamic-update-slice., ...), channel_id=1, replica_groups=mesh['fsdp'=8,'seq'=4] {'fsdp'}, use_global_device_ids=true, to_apply=%add.1 | all-reduce | flops 3328 | bytes 13312
  38.0 4.3 collective-permute-start.1
  46.4 7.8 all-gather
  65.2 11.0 %all_gather.36 = bf16[512,512]{1,0:T(8,128)(2,1)} all-gather(bf16[64,512]{1,0:T(8,128)(2,1)S(1)} %copy-done.114), channel_id=1, replica_groups=mesh['fsdp'=8,'seq'=4] {'fsdp'}, dimensions={0}, use_global_device_ids=true | all-gather | bytes 589824 | tf_op jit(solution)/shard_map/all_gather | solution.py:119
  76.3 11.1 %all_gather.88 = bf16[512,512]{1,0:T(8,128)(2,1)} all-gather(bf16[64,512]{1,0:T(8,128)(2,1)S(1)} %copy-done.115), channel_id=1, replica_groups=mesh['fsdp'=8,'seq'=4] {'fsdp'}, dimensions={0}, use_global_device_ids=true | all-gather | bytes 589824 | tf_op jit(solution)/shard_map/all_gather | solution.py:127
  115.7 4.3 copy_dynamic-update-slice_fusion.6
  135.5 10.4 %all_gather.91 = bf16[512,512]{1,0:T(8,128)(2,1)} all-gather(bf16[64,512]{1,0:T(8,128)(2,1)S(1)} %copy-done.116), channel_id=1, replica_groups=mesh['fsdp'=8,'seq'=4] {'fsdp'}, dimensions={0}, use_global_device_ids=true | all-gather | bytes 589824 | tf_op jit(solution)/shard_map/all_gather | solution.py:129
  175.8 11.2 %fusion.547 = (f32[8,512]{1,0:T(8,128)S(1)}, f32[8,512,1024]{2,1,0:T(8,128)}) fusion(f32[8,512,1024]{2,1,0:T(8,128)} %copy_dynamic-update-slice_fusion, bf16[512,8,64]{0,2,1:T(8,128)(2,1)S(1)} %bitcast.394, bf16[1024,8,64]{0,2,1:T(8,128)(2,1)S(1)} %bitcast.385, pred[512,1024]{1,0:T(8,128)(4,1)S(1)} %copy-done.48), kind=kOutput, calls=%fused_computation.723 | convolution fusion | flops 553644032 | bytes 35667968 | tf_op jit(solution)/shard_map/qhd,khd->hqk/dot_general | solution.py:235
  187.0 7.8 exponential_reduce_fusion
  194.9 14.1 %fusion.549 = (f32[8,512]{1,0:T(8,128)S(1)}, f32[8,512,1024]{2,1,0:T(8,128)}) fusion(f32[8,512,1024]{2,1,0:T(8,128)} %copy_dynamic-update-slice_fusion, bf16[512,8,64]{0,2,1:T(8,128)(2,1)S(1)} %bitcast.396, bf16[1024,8,64]{0,2,1:T(8,128)(2,1)} %bitcast.387, pred[512,1024]{1,0:T(8,128)(4,1)} %fusion.91), kind=kOutput, calls=%fused_computation.725 | convolution fusion | flops 553644032 | bytes 35667968 | tf_op jit(solution)/shard_map/qhd,khd->hqk/dot_general | solution.py:235
  209.0 8.8 exponential_reduce_fusion.1
  217.9 5.2 fusion.119
  225.2 8.7 fusion.116
  240.1 20.5 %fusion.25 = (bf16[512,2048]{1,0:T(8,128)(2,1)}, bf16[512,2048]{1,0:T(8,128)(2,1)}, f32[512,2048]{1,0:T(8,128)}) fusion(f32[2048]{0:T(1024)S(1)} %bitcast.427, f32[512,2048]{1,0:T(8,128)S(1)} %fusion.537, bf16[512,2048]{1,0:T(8,128)(2,1)S(1)} %copy-done.76, f32[512,512]{0,1:T(8,128)S(1)} %get-tuple-element.176, f32[512]{0:T(512)S(1)} %add_rsqrt_fusion, ...), kind=kOutput, calls=%fused_computation.63 | convolution fusion | flops 1213464576 | bytes 15745024 | tf_op jit(solution)/shard_map/dot_general | solution.py:99
  287.6 73.7 %gather_fusion = bf16[4096,512]{1,0:T(8,128)(2,1)} fusion(bf16[2,2048,512]{2,1,0:T(8,128)(2,1)} %all-gather.13.cloned.1.call-done, s32[4096]{0:T(1024)S(1)} %bitcast.376), kind=kCustom, calls=%fused_computation | custom fusion | bytes 8421376 | tf_op jit(solution)/shard_map/jit(take_along_axis)/gather | solution.py:180
  361.3 5.2 select_select_fusion
  366.6 6.1 convolution_convert_fusion
  372.7 11.6 %reshape.1327 = bf16[512,4,2,8,64]{4,3,2,1,0:T(8,128)(2,1)} reshape(bf16[2048,1024]{1,0:T(8,128)(2,1)} %convolution_convert_fusion) | data formatting | bytes 8388608 | tf_op jit(solution)/shard_map/reshape | solution.py:259
  384.3 9.5 multiply_reduce_fusion.3
  399.3 15.2 %multiply_reduce_fusion.2 = (f32[512,8,64]{2,1,0:T(8,128)}, bf16[512,8,64]{2,1,0:T(8,128)(2,1)}) fusion(f32[512,8,4]{1,2,0:T(4,128)S(1)} %subtract_multiply_fusion, bf16[512,4,2,8,64]{4,3,2,1,0:T(8,128)(2,1)} %reshape.1327, f32[512,8,4]{1,2,0:T(4,128)S(1)} %fusion.240), kind=kLoop, calls=%fused_computation.18 | loop fusion | flops 5767168 | bytes 5898240
  414.4 4.9 fusion.40
  419.4 4.4 convolution_convert_fusion.1
  423.8 11.7 %reshape.1322 = bf16[512,4,2,8,64]{4,3,2,1,0:T(8,128)(2,1)} reshape(bf16[2048,1024]{1,0:T(8,128)(2,1)} %convolution_convert_fusion.1) | data formatting | bytes 8388608 | tf_op jit(solution)/shard_map/reshape | solution.py:259
  448.3 5.2 convert_reduce_fusion
  458.9 9.0 multiply_reduce_fusion.5
  467.9 3.8 fusion.243
  474.8 15.3 %multiply_reduce_fusion.4 = (f32[512,8,64]{2,1,0:T(8,128)}, bf16[512,8,64]{2,1,0:T(8,128)(2,1)}) fusion(f32[512,8,4]{1,2,0:T(4,128)S(1)} %subtract_multiply_fusion.1, bf16[512,4,2,8,64]{4,3,2,1,0:T(8,128)(2,1)} %reshape.1322, f32[512,8,4]{1,2,0:T(4,128)S(1)} %copy-done.63), kind=kLoop, calls=%fused_computation.20 | loop fusion | flops 5767168 | bytes 5898240
  526.9 4.6 fusion.39
  531.6 4.8 fusion.38
  536.4 6.9 concatenate.65
  557.1 6.5 concatenate.63
  563.6 6.6 concatenate.62
  573.2 11.2 %multiply_reduce_fusion = (f32[8,512]{1,0:T(8,128)S(1)}, f32[8,512,1024]{2,1,0:T(8,128)}) fusion(f32[8,512,1024]{2,1,0:T(8,128)} %get-tuple-element.174, f32[8,512]{1,0:T(8,128)S(1)} %copy-done.105, bf16[512,8,64]{0,2,1:T(8,128)(2,1)S(1)} %bitcast.400, bf16[1024,8,64]{0,2,1:T(8,128)(2,1)S(1)} %bitcast.392), kind=kOutput, calls=%fused_computation.6 | convolution fusion | flops 549449728 | bytes 35160064 | tf_op jit(solution)/shard_map/qhd,khd->hqk/dot_general | solution.py:360
  584.4 4.6 fusion.41
  592.3 6.5 concatenate.66
  598.7 6.5 fusion.92
  608.7 6.3 add_convert_fusion.2
  615.3 5.7 add_convert_fusion.1
  620.9 11.3 %multiply_reduce_fusion.1 = (f32[8,512]{1,0:T(8,128)S(1)}, f32[8,512,1024]{2,1,0:T(8,128)}) fusion(f32[8,512,1024]{2,1,0:T(8,128)} %get-tuple-element.178, f32[8,512]{1,0:T(8,128)S(1)} %copy-done.107, bf16[512,8,64]{0,2,1:T(8,128)(2,1)S(1)} %bitcast.398, bf16[1024,8,64]{0,2,1:T(8,128)(2,1)S(1)} %bitcast.390), kind=kOutput, calls=%fused_computation.8 | convolution fusion | flops 549449728 | bytes 35160064 | tf_op jit(solution)/shard_map/qhd,khd->hqk/dot_general | solution.py:360
  632.3 34.4 %convert_add_fusion = (f32[8,512,1024]{2,1,0:T(8,128)}, bf16[8,512,1024]{2,1,0:T(8,128)(2,1)}, bf16[8,512,1024]{2,1,0:T(8,128)(2,1)}) fusion(f32[8,512,1024]{2,1,0:T(8,128)} %get-tuple-element.184, f32[8,512]{1,0:T(8,128)S(1)} %get-tuple-element.183, f32[8,512,1024]{2,1,0:T(8,128)} %get-tuple-element.178, f32[8,512]{1,0:T(8,128)S(1)} %copy-done.107, ...), kind=kLoop, calls=%fused_computation.4 | loop fusion | flops 46137344 | bytes 100728832 | tf_op jit(solution)/shard_map/add | solution.py:365
  666.7 7.7 fusion.94
  676.4 8.0 fusion.97
  693.7 5.1 multiply_bitcast_fusion
  707.7 19.5 %collective-permute-done.2 = bf16[512,1024]{0,1:T(8,128)(2,1)S(1)} collective-permute-done((bf16[512,1024]{0,1:T(8,128)(2,1)S(1)}, bf16[512,1024]{0,1:T(8,128)(2,1)S(1)}, u32[]{:S(2)}, u32[]{:S(2)}) %collective-permute-start.2) | collective-permute-done | bytes 1048608 | tf_op jit(solution)/shard_map/ppermute | solution.py:24
  727.5 21.2 %collective-permute-done.3 = bf16[512,1024]{0,1:T(8,128)(2,1)S(1)} collective-permute-done((bf16[512,1024]{0,1:T(8,128)(2,1)S(1)}, bf16[512,1024]{0,1:T(8,128)(2,1)S(1)}, u32[]{:S(2)}, u32[]{:S(2)}) %collective-permute-start.3) | collective-permute-done | bytes 1048608 | tf_op jit(solution)/shard_map/ppermute | solution.py:24
  757.3 29.5 %reduce-scatter.17.cloned.1.call-done = bf16[256,512]{1,0:T(8,128)(2,1)} async-done(((bf16[2048,512]{1,0:T(8,128)(2,1)}), bf16[256,512]{1,0:T(8,128)(2,1)}) %reduce-scatter.17.cloned.1.call-update) | async-done | bytes 262160 | tf_op jit(solution)/shard_map/reduce_scatter | solution.py:461
  786.8 42.6 %reduce-scatter.11.cloned.1.call-done = bf16[64,1536]{1,0:T(8,128)(2,1)} async-done(((bf16[512,1536]{1,0:T(8,128)(2,1)}), bf16[64,1536]{1,0:T(8,128)(2,1)}) %reduce-scatter.11.cloned.1.call-update) | async-done | bytes 196624 | tf_op jit(solution)/shard_map/reduce_scatter | solution.py:440
  829.8 4.8 convolution_bitcast_fusion
  837.2 4.3 pad_maximum_fusion
  841.4 29.0 %scatter_custom_fusion = f32[4096,512]{1,0:T(8,128)} fusion(s32[4096]{0:T(1024)S(1)} %bitcast.426, f32[4096,512]{1,0:T(8,128)} %bitcast.393, f32[]{:T(128)} %constant.82.clone.1), kind=kCustom, calls=%fused_computation.80 | custom fusion | flops 2097152 | bytes 8389120
  870.4 6.0 convert_element_type.3242
  876.4 6.3 copy.179
  886.3 6.9 fusion.539
  893.2 4.6 fusion.137
  897.9 4.7 fusion.179
  902.5 4.9 fusion.176
  907.5 4.7 fusion.173
  912.2 4.7 fusion.170
  916.9 5.0 fusion.167
  922.1 4.6 fusion.164
  926.7 4.9 fusion.182
  936.4 3.7 fusion.552
  947.8 24.0 %all-reduce.15 = (bf16[512]{0:T(512)(128)(2,1)S(1)}, bf16[512]{0:T(512)(128)(2,1)S(1)}, bf16[256]{0:T(256)(128)(2,1)S(1)}, bf16[512]{0:T(512)(128)(2,1)S(1)}, bf...) all-reduce(bf16[512]{0:T(512)(128)(2,1)S(1)} %add_convert_fusion.13, ...), channel_id=3, replica_groups=mesh['fsdp'=8,'seq'=4] {'fsdp'}, use_global_device_ids=true, to_apply=%region_36.37.clone | all-reduce | flops 5376 | bytes 21504
  972.5 11.4 %all-reduce.17 = (bf16[64]{0:T(256)(128)(2,1)S(1)}, bf16[64]{0:T(256)(128)(2,1)S(1)}, bf16[32]{0:T(256)(128)(2,1)S(1)}, bf16[64]{0:T(256)(128)(2,1)S(1)}, bf16[6...) all-reduce(bf16[64]{0:T(256)(128)(2,1)S(1)} %dynamic-slice.8, ...), channel_id=1, replica_groups=mesh['fsdp'=8,'seq'=4] {'seq'}, use_global_device_ids=true, to_apply=%region_37.38 | all-reduce | flops 672 | bytes 2688 | tf_op jit(solution)/shard_map/psum | solution.py:481
  (607 shorter events, 291.2 us)
Async XLA Ops:
  7.2 138.8 %all-gather.7.cloned.1.call-start = ((), (), s32[]{:S(2)}) async-start(), calls=%async_computation.8 | async-start | bytes 1769472 | tf_op jit(solution)/shard_map/all_gather | solution.py:118
  7.9 227.0 %all-gather.9.cloned.1.call-start = ((), (), s32[]{:S(2)}) async-start(), calls=%async_computation.9 | async-start | bytes 2359296 | tf_op jit(solution)/shard_map/all_gather | solution.py:123
  8.7 252.0 %all-gather.11.cloned.1.call-start = ((), (), s32[]{:S(2)}) async-start(), calls=%async_computation.10 | async-start | bytes 2359296 | tf_op jit(solution)/shard_map/all_gather | solution.py:125
  9.4 278.2 %all-gather.13.cloned.1.call-start = ((), (), s32[]{:S(2)}) async-start(), calls=%async_computation.11 | async-start | bytes 5242880 | tf_op jit(solution)/shard_map/all_gather | solution.py:177
  10.0 356.6 %all-gather.15.cloned.1.call-start = ((), (), s32[]{:S(2)}) async-start(), calls=%async_computation.12 | async-start | bytes 1179648 | tf_op jit(solution)/shard_map/all_gather | solution.py:128
  34.2 11.7 %copy-start.112 = (s32[2,512,4]{1,2,0:T(4,128)S(1)}, s32[2,512,4]{1,2,0:T(4,128)}, u32[]{:S(2)}) copy-start(s32[2,512,4]{1,2,0:T(4,128)} %param.19) | copy-start | bytes 49156
  35.5 10.8 %copy-start.148 = (bf16[256]{0:T(256)(128)(2,1)S(1)}, bf16[256]{0:T(256)(128)(2,1)}, u32[]{:S(2)}) copy-start(bf16[256]{0:T(256)(128)(2,1)} %param.29) | copy-start | bytes 1540
  35.7 187.4 %copy-start = (bf16[1,512,512]{1,2,0:T(8,128)(2,1)}, bf16[1,512,512]{1,2,0:T(8,128)(2,1)S(1)}, u32[]{:S(2)}) copy-start(bf16[1,512,512]{1,2,0:T(8,128)(2,1)S(1)} %copy.266) | copy-start | bytes 1572868
  36.0 29.2 %copy-start.2 = (bf16[1,512,512]{1,2,0:T(8,128)(2,1)}, bf16[1,512,512]{1,2,0:T(8,128)(2,1)S(1)}, u32[]{:S(2)}) copy-start(bf16[1,512,512]{1,2,0:T(8,128)(2,1)S(1)} %copy.265) | copy-start | bytes 1572868
  36.0 29.2 %copy-start.114 = (bf16[64,512]{1,0:T(8,128)(2,1)S(1)}, bf16[64,512]{1,0:T(8,128)(2,1)}, u32[]{:S(2)}) copy-start(bf16[64,512]{1,0:T(8,128)(2,1)} %param.24) | copy-start | bytes 196612
  36.1 40.2 %copy-start.115 = (bf16[64,512]{1,0:T(8,128)(2,1)S(1)}, bf16[64,512]{1,0:T(8,128)(2,1)}, u32[]{:S(2)}) copy-start(bf16[64,512]{1,0:T(8,128)(2,1)} %param.32) | copy-start | bytes 196612
  36.2 20.3 %copy-start.119 = (f32[512]{0:T(512)}, f32[512]{0:T(512)S(1)}, u32[]{:S(2)}) copy-start(f32[512]{0:T(512)S(1)} %broadcast_multiply_fusion.9) | copy-start | bytes 6148
  36.4 20.1 %copy-start.121 = (f32[512]{0:T(512)}, f32[512]{0:T(512)S(1)}, u32[]{:S(2)}) copy-start(f32[512]{0:T(512)S(1)} %broadcast_multiply_fusion.11) | copy-start | bytes 6148
  38.0 108.0 %collective-permute-start.1 = (bf16[512,512]{0,1:T(8,128)(2,1)}, bf16[512,512]{0,1:T(8,128)(2,1)}, u32[]{:S(2)}, u32[]{:S(2)}) collective-permute-start(bf16[512,512]{0,1:T(8,128)(2,1)} %get-tuple-element.165), channel_id=1, source_target_pairs={{0,1},{1,2},{2,3},{4,5},{5,6},{6,7},{8,9},{9,10},{10,11},{12,13},{... | collective-permute-start | bytes 1572872 | tf_op jit(solution)/shard_map/ppermute | solution.py:24
  42.3 106.8 %collective-permute-start = (bf16[512,512]{0,1:T(8,128)(2,1)}, bf16[512,512]{0,1:T(8,128)(2,1)}, u32[]{:S(2)}, u32[]{:S(2)}) collective-permute-start(bf16[512,512]{0,1:T(8,128)(2,1)} %get-tuple-element.166), channel_id=1, source_target_pairs={{0,1},{1,2},{2,3},{4,5},{5,6},{6,7},{8,9},{9,10},{10,11},{12,13},{... | collective-permute-start | bytes 1572872 | tf_op jit(solution)/shard_map/ppermute | solution.py:24
  45.8 711.4 %reduce-scatter.23.cloned.1.call-start = ((), (), s32[]{:S(2)}) async-start(), calls=%async_computation.20 | async-start | bytes 589824 | tf_op jit(solution)/shard_map/reduce_scatter | solution.py:473
  46.1 45.6 %copy-start.88 = (s32[64,1024]{1,0:T(8,128)}, s32[64,1024]{1,0:T(8,128)S(1)}, u32[]{:S(2)}) copy-start(s32[64,1024]{1,0:T(8,128)S(1)} %convert_add_fusion.8) | copy-start | bytes 786436
  56.5 54.2 %copy-start.86 = (s32[64,1024]{1,0:T(8,128)}, s32[64,1024]{1,0:T(8,128)S(1)}, u32[]{:S(2)}) copy-start(s32[64,1024]{1,0:T(8,128)S(1)} %convert_add_fusion.1) | copy-start | bytes 786436
  57.4 50.2 %copy-start.90 = (s32[64,1024]{1,0:T(8,128)}, s32[64,1024]{1,0:T(8,128)S(1)}, u32[]{:S(2)}) copy-start(s32[64,1024]{1,0:T(8,128)S(1)} %convert_add_fusion.2) | copy-start | bytes 786436
  58.3 46.5 %copy-start.92 = (s32[64,1024]{1,0:T(8,128)}, s32[64,1024]{1,0:T(8,128)S(1)}, u32[]{:S(2)}) copy-start(s32[64,1024]{1,0:T(8,128)S(1)} %convert_add_fusion.3) | copy-start | bytes 786436
  65.2 28.0 %copy-start.100 = (s32[64,1024]{1,0:T(8,128)S(1)}, s32[64,1024]{1,0:T(8,128)}, u32[]{:S(2)}) copy-start(s32[64,1024]{1,0:T(8,128)} %convert_add_fusion.7) | copy-start | bytes 786436
  91.7 10.2 %copy-start.94 = (s32[64,1024]{1,0:T(8,128)S(1)}, s32[64,1024]{1,0:T(8,128)}, u32[]{:S(2)}) copy-start(s32[64,1024]{1,0:T(8,128)} %convert_add_fusion.4) | copy-start | bytes 786436
  155.7 20.1 %copy-start.24 = (bf16[1024,512]{0,1:T(8,128)(2,1)}, bf16[1024,512]{0,1:T(8,128)(2,1)S(1)}, u32[]{:S(2)}) copy-start(bf16[1024,512]{0,1:T(8,128)(2,1)S(1)} %copy.166) | copy-start | bytes 3145732
  157.4 18.4 %copy-start.44 = (bf16[512,512]{0,1:T(8,128)(2,1)}, bf16[512,512]{0,1:T(8,128)(2,1)S(1)}, u32[]{:S(2)}) copy-start(bf16[512,512]{0,1:T(8,128)(2,1)S(1)} %copy.165) | copy-start | bytes 1572868
  194.9 23.0 %copy-start.104 = (f32[8,512]{1,0:T(8,128)}, f32[8,512]{1,0:T(8,128)S(1)}, u32[]{:S(2)}) copy-start(f32[8,512]{1,0:T(8,128)S(1)} %log_add_fusion) | copy-start | bytes 49156
  194.9 23.0 %slice-start = ((s8[16777216]{0:T(1024)(128)(4,1)}), s8[4194304]{0:T(1024)(128)(4,1)S(1)}, s32[]{:S(2)}) async-start(s8[16777216]{0:T(1024)(128)(4,1)} %bitcast.374), calls=%async_computation.22 | async-start | bytes 8388608
  194.9 23.0 %slice-start.1 = ((s8[16777216]{0:T(1024)(128)(4,1)}), s8[4194304]{0:T(1024)(128)(4,1)S(1)}, s32[]{:S(2)}) async-start(s8[16777216]{0:T(1024)(128)(4,1)} %bitcast.374), calls=%async_computation.23 | async-start | bytes 8388608
  194.9 23.0 %slice-start.2 = ((s8[16777216]{0:T(1024)(128)(4,1)}), s8[4194304]{0:T(1024)(128)(4,1)S(1)}, s32[]{:S(2)}) async-start(s8[16777216]{0:T(1024)(128)(4,1)} %bitcast.374), calls=%async_computation.24 | async-start | bytes 8388608
  234.9 25.7 %copy-start.110 = (f32[512]{0:T(512)}, f32[512]{0:T(512)S(1)}, u32[]{:S(2)}) copy-start(f32[512]{0:T(512)S(1)} %add_rsqrt_fusion.2) | copy-start | bytes 6148
  287.6 73.7 %copy-start.127 = (pred[2,2048]{1,0:T(4,128)(4,1)S(1)}, pred[2,2048]{1,0:T(4,128)(4,1)}, u32[]{:S(2)}) copy-start(pred[2,2048]{1,0:T(4,128)(4,1)} %and.19) | copy-start | bytes 12292
  396.6 17.9 %copy-start.61 = (f32[512,8,4]{1,2,0:T(4,128)}, f32[512,8,4]{1,2,0:T(4,128)S(1)}, u32[]{:S(2)}) copy-start(f32[512,8,4]{1,2,0:T(4,128)S(1)} %fusion.240) | copy-start | bytes 196612
  399.3 15.2 %copy-start.8 = (f32[512,8,64]{2,1,0:T(8,128)S(1)}, f32[512,8,64]{2,1,0:T(8,128)}, u32[]{:S(2)}) copy-start(f32[512,8,64]{2,1,0:T(8,128)} %copy.271) | copy-start | bytes 3145732
  474.8 15.3 %copy-start.65 = (f32[512,8,4]{1,2,0:T(4,128)}, f32[512,8,4]{1,2,0:T(4,128)S(1)}, u32[]{:S(2)}) copy-start(f32[512,8,4]{1,2,0:T(4,128)S(1)} %subtract_multiply_fusion.1) | copy-start | bytes 196612
  550.6 206.6 %reduce-scatter.19.cloned.1.call-start = ((), (), s32[]{:S(2)}) async-start(), calls=%async_computation.18 | async-start | bytes 589824 | tf_op jit(solution)/shard_map/reduce_scatter | solution.py:467
  573.2 11.2 %copy-start.5 = (f32[512,8,64]{2,1,0:T(8,128)S(1)}, f32[512,8,64]{2,1,0:T(8,128)}, u32[]{:S(2)}) copy-start(f32[512,8,64]{2,1,0:T(8,128)} %copy.275) | copy-start | bytes 3145732
  573.2 11.2 %copy-start.62 = (f32[512,8,4]{1,2,0:T(4,128)S(1)}, f32[512,8,4]{1,2,0:T(4,128)}, u32[]{:S(2)}) copy-start(f32[512,8,4]{1,2,0:T(4,128)} %copy-done.61) | copy-start | bytes 196612
  589.1 168.2 %reduce-scatter.13.cloned.1.call-start = ((), (), s32[]{:S(2)}) async-start(), calls=%async_computation.15 | async-start | bytes 589824 | tf_op jit(solution)/shard_map/reduce_scatter | solution.py:443
  605.3 152.0 %reduce-scatter.21.cloned.1.call-start = ((), (), s32[]{:S(2)}) async-start(), calls=%async_computation.19 | async-start | bytes 1179648 | tf_op jit(solution)/shard_map/reduce_scatter | solution.py:470
  615.1 142.2 %reduce-scatter.15.cloned.1.call-start = ((), (), s32[]{:S(2)}) async-start(), calls=%async_computation.16 | async-start | bytes 2359296 | tf_op jit(solution)/shard_map/reduce_scatter | solution.py:455
  632.2 154.5 %reduce-scatter.17.cloned.1.call-start = ((), (), s32[]{:S(2)}) async-start(), calls=%async_computation.17 | async-start | bytes 2359296 | tf_op jit(solution)/shard_map/reduce_scatter | solution.py:461
  693.3 136.0 %reduce-scatter.11.cloned.1.call-start = ((), (), s32[]{:S(2)}) async-start(), calls=%async_computation.14 | async-start | bytes 1769472 | tf_op jit(solution)/shard_map/reduce_scatter | solution.py:440
  699.0 28.2 %collective-permute-start.2 = (bf16[512,1024]{0,1:T(8,128)(2,1)S(1)}, bf16[512,1024]{0,1:T(8,128)(2,1)S(1)}, u32[]{:S(2)}, u32[]{:S(2)}) collective-permute-start(bf16[512,1024]{0,1:T(8,128)(2,1)S(1)} %pad_maximum_fusion.8), channel_id=1, source_target_pairs={{1,0},{2,1},{3,2},{5,4},{6,5},{7,6},{9,8},{10,9},{11,10},{13,12},{... | collective-permute-start | bytes 3145736 | tf_op jit(solution)/shard_map/ppermute | solution.py:24
  700.7 48.0 %collective-permute-start.3 = (bf16[512,1024]{0,1:T(8,128)(2,1)S(1)}, bf16[512,1024]{0,1:T(8,128)(2,1)S(1)}, u32[]{:S(2)}, u32[]{:S(2)}) collective-permute-start(bf16[512,1024]{0,1:T(8,128)(2,1)S(1)} %pad_maximum_fusion.9), channel_id=1, source_target_pairs={{1,0},{2,1},{3,2},{5,4},{6,5},{7,6},{9,8},{10,9},{11,10},{13,12},{... | collective-permute-start | bytes 3145736 | tf_op jit(solution)/shard_map/ppermute | solution.py:24
  705.0 47.5 %copy-start.69 = (bf16[8,64,512]{2,1,0:T(8,128)(2,1)}, bf16[8,64,512]{2,1,0:T(8,128)(2,1)S(1)}, u32[]{:S(2)}) copy-start(bf16[8,64,512]{2,1,0:T(8,128)(2,1)S(1)} %fusion.115) | copy-start | bytes 1572868
  707.6 41.4 %slice-start.10 = ((f32[1024,8,64]{0,2,1:T(8,128)}), f32[512,8,64]{0,2,1:T(8,128)S(1)}, s32[]{:S(2)}) async-start(f32[1024,8,64]{0,2,1:T(8,128)} %copy-done.40), calls=%async_computation.32 | async-start | bytes 2097152 | tf_op jit(solution)/shard_map/slice | solution.py:389
  707.6 41.4 %copy-start.55 = (f32[512,8,64]{0,2,1:T(8,128)S(1)}, f32[512,8,64]{0,2,1:T(8,128)}, u32[]{:S(2)}) copy-start(f32[512,8,64]{0,2,1:T(8,128)} %slice.192) | copy-start | bytes 3145732
  753.4 76.4 %copy-start.147 = (bf16[512,1024]{1,0:T(8,128)(2,1)S(1)}, bf16[512,1024]{1,0:T(8,128)(2,1)}, u32[]{:S(2)}) copy-start(bf16[512,1024]{1,0:T(8,128)(2,1)} %all-gather.15.cloned.1.call-done) | copy-start | bytes 3145732
  756.8 232.8 %all-reduce.21.cloned.1.call-start = ((), (), s32[]{:S(2)}) async-start(), calls=%async_computation.21 | async-start | bytes 2097152 | tf_op jit(solution)/shard_map/psum | solution.py:483
  829.4 171.7 %reduce-scatter.9.cloned.1.call-start = ((), (), s32[]{:S(2)}) async-start(), calls=%async_computation.13 | async-start | bytes 5242880 | tf_op jit(solution)/shard_map/reduce_scatter | solution.py:429
  886.3 11.6 %copy-start.101 = (s32[64,1024]{1,0:T(8,128)S(1)}, s32[64,1024]{1,0:T(8,128)}, u32[]{:S(2)}) copy-start(s32[64,1024]{1,0:T(8,128)} %convert_add_fusion.7) | copy-start | bytes 786436
  893.2 14.2 %copy-start.97 = (s32[64,1024]{1,0:T(8,128)S(1)}, s32[64,1024]{1,0:T(8,128)}, u32[]{:S(2)}) copy-start(s32[64,1024]{1,0:T(8,128)} %convert_add_fusion.5) | copy-start | bytes 786436
  897.9 14.3 %copy-start.95 = (s32[64,1024]{1,0:T(8,128)S(1)}, s32[64,1024]{1,0:T(8,128)}, u32[]{:S(2)}) copy-start(s32[64,1024]{1,0:T(8,128)} %convert_add_fusion.4) | copy-start | bytes 786436
  902.5 14.4 %copy-start.93 = (s32[64,1024]{1,0:T(8,128)S(1)}, s32[64,1024]{1,0:T(8,128)}, u32[]{:S(2)}) copy-start(s32[64,1024]{1,0:T(8,128)} %copy-done.92) | copy-start | bytes 786436
  907.4 14.6 %copy-start.91 = (s32[64,1024]{1,0:T(8,128)S(1)}, s32[64,1024]{1,0:T(8,128)}, u32[]{:S(2)}) copy-start(s32[64,1024]{1,0:T(8,128)} %copy-done.90) | copy-start | bytes 786436
  912.2 14.5 %copy-start.87 = (s32[64,1024]{1,0:T(8,128)S(1)}, s32[64,1024]{1,0:T(8,128)}, u32[]{:S(2)}) copy-start(s32[64,1024]{1,0:T(8,128)} %copy-done.86) | copy-start | bytes 786436
  916.9 14.9 %copy-start.13 = (f32[512,512]{0,1:T(8,128)S(1)}, f32[512,512]{0,1:T(8,128)}, u32[]{:S(2)}) copy-start(f32[512,512]{0,1:T(8,128)} %copy-done.11) | copy-start | bytes 3145732
  916.9 14.9 %copy-start.129 = (f32[512]{0:T(512)S(1)}, f32[512]{0:T(512)}, u32[]{:S(2)}) copy-start(f32[512]{0:T(512)} %copy-done.128) | copy-start | bytes 6148
  922.0 10.2 %copy-start.133 = (f32[512]{0:T(512)S(1)}, f32[512]{0:T(512)}, u32[]{:S(2)}) copy-start(f32[512]{0:T(512)} %get-tuple-element.169) | copy-start | bytes 6148
  922.0 10.2 %copy-start.137 = (f32[512]{0:T(512)S(1)}, f32[512]{0:T(512)}, u32[]{:S(2)}) copy-start(f32[512]{0:T(512)} %get-tuple-element.78) | copy-start | bytes 6148
  922.0 10.2 %copy-start.132 = (f32[512]{0:T(512)S(1)}, f32[512]{0:T(512)}, u32[]{:S(2)}) copy-start(f32[512]{0:T(512)} %get-tuple-element.151) | copy-start | bytes 6148
  922.0 10.2 %copy-start.134 = (f32[512]{0:T(512)S(1)}, f32[512]{0:T(512)}, u32[]{:S(2)}) copy-start(f32[512]{0:T(512)} %get-tuple-element.149) | copy-start | bytes 6148
  922.1 10.2 %copy-start.135 = (f32[2048]{0:T(1024)S(1)}, f32[2048]{0:T(1024)}, u32[]{:S(2)}) copy-start(f32[2048]{0:T(1024)} %get-tuple-element.197) | copy-start | bytes 24580
  922.1 10.2 %copy-start.136 = (f32[2048]{0:T(1024)S(1)}, f32[2048]{0:T(1024)}, u32[]{:S(2)}) copy-start(f32[2048]{0:T(1024)} %get-tuple-element.195) | copy-start | bytes 24580
  940.1 47.9 %copy-start.10 = (f32[512,512]{0,1:T(8,128)S(1)}, f32[512,512]{0,1:T(8,128)}, u32[]{:S(2)}) copy-start(f32[512,512]{0,1:T(8,128)} %copy-done.9) | copy-start | bytes 3145732
  (116 other events, 622.7 us)
Sparse Core Ops, SparseCore 0:
  9.9 28.5 all-gather.6
  40.4 27.9 all-gather.8
  70.2 29.0 all-gather.10
  100.7 80.7 all-gather.12
  183.3 22.0 all-gather.14
  550.7 31.4 reduce-scatter.22
  589.2 31.4 reduce-scatter.18
  623.7 34.0 reduce-scatter.12
  661.3 36.0 reduce-scatter.20
  700.9 41.2 reduce-scatter.14
  745.5 41.2 reduce-scatter.16
  790.8 38.4 reduce-scatter.10
  832.5 54.3 all-reduce.20
  889.1 75.6 reduce-scatter.8
where the time goes:
time: 1020 us; the launch traced here: 1010 us
  matrix products  289 us (28%)
  local copies, waits for them, and re-layouts  249 us (24%)
  other arithmetic  234 us (23%)
  waiting for transfers between devices  116 us (11%)
  blocking collectives  91.4 us (9%)
  between operations  19.7 us (2%)
  starting transfers between devices  12.2 us (1%)
    gather x1, local copies, waits for them, and re-layouts, on_device(): jnp.take_along_axis(shard_piece, jnp.clip(flat_ids, 0, piece_rows - 1)[:,...  73.7 us
    dot_general x16, matrix products, dot_plain(): return jnp.dot(left, right, preferred_element_type=jnp.float32)  60.2 us
    unnamed x10, other arithmetic  59.7 us
    unnamed x364, local copies, waits for them, and re-layouts  59.1 us
    dot_general x14, matrix products, dot_rows(): lax.dot_general(left, right, (((0,), (0,)), ((), ())), preferred_element_...  44 us
    reduce_scatter x1, waiting for transfers between devices, on_device(): lax.psum_scatter(grad_totals[2].astype(jnp.bfloat16), 'fsdp', scatter_dim...  42.6 us
    ppermute x4, waiting for transfers between devices, from_behind(): return lax.ppermute(block, axis, route)  40.8 us
    unnamed x2, blocking collectives  39.6 us
  transfers between devices with their start and end apart: 18, of which 4 were waited for; matrix products, arithmetic and copies ran while one was open for 57% of the time, Pallas kernels for 0%

commit v1 on v0

v1 whole, which is shorter than its diff:
```python
import functools
import math

import jax
import jax.numpy as jnp
import numpy as np
from jax import lax
from jax.experimental import pallas as pl
from jax.experimental.pallas import tpu as pltpu
from jax.sharding import PartitionSpec as P

D = 512
H = 8
HD = 64
K = 4
SEG = 512
NB = 32

EPS = 1e-05
HIGH = lax.Precision.HIGHEST
MASKED = -1e30
F32 = jnp.float32
BF16 = jnp.bfloat16
ROWS = 256
SPAN = 2 * SEG + 128
VMEM = 56 << 20


def nn(left, right):
    return lax.dot_general(left, right, (((1,), (0,)), ((), ())), preferred_element_type=F32)


def nt(left, right):
    return lax.dot_general(left, right, (((1,), (1,)), ((), ())), preferred_element_type=F32)


def tn(left, right):
    return lax.dot_general(left, right, (((0,), (0,)), ((), ())), preferred_element_type=F32)


def shape(dims, dtype):
    return jax.ShapeDtypeStruct(tuple(dims), dtype)


def whole(dims):
    zeros = (0,) * len(dims)
    return pl.BlockSpec(tuple(dims), lambda *_: zeros, pipeline_mode=pl.Buffered(1))


def scalars():
    return pl.BlockSpec(memory_space=pltpu.SMEM)


def params(grid_rank):
    return pltpu.CompilerParams(
        dimension_semantics=("arbitrary",) * grid_rank, vmem_limit_bytes=VMEM
    )


def cost(flops, moved, exps=0):
    return pl.CostEstimate(
        flops=int(flops), bytes_accessed=int(moved), transcendentals=int(exps)
    )


def thresholds():
    half_count = NB // 2
    spread_ratio = 2.0 * SEG / half_count
    exact_part = list(range(1, half_count))
    log_part = [
        int(half_count * spread_ratio ** ((bucket_index - half_count) / half_count))
        for bucket_index in range(half_count, NB)
    ]
    return np.array(exact_part + log_part)


def bucket_of(distance):
    return (distance[:, None] >= thresholds()[None, :]).sum(axis=1)


def forward_selector():
    distance = 2 * SEG - np.arange(SPAN)
    bucket = bucket_of(np.maximum(distance, 0))
    return (np.arange(NB)[:, None] == bucket[None, :]).astype(np.float32)


def backward_selector():
    place = np.arange(SPAN)
    offset = np.where(place <= 2 * SEG, place, place - SPAN)
    distance = 2 * SEG - 128 - offset
    bucket = bucket_of(np.maximum(distance, 0))
    chosen = (bucket[:, None] == np.arange(NB)[None, :]) & (distance >= 0)[:, None]
    return chosen.astype(np.float32)


def norm(values):
    average = jnp.mean(values, axis=-1, keepdims=True)
    centred = values - average
    variance = jnp.mean(centred * centred, axis=-1, keepdims=True)
    rstd_value = lax.rsqrt(variance + EPS)
    return centred * rstd_value, rstd_value


def norm_back(grad_result, hat_value, rstd_value, gain):
    scaled = grad_result * gain
    return rstd_value * (
        scaled
        - jnp.mean(scaled, axis=-1, keepdims=True)
        - hat_value * jnp.mean(scaled * hat_value, axis=-1, keepdims=True)
    )


def rows_sum(values):
    return jnp.sum(values, axis=0, keepdims=True)


def pair_mask(head, values):
    lane = lax.broadcasted_iota(jnp.int32, values.shape, 1)
    keep = lane < HD if head == 0 else lane >= HD
    return jnp.where(keep, values, jnp.zeros_like(values))


def prep_kernel(parts, place_ref, small_ref, table_ref, select_ref, vec_ref, own_ref, mem_ref):
    small = small_ref[...].astype(F32)
    devices = small.shape[0]
    vec_ref[...] = jnp.zeros_like(vec_ref)
    start = 0
    for row, width in enumerate(parts):
        pieces = [small[d : d + 1, start : start + width] for d in range(devices)]
        vec_ref[row : row + 1, : width * devices] = jnp.concatenate(pieces, axis=1)
        start += width
    by_distance = lax.dot_general(
        table_ref[...],
        select_ref[...],
        (((1,), (0,)), ((), ())),
        precision=HIGH,
        preferred_element_type=F32,
    )
    lane = lax.broadcasted_iota(jnp.int32, by_distance.shape, 1)
    by_distance = jnp.where(lane > 2 * SEG, MASKED, by_distance)
    hidden = jnp.where(place_ref[1] > 0, 0.0, MASKED)
    for head in range(H):
        line = jnp.broadcast_to(by_distance[head : head + 1, :], (128, SPAN))
        skewed = pltpu.roll(line, 0, 1, stride=1, stride_axis=0)
        tile = skewed[:, 128:].T
        own_ref[head] = tile
        mem_ref[head] = tile + hidden


def prep(place, small, table, parts, ff_width):
    devices, width = small.shape
    tiles = shape((H, 2 * SEG, 128), F32)
    return pl.pallas_call(
        functools.partial(prep_kernel, parts),
        in_specs=[scalars()] + [pl.BlockSpec(memory_space=pltpu.VMEM)] * 3,
        out_specs=[pl.BlockSpec(memory_space=pltpu.VMEM)] * 3,
        out_shape=[shape((8, ff_width), F32), tiles, tiles],
        compiler_params=pltpu.CompilerParams(vmem_limit_bytes=VMEM),
        cost_estimate=cost(0, 9 << 20),
        name="prep",
    )(place, small, table, jnp.asarray(forward_selector()))


def device_of(place_ref, chip_step, core_step):
    index = place_ref[0]
    chip = lax.shift_right_logical(index, 1)
    core = jnp.bitwise_and(index, 1)
    return jnp.bitwise_xor(chip, chip_step) * 2 + jnp.bitwise_xor(core, core_step)


def assemble_kernel(layout, place_ref, near_ref, far_ref, *out_refs):
    steps, rows, _ = near_ref.shape
    for core_step, ref in ((0, near_ref), (1, far_ref)):
        for step in range(steps):
            owner = device_of(place_ref, step, core_step)
            start = 0
            for out_ref, (chunks, width) in zip(out_refs, layout):
                for chunk in range(chunks):
                    target = pl.multiple_of((owner * chunks + chunk) * rows, rows)
                    out_ref[pl.ds(target, rows), :] = ref[step, :, start : start + width]
                    start += width


def assemble(place, near, far, layout):
    steps, rows, columns = near.shape
    total = 2 * steps * rows
    outs = [shape((total * chunks, width), BF16) for chunks, width in layout]
    return pl.pallas_call(
        functools.partial(assemble_kernel, layout),
        in_specs=[scalars()] + [pl.BlockSpec(memory_space=pltpu.VMEM)] * 2,
        out_specs=[pl.BlockSpec(memory_space=pltpu.VMEM)] * len(outs),
        out_shape=outs,
        compiler_params=pltpu.CompilerParams(vmem_limit_bytes=VMEM),
        cost_estimate=cost(0, 4 * total * columns),
        name="assemble",
    )(place, near, far)


def project_kernel(first, x_ref, vec_ref, w_ref, out_ref):
    hat_value, _ = norm(x_ref[0].astype(F32))
    normed = (hat_value * vec_ref[0:1, :D] + vec_ref[1:2, :D]).astype(BF16)
    out_ref[0] = nn(normed, w_ref[:, first:]).astype(BF16)


def project(x, vec, weight, first):
    batch, rows, _ = x.shape
    width = weight.shape[1] - first
    return pl.pallas_call(
        functools.partial(project_kernel, first),
        grid=(batch,),
        in_specs=[
            pl.BlockSpec((1, rows, D), lambda b: (b, 0, 0)),
            whole(vec.shape),
            whole(weight.shape),
        ],
        out_specs=pl.BlockSpec((1, rows, width), lambda b: (b, 0, 0)),
        out_shape=shape((batch, rows, width), BF16),
        compiler_params=params(1),
        cost_estimate=cost(2 * batch * rows * D * width, 2 * batch * rows * (D + width)),
        name="project",
    )(x, vec, weight)


def attend_kernel(q_ref, k_ref, v_ref, km_ref, vm_ref, own_ref, mem_ref, out_ref, prob_ref):
    keys = jnp.concatenate([km_ref[0], k_ref[0]], axis=0)
    values = jnp.concatenate([vm_ref[0], v_ref[0]], axis=0)
    for half in range(SEG // ROWS):
        width = SEG + (half + 1) * ROWS
        span = slice(half * ROWS, (half + 1) * ROWS)
        query = q_ref[0, span, :] * BF16(HD**-0.5)
        total = None
        for head in range(2):
            scores = nt(keys[:width], pair_mask(head, query))
            columns = []
            for part in range(ROWS // 128):
                block = half * (ROWS // 128) + part
                bias = jnp.concatenate(
                    [
                        mem_ref[head, (3 - block) * 128 : (7 - block) * 128, :],
                        own_ref[head, (7 - block) * 128 :, :],
                    ],
                    axis=0,
                )
                used = bias.shape[0]
                piece = scores[:used, part * 128 : (part + 1) * 128] + bias
                top = jnp.max(piece, axis=0, keepdims=True)
                weight = jnp.exp(piece - top)
                weight = (weight * (1.0 / jnp.sum(weight, axis=0, keepdims=True))).astype(BF16)
                if used < width:
                    weight = jnp.concatenate(
                        [weight, jnp.zeros((width - used, 128), BF16)], axis=0
                    )
                columns.append(weight)
            probs = jnp.concatenate(columns, axis=1)
            prob_ref[0, head, :width, span] = probs
            product = tn(probs, pair_mask(head, values)[:width])
            total = product if total is None else total + product
        out_ref[0, span, :] = total.astype(BF16)


def attend(joined, memory, own_bias, mem_bias):
    batch = joined.shape[0]
    pairs = H // 2

    def lanes(offset):
        return pl.BlockSpec((1, SEG, 128), lambda b, h: (b, 0, offset + h))

    bias = pl.BlockSpec((2, 2 * SEG, 128), lambda b, h: (h, 0, 0))
    work = batch * H * SEG * 2 * SEG
    return pl.pallas_call(
        attend_kernel,
        grid=(batch, pairs),
        in_specs=[lanes(0), lanes(pairs), lanes(2 * pairs), lanes(0), lanes(pairs), bias, bias],
        out_specs=[
            lanes(0),
            pl.BlockSpec((1, 2, 2 * SEG, SEG), lambda b, h: (b, h, 0, 0)),
        ],
        out_shape=[shape((batch, SEG, D), BF16), shape((batch, H, 2 * SEG, SEG), BF16)],
        compiler_params=params(2),
        cost_estimate=cost(16 * HD * work, 3 * work, work),
        name="attend",
    )(joined, joined, joined, memory, memory, own_bias, mem_bias)


def attend_back_kernel(
    q_ref, k_ref, v_ref, km_ref, vm_ref, grad_ref, out_ref, prob_ref,
    dq_ref, dk_ref, dv_ref, dkm_ref, dvm_ref, diag_ref, grid_ref,
):
    keys = jnp.concatenate([km_ref[0], k_ref[0]], axis=0)
    values = jnp.concatenate([vm_ref[0], v_ref[0]], axis=0)
    step = pl.program_id(1)

    @pl.when(step == 0)
    def _():
        grid_ref[...] = jnp.zeros_like(grid_ref)

    key_parts = []
    value_parts = []
    for half in range(SEG // ROWS):
        width = SEG + (half + 1) * ROWS
        span = slice(half * ROWS, (half + 1) * ROWS)
        grad = grad_ref[0, span, :]
        query = q_ref[0, span, :] * BF16(HD**-0.5)
        product = (grad.astype(F32) * out_ref[0, span, :].astype(F32)).T
        query_total = key_total = value_total = None
        for head in range(2):
            grad_head = pair_mask(head, grad)
            delta = jnp.sum(product[head * HD : (head + 1) * HD], axis=0, keepdims=True)
            probs = prob_ref[0, head, :width, span]
            scored = probs.astype(F32) * (nt(values[:width], grad_head) - delta)
            for part in range(ROWS // 128):
                block = half * (ROWS // 128) + part
                used = SEG + (block + 1) * 128
                grid_ref[head, (3 - block) * 128 :, :] += scored[
                    :used, part * 128 : (part + 1) * 128
                ]
            scored = scored.astype(BF16)
            for_key = nn(scored, pair_mask(head, query))
            for_value = nn(probs, grad_head)
            for_query = tn(scored, pair_mask(head, keys)[:width])
            key_total = for_key if key_total is None else key_total + for_key
            value_total = for_value if value_total is None else value_total + for_value
            query_total = for_query if query_total is None else query_total + for_query
        dq_ref[0, span, :] = (query_total * HD**-0.5).astype(BF16)
        key_parts.append(key_total)
        value_parts.append(value_total)
    for pieces, mem_ref, own_ref in (
        (key_parts, dkm_ref, dk_ref),
        (value_parts, dvm_ref, dv_ref),
    ):
        both = pieces[0] + pieces[1][: SEG + ROWS]
        mem_ref[0] = both[:SEG].astype(BF16)
        own_ref[0, :ROWS] = both[SEG:].astype(BF16)
        own_ref[0, ROWS:] = pieces[1][SEG + ROWS :].astype(BF16)

    @pl.when(step == pl.num_programs(1) - 1)
    def _():
        for head in range(2):
            line = jnp.concatenate(
                [grid_ref[head].T, jnp.zeros((128, SPAN - 2 * SEG), F32)], axis=1
            )
            row = lax.broadcasted_iota(jnp.int32, line.shape, 0)
            for bit in range(7):
                moved = pltpu.roll(line, SPAN - (1 << bit), 1)
                odd = jnp.bitwise_and(lax.shift_right_logical(row, bit), 1) == 1
                line = jnp.where(odd, moved, line)
            diag_ref[0, head : head + 1, :] = rows_sum(line)


def attend_back(joined, memory, grad, attended, probs):
    batch = joined.shape[0]
    pairs = H // 2

    def lanes(offset):
        return pl.BlockSpec((1, SEG, 128), lambda h, b: (b, 0, offset + h))

    half = shape((batch, SEG, D), BF16)
    work = batch * H * SEG * 2 * SEG
    return pl.pallas_call(
        attend_back_kernel,
        grid=(pairs, batch),
        in_specs=[lanes(0), lanes(pairs), lanes(2 * pairs), lanes(0), lanes(pairs)]
        + [lanes(0)] * 2
        + [pl.BlockSpec((1, 2, 2 * SEG, SEG), lambda h, b: (b, h, 0, 0))],
        out_specs=[lanes(0)] * 5 + [pl.BlockSpec((1, 2, SPAN), lambda h, b: (h, 0, 0))],
        out_shape=[half] * 5 + [shape((pairs, 2, SPAN), F32)],
        scratch_shapes=[pltpu.VMEM((2, 2 * SEG, 128), F32)],
        compiler_params=params(2),
        cost_estimate=cost(32 * HD * work, 3 * work),
        name="attend_back",
    )(joined, joined, joined, memory, memory, grad, attended, probs)


def feed_kernel(
    x_ref, att_ref, vec_ref, merge_ref, expand_ref, reduce_ref, nq_ref,
    after_attn_ref, active_ref, slope_ref, after_ffn_ref, query_ref,
):
    after_attn = x_ref[...].astype(F32) + nn(att_ref[...], merge_ref[...])
    after_attn_ref[...] = after_attn
    hat_value, _ = norm(after_attn)
    normed = (hat_value * vec_ref[2:3, :D] + vec_ref[3:4, :D]).astype(BF16)
    pre = nn(normed, expand_ref[...]) + vec_ref[6:7, :]
    cdf = 0.5 * (1.0 + lax.erf(pre * (1.0 / math.sqrt(2.0))))
    slope = cdf + pre * jnp.exp(-0.5 * pre * pre) * (1.0 / math.sqrt(2.0 * math.pi))
    slope_ref[...] = slope.astype(BF16)
    active = (pre * cdf).astype(BF16)
    active_ref[...] = active
    after_ffn = after_attn + nn(active, reduce_ref[...]) + vec_ref[4:5, :D]
    after_ffn_ref[...] = after_ffn
    query_ref[...] = nn(after_ffn.astype(BF16), nq_ref[...]).astype(BF16)


def feed(x, attended, vec, merge, expand, reduce, near_query):
    count = x.shape[0]
    ff = expand.shape[1]

    def rows(width):
        return pl.BlockSpec((ROWS, width), lambda i: (i, 0))

    return pl.pallas_call(
        feed_kernel,
        grid=(count // ROWS,),
        in_specs=[rows(D), rows(D)]
        + [whole(w.shape) for w in (vec, merge, expand, reduce, near_query)],
        out_specs=[rows(D), rows(ff), rows(ff), rows(D), rows(D)],
        out_shape=[
            shape((count, D), F32),
            shape((count, ff), BF16),
            shape((count, ff), BF16),
            shape((count, D), F32),
            shape((count, D), BF16),
        ],
        compiler_params=params(1),
        cost_estimate=cost(4 * count * D * (ff + D), 12 * count * ff, 2 * count * ff),
        name="feed",
    )(x, attended, vec, merge, expand, reduce, near_query)


def add_rows(ref, row, values):
    ref[row : row + 1, : values.shape[1]] += values


def scatter_rows(place_ref, total_ref, near_ref, far_ref, start, chunks):
    steps, rows = near_ref.shape[0], near_ref.shape[1]
    width = total_ref.shape[1]
    for core_step, ref in ((0, near_ref), (1, far_ref)):
        for step in range(steps):
            owner = device_of(place_ref, step, core_step)
            for chunk in range(chunks):
                source = pl.multiple_of((owner * chunks + chunk) * rows, rows)
                column = start + chunk * width
                ref[step, :, column : column + width] = total_ref[
                    pl.ds(source, rows), :
                ].astype(BF16)
    return start + chunks * width


def feed_back_kernel(
    place_ref, grad_ref, after_ref, active_ref, slope_ref, att_ref, vec_ref,
    merge_ref, expand_ref, reduce_ref,
    after_grad_ref, att_grad_ref, small_ref, near_ref, far_ref,
    expand_total, reduce_total, merge_total,
):
    step = pl.program_id(0)

    @pl.when(step == 0)
    def _():
        expand_total[...] = jnp.zeros_like(expand_total)
        reduce_total[...] = jnp.zeros_like(reduce_total)
        merge_total[...] = jnp.zeros_like(merge_total)
        small_ref[...] = jnp.zeros_like(small_ref)

    grad = grad_ref[...]
    low = grad.astype(BF16)
    add_rows(small_ref, 2, rows_sum(low.astype(F32)))
    reduce_total[...] += tn(active_ref[...], low)
    pre_grad = (nt(low, reduce_ref[...]) * slope_ref[...].astype(F32)).astype(BF16)
    add_rows(small_ref, 3, rows_sum(pre_grad.astype(F32)))
    hat_value, rstd_value = norm(after_ref[...])
    gain = vec_ref[2:3, :D]
    normed = (hat_value * gain + vec_ref[3:4, :D]).astype(BF16)
    expand_total[...] += tn(normed, pre_grad)
    normed_grad = nt(pre_grad, expand_ref[...])
    add_rows(small_ref, 0, rows_sum(normed_grad * hat_value))
    add_rows(small_ref, 1, rows_sum(normed_grad))
    after_grad = grad + norm_back(normed_grad, hat_value, rstd_value, gain)
    after_grad_ref[...] = after_grad
    merge_grad = after_grad.astype(BF16)
    merge_total[...] += tn(att_ref[...], merge_grad)
    att_grad_ref[...] = nt(merge_grad, merge_ref[...]).astype(BF16)

    @pl.when(step == pl.num_programs(0) - 1)
    def _():
        start = scatter_rows(place_ref, expand_total, near_ref, far_ref, 0, 1)
        ratio = reduce_total.shape[0] // D
        start = scatter_rows(place_ref, reduce_total, near_ref, far_ref, start, ratio)
        scatter_rows(place_ref, merge_total, near_ref, far_ref, start, 1)


def feed_back(place, devices, grad, after_attn, active, slope, attended, vec, merge, expand, reduce):
    count = grad.shape[0]
    ff = expand.shape[1]

    def rows(width):
        return pl.BlockSpec((ROWS, width), lambda i: (i, 0))

    packed = (devices // 2, D // devices, 2 * ff + D)
    return pl.pallas_call(
        feed_back_kernel,
        grid=(count // ROWS,),
        in_specs=[scalars(), rows(D), rows(D), rows(ff), rows(ff), rows(D)]
        + [whole(w.shape) for w in (vec, merge, expand, reduce)],
        out_specs=[rows(D), rows(D), whole((8, ff)), whole(packed), whole(packed)],
        out_shape=[
            shape((count, D), F32),
            shape((count, D), BF16),
            shape((8, ff), F32),
            shape(packed, BF16),
            shape(packed, BF16),
        ],
        scratch_shapes=[
            pltpu.VMEM((D, ff), F32),
            pltpu.VMEM((ff, D), F32),
            pltpu.VMEM((D, D), F32),
        ],
        compiler_params=params(1),
        cost_estimate=cost(8 * count * D * (ff + D // 2), 16 * count * ff),
        name="feed_back",
    )(place, grad, after_attn, active, slope, attended, vec, merge, expand, reduce)


def take_kernel(started, place_ref, ids_ref, rows_ref, *refs):
    out_ref = refs[-1]
    base = place_ref[1] * SEG
    ids = ids_ref[0] - base
    place = lax.broadcasted_iota(jnp.int32, (SEG, SEG), 1)
    rows = rows_ref[0]
    for slot in range(K):
        chosen = jnp.where(ids[:, slot : slot + 1] == place, 1.0, 0.0).astype(BF16)
        taken = nn(chosen, rows)
        if started:
            taken = taken + refs[0][0, slot].astype(F32)
        out_ref[0, slot] = taken.astype(BF16)


def take(place, ids, rows, so_far):
    batch = ids.shape[0]
    block = pl.BlockSpec((1, K, SEG, D), lambda b: (b, 0, 0, 0))
    started = so_far is not None
    return pl.pallas_call(
        functools.partial(take_kernel, started),
        grid=(batch,),
        in_specs=[
            scalars(),
            pl.BlockSpec((1, SEG, K), lambda b: (b, 0, 0)),
            pl.BlockSpec((1, SEG, D), lambda b: (b, 0, 0)),
        ]
        + [block] * started,
        out_specs=block,
        out_shape=shape((batch, K, SEG, D), BF16),
        input_output_aliases={3: 0} if started else {},
        compiler_params=params(1),
        cost_estimate=cost(2 * batch * K * SEG * SEG * D, 4 * batch * K * SEG * D),
        name="take",
    )(place, ids, rows, *([so_far] if started else []))


def give_kernel(started, place_ref, ids_ref, grad_ref, *refs):
    out_ref = refs[-1]
    base = place_ref[1] * SEG
    ids = ids_ref[0] - base
    place = lax.broadcasted_iota(jnp.int32, (SEG, SEG), 0)
    total = None
    for slot in range(K):
        chosen = jnp.where(ids[slot : slot + 1, :] == place, 1.0, 0.0).astype(BF16)
        part = nn(chosen, grad_ref[0, slot])
        total = part if total is None else total + part
    if started:
        total = total + refs[0][0].astype(F32)
    out_ref[0] = total.astype(out_ref.dtype)


def give(place, ids, grads, arrived, dtype):
    batch = ids.shape[0]
    block = pl.BlockSpec((1, SEG, D), lambda b: (b, 0, 0))
    started = arrived is not None
    return pl.pallas_call(
        functools.partial(give_kernel, started),
        grid=(batch,),
        in_specs=[
            scalars(),
            pl.BlockSpec((1, K, SEG), lambda b: (b, 0, 0)),
            pl.BlockSpec((1, K, SEG, D), lambda b: (b, 0, 0, 0)),
        ]
        + [block] * started,
        out_specs=block,
        out_shape=shape((batch, SEG, D), dtype),
        compiler_params=params(1),
        cost_estimate=cost(2 * batch * K * SEG * SEG * D, 2 * batch * K * SEG * D),
        name="give",
    )(place, ids, grads, *([arrived] if started else []))


def near_kernel(
    place_ref, rows_ref, query_ref, after_ref, grad_ref, vec_ref, keys_ref, merge_ref, nq_ref,
    out_ref, row_grad_ref, after_grad_ref, small_ref, near_ref, far_ref,
    keys_total, merge_total, query_total,
):
    first = (pl.program_id(0) == 0) & (pl.program_id(1) == 0)
    last = (pl.program_id(0) == pl.num_programs(0) - 1) & (
        pl.program_id(1) == pl.num_programs(1) - 1
    )

    @pl.when(first)
    def _():
        keys_total[...] = jnp.zeros_like(keys_total)
        merge_total[...] = jnp.zeros_like(merge_total)
        query_total[...] = jnp.zeros_like(query_total)
        small_ref[...] = jnp.zeros_like(small_ref)

    row = lax.broadcasted_iota(jnp.int32, (D, D), 0)
    column = lax.broadcasted_iota(jnp.int32, (D, D), 1)
    same_head = jnp.where(
        lax.shift_right_logical(row, 6) == lax.shift_right_logical(column, 6), 1.0, 0.0
    ).astype(BF16)
    scale = HD**-0.5
    query = query_ref[0]
    query_float = query.astype(F32)
    pairs = [nn(rows_ref[0, slot], keys_ref[...]).astype(BF16) for slot in range(K)]
    near_key = [pair[:, :D].astype(F32) for pair in pairs]
    near_value = [pair[:, D:].astype(F32) for pair in pairs]
    scores = [nn((query_float * key).astype(BF16), same_head) * scale for key in near_key]
    top = functools.reduce(jnp.maximum, scores)
    weights = [jnp.exp(score - top) for score in scores]
    inverse = 1.0 / functools.reduce(jnp.add, weights)
    probs = [weight * inverse for weight in weights]
    mixed = functools.reduce(jnp.add, [p * v for p, v in zip(probs, near_value)]).astype(BF16)
    near_out = nn(mixed, merge_ref[...])
    after_ffn = after_ref[0]
    gate_vector = vec_ref[5:6, :D]
    gate = jax.nn.sigmoid(jnp.sum(after_ffn * gate_vector, axis=-1, keepdims=True))
    out_ref[0] = (gate * after_ffn + (1.0 - gate) * near_out).astype(BF16)
    grad = grad_ref[0].astype(F32)
    gate_grad = (
        jnp.sum(grad * (after_ffn - near_out), axis=-1, keepdims=True) * gate * (1.0 - gate)
    )
    add_rows(small_ref, 0, rows_sum(gate_grad * after_ffn))
    near_grad = ((1.0 - gate) * grad).astype(BF16)
    merge_total[...] += tn(mixed, near_grad)
    mixed_grad = nt(near_grad, merge_ref[...]).astype(BF16).astype(F32)
    prob_grads = [nn((mixed_grad * value).astype(BF16), same_head) for value in near_value]
    inner = functools.reduce(jnp.add, [p * g for p, g in zip(probs, prob_grads)])
    query_grad = None
    for slot in range(K):
        score_grad = probs[slot] * (prob_grads[slot] - inner) * scale
        part = score_grad * near_key[slot]
        query_grad = part if query_grad is None else query_grad + part
        pair_grad = jnp.concatenate(
            [(score_grad * query_float).astype(BF16), (probs[slot] * mixed_grad).astype(BF16)],
            axis=1,
        )
        keys_total[...] += tn(rows_ref[0, slot], pair_grad)
        row_grad_ref[0, slot] = nt(pair_grad, keys_ref[...]).astype(BF16)
    query_grad = query_grad.astype(BF16)
    query_total[...] += tn(after_ffn.astype(BF16), query_grad)
    after_grad_ref[0] = gate * grad + gate_grad * gate_vector + nt(query_grad, nq_ref[...])

    @pl.when(last)
    def _():
        start = scatter_rows(place_ref, query_total, near_ref, far_ref, 0, 1)
        start = scatter_rows(place_ref, keys_total, near_ref, far_ref, start, 1)
        scatter_rows(place_ref, merge_total, near_ref, far_ref, start, 1)


def near(place, devices, rows, query, after_ffn, grad, vec, near_keys, near_merge, near_query):
    batch = rows.shape[0]
    row_block = pl.BlockSpec((1, K, ROWS, D), lambda b, i: (b, 0, i, 0))
    block = pl.BlockSpec((1, ROWS, D), lambda b, i: (b, i, 0))
    packed = (devices // 2, D // devices, 4 * D)
    count = batch * SEG
    return pl.pallas_call(
        near_kernel,
        grid=(batch, SEG // ROWS),
        in_specs=[scalars(), row_block, block, block, block]
        + [whole(w.shape) for w in (vec, near_keys, near_merge, near_query)],
        out_specs=[block, row_block, block, whole((8, D)), whole(packed), whole(packed)],
        out_shape=[
            shape((batch, SEG, D), BF16),
            shape((batch, K, SEG, D), BF16),
            shape((batch, SEG, D), F32),
            shape((8, D), F32),
            shape(packed, BF16),
            shape(packed, BF16),
        ],
        scratch_shapes=[
            pltpu.VMEM((D, 2 * D), F32),
            pltpu.VMEM((D, D), F32),
            pltpu.VMEM((D, D), F32),
        ],
        compiler_params=params(2),
        cost_estimate=cost(
            2 * count * D * D * (8 * K + 5), count * D * (4 * K + 12), count * K * D
        ),
        name="near",
    )(place, rows, query, after_ffn, grad, vec, near_keys, near_merge, near_query)


def finish_kernel(
    parts, place_ref, x_ref, before_ref, dq_ref, dk_ref, dv_ref, dkm_ref, dvm_ref, grad_ref,
    own_ref, sent_ref, vec_ref, w_ref, gate_ref, feed_ref, diag_ref, select_ref,
    part_ref, send_ref, near_ref, far_ref,
    w_total, norm_total, small_total,
):
    step = pl.program_id(0)

    @pl.when(step == 0)
    def _():
        w_total[...] = jnp.zeros_like(w_total)
        norm_total[...] = jnp.zeros_like(norm_total)

    gain = vec_ref[0:1, :D]
    shift = vec_ref[1:2, :D]
    hat_value, rstd_value = norm(x_ref[0].astype(F32))
    normed = (hat_value * gain + shift).astype(BF16)
    hat_before, rstd_before = norm(before_ref[0].astype(F32))
    normed_before = (hat_before * gain + shift).astype(BF16)
    w_total[:, :D] += tn(normed, dq_ref[0])
    w_total[:, D : 2 * D] += tn(normed, dk_ref[0]) + tn(normed_before, dkm_ref[0])
    w_total[:, 2 * D :] += tn(normed, dv_ref[0]) + tn(normed_before, dvm_ref[0])
    normed_grad = (
        nt(dq_ref[0], w_ref[:, :D])
        + nt(dk_ref[0], w_ref[:, D : 2 * D])
        + nt(dv_ref[0], w_ref[:, 2 * D :])
    )
    before_grad = nt(dkm_ref[0], w_ref[:, D : 2 * D]) + nt(dvm_ref[0], w_ref[:, 2 * D :])
    add_rows(norm_total, 0, rows_sum(normed_grad * hat_value) + rows_sum(before_grad * hat_before))
    add_rows(norm_total, 1, rows_sum(normed_grad) + rows_sum(before_grad))
    send_ref[0] = (
        sent_ref[0].astype(F32) + norm_back(before_grad, hat_before, rstd_before, gain)
    ).astype(BF16)
    part_ref[0] = (
        grad_ref[0] + own_ref[0] + norm_back(normed_grad, hat_value, rstd_value, gain)
    )

    @pl.when(step == pl.num_programs(0) - 1)
    def _():
        devices = small_total.shape[0]
        rows = w_total.shape[0] // devices
        small_total[...] = jnp.zeros_like(small_total)
        lines = [
            norm_total[0:1, :],
            norm_total[1:2, :],
            feed_ref[0:1, :D],
            feed_ref[1:2, :D],
            feed_ref[2:3, :D],
            gate_ref[0:1, :],
            feed_ref[3:4, :],
        ]
        start = 0
        for line, width in zip(lines, parts):
            for d in range(devices):
                small_total[d : d + 1, start : start + width] = line[
                    :, d * width : (d + 1) * width
                ]
            start += width
        table = lax.dot_general(
            diag_ref[...],
            select_ref[...],
            (((1,), (0,)), ((), ())),
            precision=HIGH,
            preferred_element_type=F32,
        )
        own_buckets = NB // devices
        bucket = lax.broadcasted_iota(jnp.int32, (devices, NB), 1)
        owner = lax.broadcasted_iota(jnp.int32, (devices, NB), 0)
        for place in range(own_buckets):
            chosen = jnp.where(bucket == owner * own_buckets + place, 1.0, 0.0)
            small_total[:, start : start + H] = lax.dot_general(
                chosen,
                table,
                (((1,), (1,)), ((), ())),
                precision=HIGH,
                preferred_element_type=F32,
            )
            start += H
        width = small_total.shape[1]
        for core_step, ref in ((0, near_ref), (1, far_ref)):
            for chip_step in range(ref.shape[0]):
                target = device_of(place_ref, chip_step, core_step)
                source = pl.multiple_of(target * rows, rows)
                ref[chip_step, :rows, :] = w_total[pl.ds(source, rows), :].astype(BF16)
                ref[chip_step, rows:, :] = jnp.zeros((16, ref.shape[2]), BF16)
                line = small_total[pl.ds(target, 1), :]
                ref[chip_step, rows : rows + 16, :width] = jnp.broadcast_to(
                    line, (16, width)
                ).astype(BF16)


def finish(
    place, devices, parts, x, before, pieces, grad, own, sent, vec, weight, gate, feed_small, diag
):
    batch = x.shape[0]
    block = pl.BlockSpec((1, SEG, D), lambda b: (b, 0, 0))
    packed = (devices // 2, D // devices + 16, 3 * D)
    select = jnp.asarray(backward_selector())
    small_width = -(-(sum(parts) + NB * H // devices) // 128) * 128
    return pl.pallas_call(
        functools.partial(finish_kernel, parts),
        grid=(batch,),
        in_specs=[scalars()]
        + [block] * 10
        + [whole(w.shape) for w in (vec, weight, gate, feed_small, diag, select)],
        out_specs=[block, block, whole(packed), whole(packed)],
        out_shape=[
            shape((batch, SEG, D), F32),
            shape((batch, SEG, D), BF16),
            shape(packed, BF16),
            shape(packed, BF16),
        ],
        scratch_shapes=[
            pltpu.VMEM((D, 3 * D), F32),
            pltpu.VMEM((8, D), F32),
            pltpu.VMEM((devices, small_width), F32),
        ],
        compiler_params=params(1),
        cost_estimate=cost(20 * batch * SEG * D * D, 30 * batch * SEG * D),
        name="finish",
    )(
        place, x, before, *pieces, grad, own, sent, vec, weight, gate, feed_small, diag, select
    )


def shift_up(block, distance):
    count = lax.axis_size("seq")
    route = [(i, i + distance) for i in range(count) if 0 <= i + distance < count]
    return lax.ppermute(block, "seq", route)


def swap(block, axis, bits):
    count = lax.axis_size(axis)
    return lax.ppermute(block, axis, [(i, i ^ bits) for i in range(count)])


def gather_weight(place, shard, layout):
    steps = lax.axis_size("fsdp") // 2
    pieces = [shard] + [swap(shard, "fsdp", 2 * step) for step in range(1, steps)]
    near_half = jnp.stack(pieces)
    far_half = swap(near_half, "fsdp", 1)
    return assemble(place, near_half, far_half, layout)


def reduce_weight(near_half, far_half):
    steps = lax.axis_size("fsdp") // 2
    arrived = swap(far_half, "fsdp", 1)
    pieces = [
        (near_half[step].astype(F32) + arrived[step].astype(F32)).astype(BF16)
        for step in range(steps)
    ]
    total = pieces[0].astype(F32)
    for step in range(1, steps):
        total = total + swap(pieces[step], "fsdp", 2 * step).astype(F32)
    bits = 1
    while bits < lax.axis_size("seq"):
        low = total.astype(BF16)
        total = low.astype(F32) + swap(low, "seq", bits).astype(F32)
        bits *= 2
    return total


def on_device(
    layer_input,
    neighbour_ids,
    out_grad,
    attn_norm_gain,
    attn_norm_bias,
    attn_project,
    attn_merge,
    position_bias,
    ffn_norm_gain,
    ffn_norm_bias,
    ffn_expand,
    expand_bias,
    ffn_reduce,
    reduce_bias,
    near_query,
    near_keys,
    near_merge,
    gate_vector,
):
    batch = layer_input.shape[0]
    count = batch * SEG
    devices = lax.axis_size("fsdp")
    segments = lax.axis_size("seq")
    seg_index = lax.axis_index("seq")
    rows = attn_project.shape[0]
    ff = ffn_expand.shape[1]
    ratio = ff // D

    def place_of(segment):
        return jnp.stack([lax.axis_index("fsdp"), segment]).astype(jnp.int32)

    place = place_of(seg_index)
    states = [layer_input]
    for _ in range(1, segments):
        states.append(shift_up(states[-1], 1))
    vectors = [
        attn_norm_gain, attn_norm_bias, ffn_norm_gain, ffn_norm_bias, reduce_bias, gate_vector,
        expand_bias, position_bias,
    ]
    parts = [v.shape[0] for v in vectors[:-1]]
    filled = sum(parts)
    own_bias_width = position_bias.shape[0]
    padding = -(filled + own_bias_width) % 128
    small = jnp.concatenate(vectors + [jnp.zeros((padding,), BF16)])[None]
    small = lax.all_gather(small, "fsdp", axis=0, tiled=True)
    table = small[:, filled : filled + own_bias_width].reshape(NB, H).T.astype(F32)
    (attn_w,) = gather_weight(place, attn_project, ((1, 3 * D),))
    reduce_columns = ffn_reduce.reshape(ratio, rows, D).transpose(1, 0, 2).reshape(rows, ff)
    merge_w, expand_w, reduce_w = gather_weight(
        place,
        jnp.concatenate([attn_merge, ffn_expand, reduce_columns], axis=1),
        ((1, D), (1, ff), (ratio, D)),
    )
    query_w, keys_w, near_merge_w = gather_weight(
        place,
        jnp.concatenate([near_query, near_keys, near_merge], axis=1),
        ((1, D), (1, 2 * D), (1, D)),
    )
    near_rows = None
    for distance in range(segments):
        near_rows = take(
            place_of(seg_index - distance), neighbour_ids, states[distance], near_rows
        )
    vec, own_bias, mem_bias = prep(place, small, table, parts, ff)
    joined = project(layer_input, vec, attn_w, 0)
    before = states[1]
    memory = project(before, vec, attn_w, D)
    attended, probs = attend(joined, memory, own_bias, mem_bias)
    flat_attended = attended.reshape(count, D)
    after_attn, active, slope, after_ffn, queries = feed(
        layer_input.reshape(count, D), flat_attended, vec, merge_w, expand_w, reduce_w, query_w
    )
    output, row_grads, after_grad, gate_small, near_half, far_half = near(
        place, devices, near_rows, queries.reshape(batch, SEG, D),
        after_ffn.reshape(batch, SEG, D), out_grad, vec, keys_w, near_merge_w, query_w,
    )
    near_total = reduce_weight(near_half, far_half)
    ids_across = jnp.swapaxes(neighbour_ids, 1, 2)
    arrived = None
    for distance in range(segments - 1, 0, -1):
        message = give(place_of(seg_index - distance), ids_across, row_grads, arrived, BF16)
        if distance > 1:
            arrived = shift_up(message, -1)
    own = give(place, ids_across, row_grads, None, F32)
    grad_after, att_grad, feed_small, near_half, far_half = feed_back(
        place, devices, after_grad.reshape(count, D), after_attn, active, slope, flat_attended,
        vec, merge_w, expand_w, reduce_w,
    )
    feed_total = reduce_weight(near_half, far_half)
    *pieces, diag = attend_back(
        joined, memory, att_grad.reshape(batch, SEG, D), attended, probs
    )
    partial, message, near_half, far_half = finish(
        place, devices, parts, layer_input, before, pieces, grad_after.reshape(batch, SEG, D),
        own, message, vec, attn_w, gate_small, feed_small, diag.reshape(H, SPAN),
    )
    attn_total = reduce_weight(near_half, far_half)
    input_grad = partial + shift_up(message, -1).astype(F32)
    line = attn_total[rows]
    smalls = []
    start = 0
    for width in parts + [own_bias_width]:
        smalls.append(line[start : start + width])
        start += width
    return (
        output,
        input_grad,
        smalls[0],
        smalls[1],
        attn_total[:rows],
        feed_total[:, 2 * ff :],
        smalls[7],
        smalls[2],
        smalls[3],
        feed_total[:, :ff],
        smalls[6],
        feed_total[:, ff : 2 * ff].reshape(rows, ratio, D).transpose(1, 0, 2).reshape(-1, D),
        smalls[4],
        near_total[:, :D],
        near_total[:, D : 3 * D],
        near_total[:, 3 * D :],
        smalls[5],
    )


def solution(mesh):
    in_specs = (
        P("fsdp", "seq", None),
        P("fsdp", "seq", None),
        P("fsdp", "seq", None),
        P("fsdp"),
        P("fsdp"),
        P("fsdp", None),
        P("fsdp", None),
        P("fsdp"),
        P("fsdp"),
        P("fsdp"),
        P("fsdp", None),
        P("fsdp"),
        P("fsdp", None),
        P("fsdp"),
        P("fsdp", None),
        P("fsdp", None),
        P("fsdp", None),
        P("fsdp"),
    )
    out_specs = (
        P("fsdp", "seq", None),
        P("fsdp", "seq", None),
        P("fsdp"),
        P("fsdp"),
        P("fsdp", None),
        P("fsdp", None),
        P("fsdp"),
        P("fsdp"),
        P("fsdp"),
        P("fsdp", None),
        P("fsdp"),
        P("fsdp", None),
        P("fsdp"),
        P("fsdp", None),
        P("fsdp", None),
        P("fsdp", None),
        P("fsdp"),
    )
    return jax.shard_map(
        on_device, mesh=mesh, in_specs=in_specs, out_specs=out_specs, check_vma=False
    )
```

time: 1020 us -> 406 us (0.40)
  matrix products: 289 us -> 0 us
  local copies, waits for them, and re-layouts: 249 us -> 24.7 us
  other arithmetic: 234 us -> 11.4 us
  Pallas kernels: 0 us -> 201 us
  blocking collectives: 91.4 us -> 23.9 us
  starting transfers between devices: 12.2 us -> 49.7 us
  waiting for transfers between devices: 116 us -> 86.4 us
  between operations: 19.7 us -> 1.61 us
    dot_general x72 -> x0, matrix products: 289 us -> none  [the longest x16 60.2 us: dot_plain(): return jnp.dot(left, right, preferred_element_type=jnp.float32)]
    pallas_call x0 -> x20, Pallas kernels: none -> 201 us  [the longest x1 32.3 us: near(): pl.pallas_call(near_kernel, grid=(batch, SEG // ROWS), in_specs=[scalars(...]
    gather x1 -> x0, local copies, waits for them, and re-layouts: 73.7 us -> none  [on_device(): jnp.take_along_axis(shard_piece, jnp.clip(flat_ids, 0, piece_rows - 1)[:,...]
    reduce_scatter x8 -> x0, waiting for transfers between devices: 72.2 us -> none  [the longest x1 42.6 us: on_device(): lax.psum_scatter(grad_totals[2].astype(jnp.bfloat16), 'fsdp', scatter_dim...]
    unnamed x10 -> x0, other arithmetic: 59.7 us -> none
    unnamed x364 -> x40, local copies, waits for them, and re-layouts: 59.1 us -> 8.52 us
    ppermute x4 -> x36, waiting for transfers between devices: 40.8 us -> 86.4 us  [the longest x30 86.4 us: swap(): return lax.ppermute(block, axis, [(i, i ^ bits) for i in range(count)])]
    add x19 -> x4, other arithmetic: 45.5 us -> 1.9 us  [the longest x1 1.67 us: on_device(): input_grad = partial + shift_up(message, -1).astype(F32)]
  transfers between devices with their start and end apart: 18 -> 36, of which waited for: 4 -> 15; matrix products, arithmetic and copies ran while one was open for 57% -> 6% of each run, Pallas kernels for 0% -> 41%
where the time goes in v1:
time: 406 us; the launch traced here: 399 us
  Pallas kernels  201 us (50%)
  waiting for transfers between devices  86.4 us (21%)
  starting transfers between devices  49.7 us (12%)
  local copies, waits for them, and re-layouts  24.7 us (6%)
  blocking collectives  23.9 us (6%)
  other arithmetic  11.4 us (3%)
    ppermute x30, waiting for transfers between devices, swap(): return lax.ppermute(block, axis, [(i, i ^ bits) for i in range(count)])  86.4 us
    ppermute x30, starting transfers between devices, swap(): return lax.ppermute(block, axis, [(i, i ^ bits) for i in range(count)])  33.7 us
    pallas_call x1, Pallas kernels, near(): pl.pallas_call(near_kernel, grid=(batch, SEG // ROWS), in_specs=[scalars(...  32.3 us
    pallas_call x1, Pallas kernels, attend_back(): pl.pallas_call(attend_back_kernel, grid=(pairs, batch), in_specs=[lanes(0...  29.9 us
    all_gather x1, blocking collectives, on_device(): small = lax.all_gather(small, 'fsdp', axis=0, tiled=True)  23.9 us
    pallas_call x4, Pallas kernels, take(): pl.pallas_call(functools.partial(take_kernel, started), grid=(batch,), in...  22.6 us
    pallas_call x1, Pallas kernels, attend(): pl.pallas_call(attend_kernel, grid=(batch, pairs), in_specs=[lanes(0), la...  20.6 us
    pallas_call x4, Pallas kernels, give(): pl.pallas_call(functools.partial(give_kernel, started), grid=(batch,), in...  20.1 us
  transfers between devices with their start and end apart: 36, of which 15 were waited for; matrix products, arithmetic and copies ran while one was open for 6% of the time, Pallas kernels for 41%

profile of v1, /device:TPU:0, one launch (start us, length us, event | category | flops | bytes accessed | tf_op | source)
XLA Modules:
  0.0 398.7 jit_solution(9450994569821853482)
XLA Ops:
  0.7 1.2 copy.65
  3.8 4.0 collective-permute-start.9
  8.4 1.9 collective-permute-start.3
  10.3 3.5 collective-permute-start
  14.4 4.1 %concatenate.9 = bf16[768]{0:T(1024)(128)(2,1)S(1)} concatenate(bf16[64]{0:T(256)(128)(2,1)S(1)} %copy-done.11, bf16[64]{0:T(256)(128)(2,1)S(1)} %copy-done.12, bf16[64]{0:T(256)(128)(2,1)S(1)} %copy-done.13, bf16[64]{0:T(256)(128)(2,1)} %param.29, bf16[64]{0:T(256)(128)(2,1)} %param.33, bf16[64]{0:T(256)(128)(2,1)} %param.37, bf16[256]{0:T(256)(128)(2,1)} %param.31, ...), dimensions={0} | concatenate | bytes 3072 | tf_op jit(solution)/shard_map/concatenate | solution.py:894
  18.5 23.9 %all-gather.1 = bf16[8,1,768]{2,1,0:T(2,128)(2,1)S(1)} all-gather(bf16[1,1,768]{2,1,0:T(2,128)(2,1)S(1)} %reshape.152), channel_id=2, replica_groups=mesh['fsdp'=8,'seq'=4] {'fsdp'}, dimensions={0}, use_global_device_ids=true | all-gather | bytes 13824 | tf_op jit(solution)/shard_map/all_gather | solution.py:895
  45.0 1.7 copy.63.ids_ref
  47.3 6.8 %prep.1 = (f32[8,2048]{1,0:T(8,128)}, f32[8,1024,128]{2,1,0:T(8,128)}, f32[8,1024,128]{2,1,0:T(8,128)}) custom-call(s32[2]{0:T(128)} %pad_add_fusion.place_ref, bf16[8,768]{1,0:T(8,128)(2,1)} %bitcast.97, f32[8,32]{1,0:T(8,128)} %bitcast.102, f32[32,1152]{1,0:T(8,128)} %constant.24.clone.select_ref), custom_call_target="tpu_custom_call" | custom-call | bytes 9437184 | tf_op jit(solution)/shard_map/prep/pallas_call | solution.py:153
  56.1 1.7 collective-permute-start.4
  57.9 1.4 collective-permute-start.13
  59.6 1.6 collective-permute-start.12
  61.2 3.6 collective-permute-done.5
  64.8 4.5 %collective-permute-start.1 = (bf16[2,512,512]{2,1,0:T(8,128)(2,1)S(1)}, bf16[2,512,512]{2,1,0:T(8,128)(2,1)}, u32[]{:S(2)}, u32[]{:S(2)}) collective-permute-start(bf16[2,512,512]{2,1,0:T(8,128)(2,1)S(1)} %collective-permute-done.rows_ref.x_ref.before_ref), channel_id=1, source_target_pairs={{0,1},{1,2},{2,3},{4,5},{5,6},{6,7},{8,9},{9,10},{10,11},{12,13},{... | collective-permute-start | bytes 3145736 | tf_op jit(solution)/shard_map/ppermute | solution.py:816
  69.3 4.7 %collective-permute-done.4 = bf16[64,1536]{1,0:T(8,128)(2,1)S(1)} collective-permute-done((bf16[64,1536]{1,0:T(8,128)(2,1)}, bf16[64,1536]{1,0:T(8,128)(2,1)S(1)}, u32[]{:S(2)}, u32[]{:S(2)}) %collective-permute-start.4) | collective-permute-done | bytes 196640 | tf_op jit(solution)/shard_map/ppermute | solution.py:821
  73.9 1.1 pad_maximum_fusion.2.near_ref
  77.6 5.1 %take.4.refs_0_ = bf16[2,4,512,512]{3,2,1,0:T(8,128)(2,1)} custom-call(s32[2]{0:T(128)} %pad_add_fusion.place_ref, s32[2,512,4]{2,1,0:T(8,128)} %copy.63.ids_ref, bf16[2,512,512]{2,1,0:T(8,128)(2,1)} %x_ref.3), custom_call_target="tpu_custom_call" | custom-call | flops 2147483648 | bytes 8388608 | tf_op jit(solution)/shard_map/take/pallas_call | solution.py:530
  82.7 2.4 collective-permute-done.11
  85.2 1.2 pad_maximum_fusion.1.near_ref
  86.4 2.9 assemble.3.w_ref
  89.3 5.3 %project.2.q_ref.k_ref.v_ref = bf16[2,512,1536]{2,1,0:T(8,128)(2,1)} custom-call(bf16[2,512,512]{2,1,0:T(8,128)(2,1)} %x_ref.3, f32[8,2048]{1,0:T(8,128)} %get-tuple-element.54.vec_ref, bf16[512,1536]{1,0:T(8,128)(2,1)} %assemble.3.w_ref), custom_call_target="tpu_custom_call" | custom-call | flops 1610612736 | bytes 4194304 | tf_op jit(solution)/shard_map/project/pallas_call | solution.py:208
  94.6 4.6 %project.3.km_ref.vm_ref = bf16[2,512,1024]{2,1,0:T(8,128)(2,1)} custom-call(bf16[2,512,512]{2,1,0:T(8,128)(2,1)} %copy-done.2, f32[8,2048]{1,0:T(8,128)} %get-tuple-element.54.vec_ref, bf16[512,1536]{1,0:T(8,128)(2,1)} %assemble.3.w_ref), custom_call_target="tpu_custom_call" | custom-call | flops 1073741824 | bytes 3145728 | tf_op jit(solution)/shard_map/project/pallas_call | solution.py:208
  99.2 3.8 collective-permute-start.2
  103.0 20.6 %attend.1 = (bf16[2,512,512]{2,1,0:T(8,128)(2,1)}, bf16[2,8,1024,512]{3,2,1,0:T(8,128)(2,1)}) custom-call(bf16[2,512,1536]{2,1,0:T(8,128)(2,1)} %project.2.q_ref.k_ref.v_ref, bf16[2,512,1536]{2,1,0:T(8,128)(2,1)} %project.2.q_ref.k_ref.v_ref, bf16[2,512,1536]{2,1,0:T(8,128)(2,1)} %project.2.q_ref.k_ref.v_ref, bf16[2,512,1024]{2,1,0:T(8,128)(2,1)} %project.3.km_ref.vm_ref, ...), custom_call_target="tpu_custom_call" | custom-call | flops 8589934592 | bytes 25165824 | tf_op jit(solution)/shard_map/attend/pallas_call | solution.py:270
  123.6 5.8 %take.5.refs_0_ = bf16[2,4,512,512]{3,2,1,0:T(8,128)(2,1)} custom-call(s32[2]{0:T(128)} %pad_add_fusion.3.place_ref, s32[2,512,4]{2,1,0:T(8,128)} %copy.63.ids_ref, bf16[2,512,512]{2,1,0:T(8,128)(2,1)} %copy-done.2, bf16[2,4,512,512]{3,2,1,0:T(8,128)(2,1)} %take.4.refs_0_), custom_call_target="tpu_custom_call", output_to_operand_aliasing={{}: (3, {})} | custom-call | flops 2147483648 | bytes 8388608 | tf_op jit(solution)/shard_map/take/pallas_call | solution.py:530
  129.4 3.1 assemble.5
  132.5 5.8 %take.6.refs_0_ = bf16[2,4,512,512]{3,2,1,0:T(8,128)(2,1)} custom-call(s32[2]{0:T(128)} %pad_add_fusion.2.place_ref, s32[2,512,4]{2,1,0:T(8,128)} %copy.63.ids_ref, bf16[2,512,512]{2,1,0:T(8,128)(2,1)} %collective-permute-done.1.rows_ref, bf16[2,4,512,512]{3,2,1,0:T(8,128)(2,1)} %take.5.refs_0_), custom_call_target="tpu_custom_call", output_to_operand_aliasing={{}: (3, {})} | custom-call | flops 2147483648 | bytes 8388608 | tf_op jit(solution)/shard_map/take/pallas_call | solution.py:530
  138.3 1.4 copy-done.4
  139.8 4.9 %assemble.4 = (bf16[512,512]{1,0:T(8,128)(2,1)}, bf16[512,2048]{1,0:T(8,128)(2,1)}, bf16[2048,512]{1,0:T(8,128)(2,1)}) custom-call(s32[2]{0:T(128)} %pad_add_fusion.place_ref, bf16[4,64,4608]{2,1,0:T(8,128)(2,1)} %copy-done, bf16[4,64,4608]{2,1,0:T(8,128)(2,1)} %copy-done.4), custom_call_target="tpu_custom_call" | custom-call | bytes 9437184 | tf_op jit(solution)/shard_map/assemble/pallas_call | solution.py:188
  144.6 12.7 %feed.1 = (f32[1024,512]{1,0:T(8,128)}, bf16[1024,2048]{1,0:T(8,128)(2,1)}, bf16[1024,2048]{1,0:T(8,128)(2,1)}, f32[1024,512]{1,0:T(8,128)}, bf16[1024,512]{1,0:T(8,128)(2,1)}) custom-call(bf16[1024,512]{1,0:T(8,128)(2,1)} %bitcast.5.x_ref, bf16[1024,512]{1,0:T(8,128)(2,1)} %bitcast.107, f32[8,2048]{1,0:T(8,128)} %get-tuple-element.54.vec_ref, ...), custom_call_target="tpu_custom_call" | custom-call | flops 5368709120 | bytes 25165824 | tf_op jit(solution)/shard_map/feed/pallas_call | solution.py:400
  158.3 5.8 %take.7.rows_ref = bf16[2,4,512,512]{3,2,1,0:T(8,128)(2,1)} custom-call(s32[2]{0:T(128)} %pad_add_fusion.1.place_ref, s32[2,512,4]{2,1,0:T(8,128)} %copy.63.ids_ref, bf16[2,512,512]{2,1,0:T(8,128)(2,1)} %copy-done.7, bf16[2,4,512,512]{3,2,1,0:T(8,128)(2,1)} %take.6.refs_0_), custom_call_target="tpu_custom_call", output_to_operand_aliasing={{}: (3, {})} | custom-call | flops 2147483648 | bytes 8388608 | tf_op jit(solution)/shard_map/take/pallas_call | solution.py:530
  164.1 32.3 %near.1 = (bf16[2,512,512]{2,1,0:T(8,128)(2,1)}, bf16[2,4,512,512]{3,2,1,0:T(8,128)(2,1)}, f32[2,512,512]{2,1,0:T(8,128)}, f32[8,512]{1,0:T(8,128)}, bf16[4,64,2...) custom-call(s32[2]{0:T(128)} %pad_add_fusion.place_ref, bf16[2,4,512,512]{3,2,1,0:T(8,128)(2,1)} %take.7.rows_ref, ...), custom_call_target="tpu_custom_call" | custom-call | flops 19864223744 | bytes 14680064 | tf_op jit(solution)/shard_map/near/pallas_call | solution.py:661
  196.4 2.9 collective-permute-done.30
  199.3 1.4 fusion.14
  201.3 1.4 collective-permute-start.33
  202.7 1.5 collective-permute-start.32
  204.2 4.9 %give.5 = bf16[2,512,512]{2,1,0:T(8,128)(2,1)} custom-call(s32[2]{0:T(128)} %pad_add_fusion.1.place_ref, s32[2,4,512]{2,1,0:T(4,128)} %bitcast.98, bf16[2,4,512,512]{3,2,1,0:T(8,128)(2,1)} %get-tuple-element.79.grad_ref), custom_call_target="tpu_custom_call" | custom-call | flops 2147483648 | bytes 4194304 | tf_op jit(solution)/shard_map/give/pallas_call | solution.py:567
  209.2 1.3 collective-permute-start.15
  210.5 4.3 %collective-permute-done.33 = bf16[64,2048]{1,0:T(8,128)(2,1)S(1)} collective-permute-done((bf16[64,2048]{1,0:T(8,128)(2,1)S(1)}, bf16[64,2048]{1,0:T(8,128)(2,1)S(1)}, u32[]{:S(2)}, u32[]{:S(2)}) %collective-permute-start.33) | collective-permute-done | bytes 262176 | tf_op jit(solution)/shard_map/ppermute | solution.py:821
  214.8 1.4 collective-permute-done.32
  216.1 1.1 fusion.9
  217.2 1.6 collective-permute-start.34
  218.8 20.0 %feed_back.1 = (f32[1024,512]{1,0:T(8,128)}, bf16[1024,512]{1,0:T(8,128)(2,1)}, f32[8,2048]{1,0:T(8,128)}, bf16[4,64,4608]{2,1,0:T(8,128)(2,1)}, bf16[4,64,4608]{2,1,0:T(8,128)(2,1)}) custom-call(s32[2]{0:T(128)} %pad_add_fusion.place_ref, f32[1024,512]{1,0:T(8,128)} %bitcast.105, f32[1024,512]{1,0:T(8,128)} %get-tuple-element.68.after_ref, ...), custom_call_target="tpu_custom_call" | custom-call | flops 9663676416 | bytes 33554432 | tf_op jit(solution)/shard_map/feed_back/pallas_call | solution.py:488
  239.9 5.0 %give.6 = bf16[2,512,512]{2,1,0:T(8,128)(2,1)} custom-call(s32[2]{0:T(128)} %pad_add_fusion.2.place_ref, s32[2,4,512]{2,1,0:T(4,128)} %bitcast.99, bf16[2,4,512,512]{3,2,1,0:T(8,128)(2,1)} %get-tuple-element.79.grad_ref, bf16[2,512,512]{2,1,0:T(8,128)(2,1)} %copy-done.15), custom_call_target="tpu_custom_call" | custom-call | flops 2147483648 | bytes 4194304 | tf_op jit(solution)/shard_map/give/pallas_call | solution.py:567
  244.9 1.3 collective-permute-start.16
  246.3 2.6 collective-permute-start.35
  249.0 29.9 %attend_back.1 = (bf16[2,512,512]{2,1,0:T(8,128)(2,1)}, bf16[2,512,512]{2,1,0:T(8,128)(2,1)}, bf16[2,512,512]{2,1,0:T(8,128)(2,1)}, bf16[2,512,512]{2,1,0:T(8,12...) custom-call(bf16[2,512,1536]{2,1,0:T(8,128)(2,1)} %project.2.q_ref.k_ref.v_ref, ...), custom_call_target="tpu_custom_call" | custom-call | flops 17179869184 | bytes 25165824 | tf_op jit(solution)/shard_map/attend_back/pallas_call | solution.py:359
  278.9 1.4 reshape.144.diag_ref
  280.3 5.1 %give.4.own_ref = f32[2,512,512]{2,1,0:T(8,128)} custom-call(s32[2]{0:T(128)} %pad_add_fusion.place_ref, s32[2,4,512]{2,1,0:T(4,128)} %bitcast.100, bf16[2,4,512,512]{3,2,1,0:T(8,128)(2,1)} %get-tuple-element.79.grad_ref), custom_call_target="tpu_custom_call" | custom-call | flops 2147483648 | bytes 4194304 | tf_op jit(solution)/shard_map/give/pallas_call | solution.py:567
  285.4 5.0 %give.7.sent_ref = bf16[2,512,512]{2,1,0:T(8,128)(2,1)} custom-call(s32[2]{0:T(128)} %pad_add_fusion.3.place_ref, s32[2,4,512]{2,1,0:T(4,128)} %bitcast.101, bf16[2,4,512,512]{3,2,1,0:T(8,128)(2,1)} %get-tuple-element.79.grad_ref, bf16[2,512,512]{2,1,0:T(8,128)(2,1)} %collective-permute-done.16.refs_0_), custom_call_target="tpu_custom_call" | custom-call | flops 2147483648 | bytes 4194304 | tf_op jit(solution)/shard_map/give/pallas_call | solution.py:567
  290.5 15.4 %finish.1 = (f32[2,512,512]{2,1,0:T(8,128)}, bf16[2,512,512]{2,1,0:T(8,128)(2,1)}, bf16[4,80,1536]{2,1,0:T(8,128)(2,1)}, bf16[4,80,1536]{2,1,0:T(8,128)(2,1)}) custom-call(s32[2]{0:T(128)} %pad_add_fusion.place_ref, bf16[2,512,512]{2,1,0:T(8,128)(2,1)} %x_ref.3, bf16[2,512,512]{2,1,0:T(8,128)(2,1)} %copy-done.2, ...), custom_call_target="tpu_custom_call" | custom-call | flops 5368709120 | bytes 15728640 | tf_op jit(solution)/shard_map/finish/pallas_call | solution.py:787
  307.0 2.4 collective-permute-start.27
  311.4 1.6 collective-permute-start.17
  313.8 8.8 %collective-permute-done.25 = bf16[64,4608]{1,0:T(8,128)(2,1)S(1)} collective-permute-done((bf16[64,4608]{1,0:T(8,128)(2,1)S(1)}, bf16[64,4608]{1,0:T(8,128)(2,1)S(1)}, u32[]{:S(2)}, u32[]{:S(2)}) %collective-permute-start.25) | collective-permute-done | bytes 589856 | tf_op jit(solution)/shard_map/ppermute | solution.py:821
  322.6 1.5 collective-permute-start.21
  324.1 12.2 %collective-permute-done.27 = bf16[64,4608]{1,0:T(8,128)(2,1)S(1)} collective-permute-done((bf16[64,4608]{1,0:T(8,128)(2,1)S(1)}, bf16[64,4608]{1,0:T(8,128)(2,1)S(1)}, u32[]{:S(2)}, u32[]{:S(2)}) %collective-permute-start.27) | collective-permute-done | bytes 589856 | tf_op jit(solution)/shard_map/ppermute | solution.py:821
  337.6 2.1 collective-permute-start.28
  340.5 5.9 %collective-permute-done.21 = bf16[80,1536]{1,0:T(8,128)(2,1)S(1)} collective-permute-done((bf16[80,1536]{1,0:T(8,128)(2,1)S(1)}, bf16[80,1536]{1,0:T(8,128)(2,1)S(1)}, u32[]{:S(2)}, u32[]{:S(2)}) %collective-permute-start.21) | collective-permute-done | bytes 245792 | tf_op jit(solution)/shard_map/ppermute | solution.py:821
  346.4 2.2 collective-permute-done.20
  348.8 2.1 collective-permute-start.22
  350.9 1.7 convert_add_fusion
  352.6 4.9 %collective-permute-done.22 = bf16[80,1536]{1,0:T(8,128)(2,1)S(1)} collective-permute-done((bf16[80,1536]{1,0:T(8,128)(2,1)S(1)}, bf16[80,1536]{1,0:T(8,128)(2,1)S(1)}, u32[]{:S(2)}, u32[]{:S(2)}) %collective-permute-start.22) | collective-permute-done | bytes 245792 | tf_op jit(solution)/shard_map/ppermute | solution.py:821
  358.7 2.1 collective-permute-start.29
  360.7 22.9 %collective-permute-done.23 = bf16[80,1536]{1,0:T(8,128)(2,1)S(1)} collective-permute-done((bf16[80,1536]{1,0:T(8,128)(2,1)S(1)}, bf16[80,1536]{1,0:T(8,128)(2,1)S(1)}, u32[]{:S(2)}, u32[]{:S(2)}) %collective-permute-start.23) | collective-permute-done | bytes 245792 | tf_op jit(solution)/shard_map/ppermute | solution.py:821
  386.2 9.1 %collective-permute-done.29 = bf16[64,4608]{1,0:T(8,128)(2,1)S(1)} collective-permute-done((bf16[64,4608]{1,0:T(8,128)(2,1)S(1)}, bf16[64,4608]{1,0:T(8,128)(2,1)S(1)}, u32[]{:S(2)}, u32[]{:S(2)}) %collective-permute-start.29) | collective-permute-done | bytes 589856 | tf_op jit(solution)/shard_map/ppermute | solution.py:821
  (108 shorter events, 26.9 us)
Async XLA Ops:
  0.7 13.7 %copy-start.13 = (bf16[64]{0:T(256)(128)(2,1)S(1)}, bf16[64]{0:T(256)(128)(2,1)}, u32[]{:S(2)}) copy-start(bf16[64]{0:T(256)(128)(2,1)} %param.28) | copy-start | bytes 388
  0.7 13.7 %copy-start.12 = (bf16[64]{0:T(256)(128)(2,1)S(1)}, bf16[64]{0:T(256)(128)(2,1)}, u32[]{:S(2)}) copy-start(bf16[64]{0:T(256)(128)(2,1)} %param.24) | copy-start | bytes 388
  0.7 13.7 %copy-start.11 = (bf16[64]{0:T(256)(128)(2,1)S(1)}, bf16[64]{0:T(256)(128)(2,1)}, u32[]{:S(2)}) copy-start(bf16[64]{0:T(256)(128)(2,1)} %param.23) | copy-start | bytes 388
  0.7 54.3 %copy-start.9 = (bf16[64,1024]{1,0:T(8,128)(2,1)S(1)}, bf16[64,1024]{1,0:T(8,128)(2,1)}, u32[]{:S(2)}) copy-start(bf16[64,1024]{1,0:T(8,128)(2,1)} %param.35) | copy-start | bytes 393220
  3.8 52.1 %collective-permute-start.9 = (bf16[64,4608]{1,0:T(8,128)(2,1)S(1)}, bf16[64,4608]{1,0:T(8,128)(2,1)S(1)}, u32[]{:S(2)}, u32[]{:S(2)}) collective-permute-start(bf16[64,4608]{1,0:T(8,128)(2,1)S(1)} %constant_dynamic-update-slice_fusion), channel_id=1, source_target_pairs={{0,24},{4,28},{8,16},{12,20},{16,8},{20,12},{24,0},{28,4},{1,25},{... | collective-permute-start | bytes 1769480 | tf_op jit(solution)/shard_map/ppermute | solution.py:821
  7.8 48.4 %collective-permute-start.8 = (bf16[64,4608]{1,0:T(8,128)(2,1)S(1)}, bf16[64,4608]{1,0:T(8,128)(2,1)S(1)}, u32[]{:S(2)}, u32[]{:S(2)}) collective-permute-start(bf16[64,4608]{1,0:T(8,128)(2,1)S(1)} %constant_dynamic-update-slice_fusion), channel_id=1, source_target_pairs={{0,16},{4,20},{8,24},{12,28},{16,0},{20,4},{24,8},{28,12},{1,17},{... | collective-permute-start | bytes 1769480 | tf_op jit(solution)/shard_map/ppermute | solution.py:821
  8.3 49.6 %collective-permute-start.7 = (bf16[64,4608]{1,0:T(8,128)(2,1)S(1)}, bf16[64,4608]{1,0:T(8,128)(2,1)S(1)}, u32[]{:S(2)}, u32[]{:S(2)}) collective-permute-start(bf16[64,4608]{1,0:T(8,128)(2,1)S(1)} %constant_dynamic-update-slice_fusion), channel_id=1, source_target_pairs={{0,8},{4,12},{8,0},{12,4},{16,24},{20,28},{24,16},{28,20},{1,9},{5... | collective-permute-start | bytes 1769480 | tf_op jit(solution)/shard_map/ppermute | solution.py:821
  8.4 51.2 %collective-permute-start.3 = (bf16[64,1536]{1,0:T(8,128)(2,1)}, bf16[64,1536]{1,0:T(8,128)(2,1)}, u32[]{:S(2)}, u32[]{:S(2)}) collective-permute-start(bf16[64,1536]{1,0:T(8,128)(2,1)} %param.25), channel_id=1, source_target_pairs={{0,8},{4,12},{8,0},{12,4},{16,24},{20,28},{24,16},{28,20},{1,9},{5... | collective-permute-start | bytes 589832 | tf_op jit(solution)/shard_map/ppermute | solution.py:821
  10.3 54.5 %collective-permute-start = (bf16[2,512,512]{2,1,0:T(8,128)(2,1)}, bf16[2,512,512]{2,1,0:T(8,128)(2,1)S(1)}, u32[]{:S(2)}, u32[]{:S(2)}) collective-permute-start(bf16[2,512,512]{2,1,0:T(8,128)(2,1)} %x_ref.3), channel_id=1, source_target_pairs={{0,1},{1,2},{2,3},{4,5},{5,6},{6,7},{8,9},{9,10},{10,11},{12,13},{... | collective-permute-start | bytes 3145736 | tf_op jit(solution)/shard_map/ppermute | solution.py:816
  42.4 0.6 copy-start.10
  55.9 8.9 %collective-permute-start.5 = (bf16[64,1536]{1,0:T(8,128)(2,1)}, bf16[64,1536]{1,0:T(8,128)(2,1)S(1)}, u32[]{:S(2)}, u32[]{:S(2)}) collective-permute-start(bf16[64,1536]{1,0:T(8,128)(2,1)} %param.25), channel_id=1, source_target_pairs={{0,24},{4,28},{8,16},{12,20},{16,8},{20,12},{24,0},{28,4},{1,25},{... | collective-permute-start | bytes 589832 | tf_op jit(solution)/shard_map/ppermute | solution.py:821
  56.1 17.8 %collective-permute-start.4 = (bf16[64,1536]{1,0:T(8,128)(2,1)}, bf16[64,1536]{1,0:T(8,128)(2,1)S(1)}, u32[]{:S(2)}, u32[]{:S(2)}) collective-permute-start(bf16[64,1536]{1,0:T(8,128)(2,1)} %param.25), channel_id=1, source_target_pairs={{0,16},{4,20},{8,24},{12,28},{16,0},{20,4},{24,8},{28,12},{1,17},{... | collective-permute-start | bytes 589832 | tf_op jit(solution)/shard_map/ppermute | solution.py:821
  57.9 18.6 %collective-permute-start.13 = (bf16[64,2048]{1,0:T(8,128)(2,1)S(1)}, bf16[64,2048]{1,0:T(8,128)(2,1)S(1)}, u32[]{:S(2)}, u32[]{:S(2)}) collective-permute-start(bf16[64,2048]{1,0:T(8,128)(2,1)S(1)} %constant_dynamic-update-slice_fusion.3), channel_id=1, source_target_pairs={{0,24},{4,28},{8,16},{12,20},{16,8},{20,12},{24,0},{28,4},{1,25},{... | collective-permute-start | bytes 786440 | tf_op jit(solution)/shard_map/ppermute | solution.py:821
  59.6 23.1 %copy-start = (bf16[4,64,4608]{2,1,0:T(8,128)(2,1)}, bf16[4,64,4608]{2,1,0:T(8,128)(2,1)S(1)}, u32[]{:S(2)}) copy-start(bf16[4,64,4608]{2,1,0:T(8,128)(2,1)S(1)} %pad_maximum_fusion.near_ref) | copy-start | bytes 7077892
  59.6 23.1 %collective-permute-start.12 = (bf16[64,2048]{1,0:T(8,128)(2,1)S(1)}, bf16[64,2048]{1,0:T(8,128)(2,1)}, u32[]{:S(2)}, u32[]{:S(2)}) collective-permute-start(bf16[64,2048]{1,0:T(8,128)(2,1)S(1)} %constant_dynamic-update-slice_fusion.3), channel_id=1, source_target_pairs={{0,16},{4,20},{8,24},{12,28},{16,0},{20,4},{24,8},{28,12},{1,17},{... | collective-permute-start | bytes 786440 | tf_op jit(solution)/shard_map/ppermute | solution.py:821
  64.8 73.6 %collective-permute-start.10 = (bf16[4,64,4608]{2,1,0:T(8,128)(2,1)S(1)}, bf16[4,64,4608]{2,1,0:T(8,128)(2,1)S(1)}, u32[]{:S(2)}, u32[]{:S(2)}) collective-permute-start(bf16[4,64,4608]{2,1,0:T(8,128)(2,1)S(1)} %pad_maximum_fusion.near_ref), channel_id=1, source_target_pairs={{0,4},{4,0},{8,12},{12,8},{16,20},{20,16},{24,28},{28,24},{1,5},{5... | collective-permute-start | bytes 7077896 | tf_op jit(solution)/shard_map/ppermute | solution.py:821
  64.8 17.9 %copy-start.2 = (bf16[2,512,512]{2,1,0:T(8,128)(2,1)}, bf16[2,512,512]{2,1,0:T(8,128)(2,1)S(1)}, u32[]{:S(2)}) copy-start(bf16[2,512,512]{2,1,0:T(8,128)(2,1)S(1)} %collective-permute-done.rows_ref.x_ref.before_ref) | copy-start | bytes 3145732
  64.8 34.4 %collective-permute-start.1 = (bf16[2,512,512]{2,1,0:T(8,128)(2,1)S(1)}, bf16[2,512,512]{2,1,0:T(8,128)(2,1)}, u32[]{:S(2)}, u32[]{:S(2)}) collective-permute-start(bf16[2,512,512]{2,1,0:T(8,128)(2,1)S(1)} %collective-permute-done.rows_ref.x_ref.before_ref), channel_id=1, source_target_pairs={{0,1},{1,2},{2,3},{4,5},{5,6},{6,7},{8,9},{9,10},{10,11},{12,13},{... | collective-permute-start | bytes 3145736 | tf_op jit(solution)/shard_map/ppermute | solution.py:816
  75.0 7.7 %copy-start.3 = (bf16[4,64,1536]{2,1,0:T(8,128)(2,1)}, bf16[4,64,1536]{2,1,0:T(8,128)(2,1)S(1)}, u32[]{:S(2)}) copy-start(bf16[4,64,1536]{2,1,0:T(8,128)(2,1)S(1)} %pad_maximum_fusion.2.near_ref) | copy-start | bytes 2359300
  75.1 11.4 %collective-permute-start.6 = (bf16[4,64,1536]{2,1,0:T(8,128)(2,1)S(1)}, bf16[4,64,1536]{2,1,0:T(8,128)(2,1)}, u32[]{:S(2)}, u32[]{:S(2)}) collective-permute-start(bf16[4,64,1536]{2,1,0:T(8,128)(2,1)S(1)} %pad_maximum_fusion.2.near_ref), channel_id=1, source_target_pairs={{0,4},{4,0},{8,12},{12,8},{16,20},{20,16},{24,28},{28,24},{1,5},{5... | collective-permute-start | bytes 2359304 | tf_op jit(solution)/shard_map/ppermute | solution.py:821
  76.4 8.7 %collective-permute-start.11 = (bf16[64,2048]{1,0:T(8,128)(2,1)S(1)}, bf16[64,2048]{1,0:T(8,128)(2,1)}, u32[]{:S(2)}, u32[]{:S(2)}) collective-permute-start(bf16[64,2048]{1,0:T(8,128)(2,1)S(1)} %constant_dynamic-update-slice_fusion.3), channel_id=1, source_target_pairs={{0,8},{4,12},{8,0},{12,4},{16,24},{20,28},{24,16},{28,20},{1,9},{5... | collective-permute-start | bytes 786440 | tf_op jit(solution)/shard_map/ppermute | solution.py:821
  86.3 8.3 %copy-start.1 = (bf16[4,64,2048]{2,1,0:T(8,128)(2,1)}, bf16[4,64,2048]{2,1,0:T(8,128)(2,1)S(1)}, u32[]{:S(2)}) copy-start(bf16[4,64,2048]{2,1,0:T(8,128)(2,1)S(1)} %pad_maximum_fusion.1.near_ref) | copy-start | bytes 3145732
  86.3 43.1 %collective-permute-start.14 = (bf16[4,64,2048]{2,1,0:T(8,128)(2,1)S(1)}, bf16[4,64,2048]{2,1,0:T(8,128)(2,1)}, u32[]{:S(2)}, u32[]{:S(2)}) collective-permute-start(bf16[4,64,2048]{2,1,0:T(8,128)(2,1)S(1)} %pad_maximum_fusion.1.near_ref), channel_id=1, source_target_pairs={{0,4},{4,0},{8,12},{12,8},{16,20},{20,16},{24,28},{28,24},{1,5},{5... | collective-permute-start | bytes 3145736 | tf_op jit(solution)/shard_map/ppermute | solution.py:821
  99.2 58.1 %collective-permute-start.2 = (bf16[2,512,512]{2,1,0:T(8,128)(2,1)}, bf16[2,512,512]{2,1,0:T(8,128)(2,1)S(1)}, u32[]{:S(2)}, u32[]{:S(2)}) collective-permute-start(bf16[2,512,512]{2,1,0:T(8,128)(2,1)} %collective-permute-done.1.rows_ref), channel_id=1, source_target_pairs={{0,1},{1,2},{2,3},{4,5},{5,6},{6,7},{8,9},{9,10},{10,11},{12,13},{... | collective-permute-start | bytes 3145736 | tf_op jit(solution)/shard_map/ppermute | solution.py:816
  138.3 1.4 copy-start.4
  157.3 1.0 copy-start.7
  196.4 2.9 collective-permute-start.30
  200.7 9.8 %collective-permute-start.31 = (bf16[64,2048]{1,0:T(8,128)(2,1)S(1)}, bf16[64,2048]{1,0:T(8,128)(2,1)S(1)}, u32[]{:S(2)}, u32[]{:S(2)}) collective-permute-start(bf16[64,2048]{1,0:T(8,128)(2,1)S(1)} %get-tuple-element.94), channel_id=1, source_target_pairs={{0,8},{4,12},{8,0},{12,4},{16,24},{20,28},{24,16},{28,20},{1,9},{5... | collective-permute-start | bytes 786440 | tf_op jit(solution)/shard_map/ppermute | solution.py:821
  201.3 13.5 %collective-permute-start.33 = (bf16[64,2048]{1,0:T(8,128)(2,1)S(1)}, bf16[64,2048]{1,0:T(8,128)(2,1)S(1)}, u32[]{:S(2)}, u32[]{:S(2)}) collective-permute-start(bf16[64,2048]{1,0:T(8,128)(2,1)S(1)} %get-tuple-element.95), channel_id=1, source_target_pairs={{0,24},{4,28},{8,16},{12,20},{16,8},{20,12},{24,0},{28,4},{1,25},{... | collective-permute-start | bytes 786440 | tf_op jit(solution)/shard_map/ppermute | solution.py:821
  202.7 13.4 %collective-permute-start.32 = (bf16[64,2048]{1,0:T(8,128)(2,1)S(1)}, bf16[64,2048]{1,0:T(8,128)(2,1)S(1)}, u32[]{:S(2)}, u32[]{:S(2)}) collective-permute-start(bf16[64,2048]{1,0:T(8,128)(2,1)S(1)} %get-tuple-element.96), channel_id=1, source_target_pairs={{0,16},{4,20},{8,24},{12,28},{16,0},{20,4},{24,8},{28,12},{1,17},{... | collective-permute-start | bytes 786440 | tf_op jit(solution)/shard_map/ppermute | solution.py:821
  209.2 29.7 %collective-permute-start.15 = (bf16[2,512,512]{2,1,0:T(8,128)(2,1)}, bf16[2,512,512]{2,1,0:T(8,128)(2,1)S(1)}, u32[]{:S(2)}, u32[]{:S(2)}) collective-permute-start(bf16[2,512,512]{2,1,0:T(8,128)(2,1)} %give.5), channel_id=1, source_target_pairs={{1,0},{2,1},{3,2},{5,4},{6,5},{7,6},{9,8},{10,9},{11,10},{13,12},{... | collective-permute-start | bytes 3145736 | tf_op jit(solution)/shard_map/ppermute | solution.py:816
  217.2 29.0 %collective-permute-start.34 = (bf16[64,2048]{1,0:T(8,128)(2,1)S(1)}, bf16[64,2048]{1,0:T(8,128)(2,1)S(1)}, u32[]{:S(2)}, u32[]{:S(2)}) collective-permute-start(bf16[64,2048]{1,0:T(8,128)(2,1)S(1)} %fusion.9), channel_id=1, source_target_pairs={{0,1},{1,0},{2,3},{3,2},{4,5},{5,4},{6,7},{7,6},{8,9},{9,8},{10,11... | collective-permute-start | bytes 786440 | tf_op jit(solution)/shard_map/ppermute | solution.py:821
  238.8 67.2 %collective-permute-start.24 = (bf16[4,64,4608]{2,1,0:T(8,128)(2,1)}, bf16[4,64,4608]{2,1,0:T(8,128)(2,1)S(1)}, u32[]{:S(2)}, u32[]{:S(2)}) collective-permute-start(bf16[4,64,4608]{2,1,0:T(8,128)(2,1)} %get-tuple-element.88), channel_id=1, source_target_pairs={{0,4},{4,0},{8,12},{12,8},{16,20},{20,16},{24,28},{28,24},{1,5},{5... | collective-permute-start | bytes 7077896 | tf_op jit(solution)/shard_map/ppermute | solution.py:821
  238.9 1.0 copy-start.15
  244.9 40.5 %collective-permute-start.16 = (bf16[2,512,512]{2,1,0:T(8,128)(2,1)}, bf16[2,512,512]{2,1,0:T(8,128)(2,1)}, u32[]{:S(2)}, u32[]{:S(2)}) collective-permute-start(bf16[2,512,512]{2,1,0:T(8,128)(2,1)} %give.6), channel_id=1, source_target_pairs={{1,0},{2,1},{3,2},{5,4},{6,5},{7,6},{9,8},{10,9},{11,10},{13,12},{... | collective-permute-start | bytes 3145736 | tf_op jit(solution)/shard_map/ppermute | solution.py:816
  246.3 39.1 %collective-permute-start.35 = (bf16[64,2048]{1,0:T(8,128)(2,1)S(1)}, bf16[64,2048]{1,0:T(8,128)(2,1)S(1)}, u32[]{:S(2)}, u32[]{:S(2)}) collective-permute-start(bf16[64,2048]{1,0:T(8,128)(2,1)S(1)} %add_convert_fusion.5), channel_id=1, source_target_pairs={{0,2},{1,3},{2,0},{3,1},{4,6},{5,7},{6,4},{7,5},{8,10},{9,11},{10,... | collective-permute-start | bytes 786440 | tf_op jit(solution)/shard_map/ppermute | solution.py:821
  290.5 15.5 %copy-start.5 = (bf16[4,64,4608]{2,1,0:T(8,128)(2,1)S(1)}, bf16[4,64,4608]{2,1,0:T(8,128)(2,1)}, u32[]{:S(2)}) copy-start(bf16[4,64,4608]{2,1,0:T(8,128)(2,1)} %get-tuple-element.87) | copy-start | bytes 7077892
  305.9 7.1 %collective-permute-start.18 = (bf16[4,80,1536]{2,1,0:T(8,128)(2,1)}, bf16[4,80,1536]{2,1,0:T(8,128)(2,1)S(1)}, u32[]{:S(2)}, u32[]{:S(2)}) collective-permute-start(bf16[4,80,1536]{2,1,0:T(8,128)(2,1)} %get-tuple-element.86), channel_id=1, source_target_pairs={{0,4},{4,0},{8,12},{12,8},{16,20},{20,16},{24,28},{28,24},{1,5},{5... | collective-permute-start | bytes 2949128 | tf_op jit(solution)/shard_map/ppermute | solution.py:821
  306.0 5.4 %copy-start.14 = (bf16[2,512,512]{2,1,0:T(8,128)(2,1)S(1)}, bf16[2,512,512]{2,1,0:T(8,128)(2,1)}, u32[]{:S(2)}) copy-start(bf16[2,512,512]{2,1,0:T(8,128)(2,1)} %get-tuple-element.84) | copy-start | bytes 3145732
  306.0 7.0 %copy-start.8 = (bf16[4,80,1536]{2,1,0:T(8,128)(2,1)S(1)}, bf16[4,80,1536]{2,1,0:T(8,128)(2,1)}, u32[]{:S(2)}) copy-start(bf16[4,80,1536]{2,1,0:T(8,128)(2,1)} %get-tuple-element.85) | copy-start | bytes 2949124
  306.4 16.2 %collective-permute-start.25 = (bf16[64,4608]{1,0:T(8,128)(2,1)S(1)}, bf16[64,4608]{1,0:T(8,128)(2,1)S(1)}, u32[]{:S(2)}, u32[]{:S(2)}) collective-permute-start(bf16[64,4608]{1,0:T(8,128)(2,1)S(1)} %get-tuple-element.91), channel_id=1, source_target_pairs={{0,8},{4,12},{8,0},{12,4},{16,24},{20,28},{24,16},{28,20},{1,9},{5... | collective-permute-start | bytes 1769480 | tf_op jit(solution)/shard_map/ppermute | solution.py:821
  307.0 29.2 %collective-permute-start.27 = (bf16[64,4608]{1,0:T(8,128)(2,1)S(1)}, bf16[64,4608]{1,0:T(8,128)(2,1)S(1)}, u32[]{:S(2)}, u32[]{:S(2)}) collective-permute-start(bf16[64,4608]{1,0:T(8,128)(2,1)S(1)} %get-tuple-element.92), channel_id=1, source_target_pairs={{0,24},{4,28},{8,16},{12,20},{16,8},{20,12},{24,0},{28,4},{1,25},{... | collective-permute-start | bytes 1769480 | tf_op jit(solution)/shard_map/ppermute | solution.py:821
  309.4 27.8 %collective-permute-start.26 = (bf16[64,4608]{1,0:T(8,128)(2,1)S(1)}, bf16[64,4608]{1,0:T(8,128)(2,1)S(1)}, u32[]{:S(2)}, u32[]{:S(2)}) collective-permute-start(bf16[64,4608]{1,0:T(8,128)(2,1)S(1)} %get-tuple-element.93), channel_id=1, source_target_pairs={{0,16},{4,20},{8,24},{12,28},{16,0},{20,4},{24,8},{28,12},{1,17},{... | collective-permute-start | bytes 1769480 | tf_op jit(solution)/shard_map/ppermute | solution.py:821
  311.4 39.5 %collective-permute-start.17 = (bf16[2,512,512]{2,1,0:T(8,128)(2,1)S(1)}, bf16[2,512,512]{2,1,0:T(8,128)(2,1)S(1)}, u32[]{:S(2)}, u32[]{:S(2)}) collective-permute-start(bf16[2,512,512]{2,1,0:T(8,128)(2,1)S(1)} %copy-done.14), channel_id=1, source_target_pairs={{1,0},{2,1},{3,2},{5,4},{6,5},{7,6},{9,8},{10,9},{11,10},{13,12},{... | collective-permute-start | bytes 3145736 | tf_op jit(solution)/shard_map/ppermute | solution.py:816
  313.2 27.4 %collective-permute-start.19 = (bf16[80,1536]{1,0:T(8,128)(2,1)S(1)}, bf16[80,1536]{1,0:T(8,128)(2,1)S(1)}, u32[]{:S(2)}, u32[]{:S(2)}) collective-permute-start(bf16[80,1536]{1,0:T(8,128)(2,1)S(1)} %get-tuple-element.97), channel_id=1, source_target_pairs={{0,8},{4,12},{8,0},{12,4},{16,24},{20,28},{24,16},{28,20},{1,9},{5... | collective-permute-start | bytes 737288 | tf_op jit(solution)/shard_map/ppermute | solution.py:821
  322.6 23.9 %collective-permute-start.21 = (bf16[80,1536]{1,0:T(8,128)(2,1)S(1)}, bf16[80,1536]{1,0:T(8,128)(2,1)S(1)}, u32[]{:S(2)}, u32[]{:S(2)}) collective-permute-start(bf16[80,1536]{1,0:T(8,128)(2,1)S(1)} %get-tuple-element.98), channel_id=1, source_target_pairs={{0,24},{4,28},{8,16},{12,20},{16,8},{20,12},{24,0},{28,4},{1,25},{... | collective-permute-start | bytes 737288 | tf_op jit(solution)/shard_map/ppermute | solution.py:821
  336.2 14.7 %copy-start.6 = (f32[2,512,512]{2,1,0:T(8,128)S(1)}, f32[2,512,512]{2,1,0:T(8,128)}, u32[]{:S(2)}) copy-start(f32[2,512,512]{2,1,0:T(8,128)} %get-tuple-element.83) | copy-start | bytes 6291460
  336.2 12.4 %collective-permute-start.20 = (bf16[80,1536]{1,0:T(8,128)(2,1)S(1)}, bf16[80,1536]{1,0:T(8,128)(2,1)S(1)}, u32[]{:S(2)}, u32[]{:S(2)}) collective-permute-start(bf16[80,1536]{1,0:T(8,128)(2,1)S(1)} %get-tuple-element.99), channel_id=1, source_target_pairs={{0,16},{4,20},{8,24},{12,28},{16,0},{20,4},{24,8},{28,12},{1,17},{... | collective-permute-start | bytes 737288 | tf_op jit(solution)/shard_map/ppermute | solution.py:821
  337.6 20.9 %collective-permute-start.28 = (bf16[64,4608]{1,0:T(8,128)(2,1)S(1)}, bf16[64,4608]{1,0:T(8,128)(2,1)S(1)}, u32[]{:S(2)}, u32[]{:S(2)}) collective-permute-start(bf16[64,4608]{1,0:T(8,128)(2,1)S(1)} %fusion.2), channel_id=1, source_target_pairs={{0,1},{1,0},{2,3},{3,2},{4,5},{5,4},{6,7},{7,6},{8,9},{9,8},{10,11... | collective-permute-start | bytes 1769480 | tf_op jit(solution)/shard_map/ppermute | solution.py:821
  348.8 8.7 %collective-permute-start.22 = (bf16[80,1536]{1,0:T(8,128)(2,1)S(1)}, bf16[80,1536]{1,0:T(8,128)(2,1)S(1)}, u32[]{:S(2)}, u32[]{:S(2)}) collective-permute-start(bf16[80,1536]{1,0:T(8,128)(2,1)S(1)} %fusion.12), channel_id=1, source_target_pairs={{0,1},{1,0},{2,3},{3,2},{4,5},{5,4},{6,7},{7,6},{8,9},{9,8},{10,11... | collective-permute-start | bytes 737288 | tf_op jit(solution)/shard_map/ppermute | solution.py:821
  357.5 26.1 %collective-permute-start.23 = (bf16[80,1536]{1,0:T(8,128)(2,1)S(1)}, bf16[80,1536]{1,0:T(8,128)(2,1)S(1)}, u32[]{:S(2)}, u32[]{:S(2)}) collective-permute-start(bf16[80,1536]{1,0:T(8,128)(2,1)S(1)} %add_convert_fusion.10), channel_id=1, source_target_pairs={{0,2},{1,3},{2,0},{3,1},{4,6},{5,7},{6,4},{7,5},{8,10},{9,11},{10,... | collective-permute-start | bytes 737288 | tf_op jit(solution)/shard_map/ppermute | solution.py:821
  358.7 36.6 %collective-permute-start.29 = (bf16[64,4608]{1,0:T(8,128)(2,1)S(1)}, bf16[64,4608]{1,0:T(8,128)(2,1)S(1)}, u32[]{:S(2)}, u32[]{:S(2)}) collective-permute-start(bf16[64,4608]{1,0:T(8,128)(2,1)S(1)} %add_convert_fusion), channel_id=1, source_target_pairs={{0,2},{1,3},{2,0},{3,1},{4,6},{5,7},{6,4},{7,5},{8,10},{9,11},{10,... | collective-permute-start | bytes 1769480 | tf_op jit(solution)/shard_map/ppermute | solution.py:821

commit v2 on v1

v2 whole, which is shorter than its diff:
```python
import functools
import math

import jax
import jax.numpy as jnp
import numpy as np
from jax import lax
from jax.experimental import pallas as pl
from jax.experimental.pallas import tpu as pltpu
from jax.sharding import PartitionSpec as P

D = 512
H = 8
HD = 64
K = 4
SEG = 512
NB = 32

EPS = 1e-05
HIGH = lax.Precision.HIGHEST
MASKED = -1e30
F32 = jnp.float32
BF16 = jnp.bfloat16
ROWS = 256
SPAN = 2 * SEG + 128
VMEM = 56 << 20


def nn(left, right):
    return lax.dot_general(left, right, (((1,), (0,)), ((), ())), preferred_element_type=F32)


def nt(left, right):
    return lax.dot_general(left, right, (((1,), (1,)), ((), ())), preferred_element_type=F32)


def tn(left, right):
    return lax.dot_general(left, right, (((0,), (0,)), ((), ())), preferred_element_type=F32)


def shape(dims, dtype):
    return jax.ShapeDtypeStruct(tuple(dims), dtype)


def whole(dims):
    zeros = (0,) * len(dims)
    return pl.BlockSpec(tuple(dims), lambda *_: zeros, pipeline_mode=pl.Buffered(1))


def scalars():
    return pl.BlockSpec(memory_space=pltpu.SMEM)


def params(grid_rank):
    return pltpu.CompilerParams(
        dimension_semantics=("arbitrary",) * grid_rank, vmem_limit_bytes=VMEM
    )


def cost(flops, moved, exps=0):
    return pl.CostEstimate(
        flops=int(flops / 30), bytes_accessed=int(moved / 30), transcendentals=int(exps / 30)
    )


def thresholds():
    half_count = NB // 2
    spread_ratio = 2.0 * SEG / half_count
    exact_part = list(range(1, half_count))
    log_part = [
        int(half_count * spread_ratio ** ((bucket_index - half_count) / half_count))
        for bucket_index in range(half_count, NB)
    ]
    return np.array(exact_part + log_part)


def bucket_of(distance):
    return (distance[:, None] >= thresholds()[None, :]).sum(axis=1)


def forward_selector():
    distance = np.arange(SPAN) - 128
    bucket = bucket_of(np.maximum(distance, 0))
    return (np.arange(NB)[:, None] == bucket[None, :]).astype(np.float32)


def backward_selector():
    chosen = forward_selector().T.copy()
    chosen[:128] = 0.0
    return chosen


def norm(values):
    average = jnp.mean(values, axis=-1, keepdims=True)
    centred = values - average
    variance = jnp.mean(centred * centred, axis=-1, keepdims=True)
    rstd_value = lax.rsqrt(variance + EPS)
    return centred * rstd_value, rstd_value


def norm_back(grad_result, hat_value, rstd_value, gain):
    scaled = grad_result * gain
    return rstd_value * (
        scaled
        - jnp.mean(scaled, axis=-1, keepdims=True)
        - hat_value * jnp.mean(scaled * hat_value, axis=-1, keepdims=True)
    )


def rows_sum(values):
    return jnp.sum(values, axis=0, keepdims=True)


def pair_mask(head, values):
    lane = lax.broadcasted_iota(jnp.int32, values.shape, 1)
    keep = lane < HD if head == 0 else lane >= HD
    return jnp.where(keep, values, jnp.zeros_like(values))


def pack_first_kernel(*refs):
    weight_ref, *vector_refs, out_ref = refs
    rows = weight_ref.shape[0]
    out_ref[:rows, :] = weight_ref[...]
    out_ref[rows:, :] = jnp.zeros((16, out_ref.shape[1]), BF16)
    for index, ref in enumerate(vector_refs):
        line = ref[...].astype(F32).reshape(1, -1).astype(BF16)
        out_ref[rows + index : rows + index + 1, : ref.shape[0]] = line


def pack_first(weight, vectors):
    rows, columns = weight.shape
    return pl.pallas_call(
        pack_first_kernel,
        out_shape=shape((rows + 16, columns), BF16),
        cost_estimate=cost(0, 4 * rows * columns),
        name="pack_first",
    )(weight, *vectors)


def pack_kernel(rows, *refs):
    out_ref = refs[-1]
    start = 0
    for ref in refs[:-1]:
        for chunk in range(ref.shape[0] // rows):
            out_ref[:, start : start + ref.shape[1]] = ref[chunk * rows : (chunk + 1) * rows, :]
            start += ref.shape[1]


def pack(rows, weights):
    columns = sum(w.size for w in weights) // rows
    return pl.pallas_call(
        functools.partial(pack_kernel, rows),
        out_shape=shape((rows, columns), BF16),
        cost_estimate=cost(0, 4 * rows * columns),
        name="pack",
    )(*weights)


def unpack_kernel(layout, terms, *refs):
    total = functools.reduce(jnp.add, [ref[...].astype(F32) for ref in refs[:terms]])
    refs = refs[terms:]
    rows = refs[0].shape[0]
    start = 0
    for ref, (chunks, width) in zip(refs, layout):
        for chunk in range(chunks):
            ref[chunk * rows : (chunk + 1) * rows, :] = total[:rows, start : start + width]
            start += width
    for index, ref in enumerate(refs[len(layout) :]):
        ref[...] = total[rows + index : rows + index + 1, : ref.shape[0]].reshape(-1)


def unpack(pair, layout, widths=()):
    rows = pair[0].shape[0] - (16 if widths else 0)
    outs = [shape((rows * chunks, width), F32) for chunks, width in layout]
    outs += [shape((width,), F32) for width in widths]
    return pl.pallas_call(
        functools.partial(unpack_kernel, layout, len(pair)),
        out_shape=outs,
        cost_estimate=cost(0, 8 * pair[0].size),
        name="unpack",
    )(*pair)


def device_of(place_ref, chip_step, core_step):
    index = place_ref[0]
    chip = lax.shift_right_logical(index, 1)
    core = jnp.bitwise_and(index, 1)
    return jnp.bitwise_xor(chip, chip_step) * 2 + jnp.bitwise_xor(core, core_step)


def assemble(place_ref, layout, piece_refs, out_refs):
    steps = len(piece_refs) // 2
    for core_step in range(2):
        for step in range(steps):
            ref = piece_refs[core_step * steps + step]
            owner = device_of(place_ref, step, core_step)
            rows = D // (2 * steps)
            start = 0
            for out_ref, (chunks, width) in zip(out_refs, layout):
                for chunk in range(chunks):
                    target = pl.multiple_of((owner * chunks + chunk) * rows, rows)
                    out_ref[pl.ds(target, rows), :] = ref[:rows, start : start + width]
                    start += width


def first_kernel(parts, count, place_ref, x_ref, before_ref, select_ref, *refs):
    piece_refs = refs[:count]
    w_ref, vec_ref, line_ref, joined_ref, memory_ref, small_ref = refs[count:]

    @pl.when(pl.program_id(0) == 0)
    def _():
        assemble(place_ref, ((1, 3 * D),), piece_refs, [w_ref])
        steps = count // 2
        rows = D // count
        for core_step in range(2):
            for step in range(steps):
                owner = device_of(place_ref, step, core_step)
                small_ref[pl.ds(pl.multiple_of(owner * 16, 16), 16), :] = piece_refs[
                    core_step * steps + step
                ][rows:, : small_ref.shape[1]].astype(F32)
        vec_ref[...] = jnp.zeros_like(vec_ref)
        for row, width in enumerate(parts):
            pieces = [small_ref[16 * d + row : 16 * d + row + 1, :width] for d in range(count)]
            vec_ref[row : row + 1, : width * count] = jnp.concatenate(pieces, axis=1)
        row = len(parts)
        table = jnp.concatenate(
            [small_ref[16 * d + row : 16 * d + row + 1, : NB * H // count] for d in range(count)],
            axis=0,
        )
        by_distance = None
        for place in range(NB // count):
            part = lax.dot_general(
                table[:, place * H : (place + 1) * H],
                select_ref[place],
                (((0,), (0,)), ((), ())),
                precision=HIGH,
                preferred_element_type=F32,
            )
            by_distance = part if by_distance is None else by_distance + part
        lane = lax.broadcasted_iota(jnp.int32, by_distance.shape, 1)
        line_ref[...] = jnp.where(lane < 128, MASKED, by_distance)

    for ref, out_ref, first in ((x_ref, joined_ref, 0), (before_ref, memory_ref, D)):
        hat_value, _ = norm(ref[0].astype(F32))
        normed = (hat_value * vec_ref[0:1, :D] + vec_ref[1:2, :D]).astype(BF16)
        out_ref[0] = nn(normed, w_ref[:, first:]).astype(BF16)


def first(place, x, before, pieces, parts, ff):
    batch = x.shape[0]
    count = len(pieces)
    small_width = -(-max(parts) // 128) * 128
    select = forward_selector().reshape(count, NB // count, SPAN).transpose(1, 0, 2)

    def block(width):
        return pl.BlockSpec((1, SEG, width), lambda b: (b, 0, 0))

    return pl.pallas_call(
        functools.partial(first_kernel, parts, count),
        grid=(batch,),
        in_specs=[scalars(), block(D), block(D), whole(select.shape)]
        + [whole(piece.shape) for piece in pieces],
        out_specs=[whole((D, 3 * D)), whole((8, ff)), whole((H, SPAN)), block(3 * D), block(2 * D)],
        out_shape=[
            shape((D, 3 * D), BF16),
            shape((8, ff), F32),
            shape((H, SPAN), F32),
            shape((batch, SEG, 3 * D), BF16),
            shape((batch, SEG, 2 * D), BF16),
        ],
        scratch_shapes=[pltpu.VMEM((16 * count, small_width), F32)],
        compiler_params=params(1),
        cost_estimate=cost(10 * batch * SEG * D * D, 8 * batch * SEG * D),
        name="first",
    )(place, x, before, jnp.asarray(select), *pieces)


def tiles(place_ref, line_ref, first, own_ref, mem_ref):
    hidden = jnp.where(place_ref[1] > 0, 0.0, MASKED)
    for head in range(2):
        index = 2 * (first + pl.program_id(0)) + head
        line = jnp.broadcast_to(line_ref[pl.ds(index, 1), :], (8, SPAN))
        line = pltpu.roll(line, 0, 1, stride=1, stride_axis=0)
        for group in range(16):
            moved = pltpu.roll(line, 8 * group, 1) if group else line
            for tile in range(2 * SEG // 128):
                start = 2 * SEG - 128 * tile
                row = 128 * tile + 8 * group
                piece = moved[:, start : start + 128]
                own_ref[head, row : row + 8, :] = piece
                mem_ref[head, row : row + 8, :] = piece + hidden


def attend_kernel(first, place_ref, q_ref, k_ref, v_ref, km_ref, vm_ref, line_ref, *refs):
    out_ref, prob_ref, own_ref, mem_ref = refs[-4:]

    @pl.when(pl.program_id(1) == 0)
    def _():
        tiles(place_ref, line_ref, first, own_ref, mem_ref)

    keys = jnp.concatenate([km_ref[0], k_ref[0]], axis=0)
    values = jnp.concatenate([vm_ref[0], v_ref[0]], axis=0)
    for half in range(SEG // ROWS):
        width = SEG + (half + 1) * ROWS
        span = slice(half * ROWS, (half + 1) * ROWS)
        query = q_ref[0, span, :] * BF16(HD**-0.5)
        total = None
        for head in range(2):
            scores = nt(keys[:width], pair_mask(head, query))
            columns = []
            for part in range(ROWS // 128):
                block = half * (ROWS // 128) + part
                bias = jnp.concatenate(
                    [
                        mem_ref[head, (3 - block) * 128 : (7 - block) * 128, :],
                        own_ref[head, (7 - block) * 128 :, :],
                    ],
                    axis=0,
                )
                used = bias.shape[0]
                piece = scores[:used, part * 128 : (part + 1) * 128] + bias
                top = jnp.max(piece, axis=0, keepdims=True)
                weight = jnp.exp(piece - top)
                weight = (weight * (1.0 / jnp.sum(weight, axis=0, keepdims=True))).astype(BF16)
                if used < width:
                    weight = jnp.concatenate(
                        [weight, jnp.zeros((width - used, 128), BF16)], axis=0
                    )
                columns.append(weight)
            probs = jnp.concatenate(columns, axis=1)
            prob_ref[0, head, :width, span] = probs
            product = tn(probs, pair_mask(head, values)[:width])
            total = product if total is None else total + product
        out_ref[0, span, :] = total.astype(BF16)


PAIRS = H // 4


def attend(place, joined, memory, line, first, so_far):
    batch = joined.shape[0]

    def lanes(offset):
        return pl.BlockSpec((1, SEG, 128), lambda h, b: (b, 0, offset + first + h))

    work = batch * H * SEG * SEG
    extra = [] if so_far is None else [so_far]
    return pl.pallas_call(
        functools.partial(attend_kernel, first),
        grid=(PAIRS, batch),
        in_specs=[scalars()]
        + [lanes(0), lanes(2 * PAIRS), lanes(4 * PAIRS), lanes(0), lanes(2 * PAIRS)]
        + [whole(line.shape)]
        + [pl.BlockSpec(memory_space=pl.ANY)] * len(extra),
        out_specs=[
            lanes(0),
            pl.BlockSpec((1, 2, 2 * SEG, SEG), lambda h, b: (b, h, 0, 0)),
        ],
        out_shape=[shape((batch, SEG, D), BF16), shape((batch, H // 2, 2 * SEG, SEG), BF16)],
        scratch_shapes=[pltpu.VMEM((2, 2 * SEG, 128), F32)] * 2,
        input_output_aliases={7: 0} if extra else {},
        compiler_params=params(2),
        cost_estimate=cost(16 * HD * work, 3 * work, work),
        name="attend",
    )(place, joined, joined, joined, memory, memory, line, *extra)


def attend_back_kernel(
    q_ref, k_ref, v_ref, km_ref, vm_ref, grad_ref, out_ref, prob_ref, *refs
):
    dq_ref, dk_ref, dv_ref, dkm_ref, dvm_ref, diag_ref, grid_ref = refs[-7:]
    keys = jnp.concatenate([km_ref[0], k_ref[0]], axis=0)
    values = jnp.concatenate([vm_ref[0], v_ref[0]], axis=0)
    step = pl.program_id(1)

    @pl.when(step == 0)
    def _():
        grid_ref[...] = jnp.zeros_like(grid_ref)

    key_parts = []
    value_parts = []
    for half in range(SEG // ROWS):
        width = SEG + (half + 1) * ROWS
        span = slice(half * ROWS, (half + 1) * ROWS)
        grad = grad_ref[0, span, :]
        query = q_ref[0, span, :] * BF16(HD**-0.5)
        product = (grad.astype(F32) * out_ref[0, span, :].astype(F32)).T
        query_total = key_total = value_total = None
        for head in range(2):
            grad_head = pair_mask(head, grad)
            delta = jnp.sum(product[head * HD : (head + 1) * HD], axis=0, keepdims=True)
            probs = prob_ref[0, head, :width, span]
            scored = probs.astype(F32) * (nt(values[:width], grad_head) - delta)
            for part in range(ROWS // 128):
                block = half * (ROWS // 128) + part
                used = SEG + (block + 1) * 128
                grid_ref[head, (3 - block) * 128 :, :] += scored[
                    :used, part * 128 : (part + 1) * 128
                ]
            scored = scored.astype(BF16)
            for_key = nn(scored, pair_mask(head, query))
            for_value = nn(probs, grad_head)
            for_query = tn(scored, pair_mask(head, keys)[:width])
            key_total = for_key if key_total is None else key_total + for_key
            value_total = for_value if value_total is None else value_total + for_value
            query_total = for_query if query_total is None else query_total + for_query
        dq_ref[0, span, :] = (query_total * HD**-0.5).astype(BF16)
        key_parts.append(key_total)
        value_parts.append(value_total)
    for pieces, mem_ref, own_ref in (
        (key_parts, dkm_ref, dk_ref),
        (value_parts, dvm_ref, dv_ref),
    ):
        both = pieces[0] + pieces[1][: SEG + ROWS]
        mem_ref[0] = both[:SEG].astype(BF16)
        own_ref[0, :ROWS] = both[SEG:].astype(BF16)
        own_ref[0, ROWS:] = pieces[1][SEG + ROWS :].astype(BF16)

    @pl.when(step == pl.num_programs(1) - 1)
    def _():
        for head in range(2):
            total = None
            for group in range(16):
                pieces = [
                    grid_ref[head, 128 * tile + 8 * group : 128 * tile + 8 * group + 8, :]
                    for tile in reversed(range(2 * SEG // 128))
                ]
                line = jnp.concatenate([jnp.zeros((8, 128), F32)] + pieces, axis=1)
                if group:
                    line = pltpu.roll(line, SPAN - 8 * group, 1)
                total = line if total is None else total + line
            lines = [total[:1]] + [
                pltpu.roll(total[row : row + 1], SPAN - row, 1) for row in range(1, 8)
            ]
            diag_ref[0, head : head + 1, :] = functools.reduce(jnp.add, lines)


def attend_back(joined, memory, grad, attended, probs, first, so_far):
    batch = joined.shape[0]

    def lanes(offset):
        return pl.BlockSpec((1, SEG, 128), lambda h, b: (b, 0, offset + first + h))

    half = shape((batch, SEG, D), BF16)
    work = batch * H * SEG * SEG
    return pl.pallas_call(
        attend_back_kernel,
        grid=(PAIRS, batch),
        in_specs=[lanes(0), lanes(2 * PAIRS), lanes(4 * PAIRS), lanes(0), lanes(2 * PAIRS)]
        + [lanes(0)] * 2
        + [pl.BlockSpec((1, 2, 2 * SEG, SEG), lambda h, b: (b, h, 0, 0))]
        + [pl.BlockSpec(memory_space=pl.ANY)] * len(so_far),
        out_specs=[lanes(0)] * 5 + [pl.BlockSpec((1, 2, SPAN), lambda h, b: (h, 0, 0))],
        out_shape=[half] * 5 + [shape((PAIRS, 2, SPAN), F32)],
        scratch_shapes=[pltpu.VMEM((2, 2 * SEG, 128), F32)],
        input_output_aliases={8 + i: i for i in range(len(so_far))},
        compiler_params=params(2),
        cost_estimate=cost(32 * HD * work, 3 * work),
        name="attend_back",
    )(joined, joined, joined, memory, memory, grad, attended, probs, *so_far)


def feed_layout(ff):
    return ((1, D), (1, ff), (ff // D, D))


def feed_scratch(ff):
    return [pltpu.VMEM((D, D), BF16), pltpu.VMEM((D, ff), BF16), pltpu.VMEM((ff, D), BF16)]


def feed_kernel(count, place_ref, x_ref, att_ref, vec_ref, *refs):
    piece_refs = refs[:count]
    (
        after_attn_ref, active_ref, slope_ref, after_ffn_ref, merge_ref, expand_ref, reduce_ref,
    ) = refs[count:]

    @pl.when(pl.program_id(0) == 0)
    def _():
        assemble(place_ref, feed_layout(expand_ref.shape[1]), piece_refs, refs[-3:])

    after_attn = x_ref[...].astype(F32) + nn(att_ref[...], merge_ref[...])
    after_attn_ref[...] = after_attn
    hat_value, _ = norm(after_attn)
    normed = (hat_value * vec_ref[2:3, :D] + vec_ref[3:4, :D]).astype(BF16)
    pre = nn(normed, expand_ref[...]) + vec_ref[6:7, :]
    cdf = 0.5 * (1.0 + lax.erf(pre * (1.0 / math.sqrt(2.0))))
    slope = cdf + pre * jnp.exp(-0.5 * pre * pre) * (1.0 / math.sqrt(2.0 * math.pi))
    slope_ref[...] = slope.astype(BF16)
    active = (pre * cdf).astype(BF16)
    active_ref[...] = active
    after_ffn = after_attn + nn(active, reduce_ref[...]) + vec_ref[4:5, :D]
    after_ffn_ref[...] = after_ffn


def feed(place, x, attended, vec, pieces):
    count = x.shape[0]
    ff = vec.shape[1]

    def rows(width):
        return pl.BlockSpec((ROWS, width), lambda i: (i, 0))

    return pl.pallas_call(
        functools.partial(feed_kernel, len(pieces)),
        grid=(count // ROWS,),
        in_specs=[scalars(), rows(D), rows(D), whole(vec.shape)]
        + [whole(piece.shape) for piece in pieces],
        out_specs=[rows(D), rows(ff), rows(ff), rows(D)],
        out_shape=[
            shape((count, D), F32),
            shape((count, ff), BF16),
            shape((count, ff), BF16),
            shape((count, D), F32),
        ],
        scratch_shapes=feed_scratch(ff),
        compiler_params=params(1),
        cost_estimate=cost(4 * count * D * (ff + D), 12 * count * ff, 2 * count * ff),
        name="feed",
    )(place, x, attended, vec, *pieces)


def add_rows(ref, row, values):
    ref[row : row + 1, : values.shape[1]] += values


def scatter_rows(place_ref, total_ref, near_ref, far_ref, start, chunks):
    steps, rows = near_ref.shape[0], near_ref.shape[1]
    width = total_ref.shape[1]
    for core_step, ref in ((0, near_ref), (1, far_ref)):
        for step in range(steps):
            owner = device_of(place_ref, step, core_step)
            for chunk in range(chunks):
                source = pl.multiple_of((owner * chunks + chunk) * rows, rows)
                column = start + chunk * width
                ref[step, :, column : column + width] = total_ref[
                    pl.ds(source, rows), :
                ].astype(BF16)
    return start + chunks * width


def feed_back_kernel(
    count, place_ref, grad_ref, after_ref, slope_ref, att_ref, vec_ref, *refs
):
    piece_refs = refs[:count]
    (
        after_grad_ref, att_grad_ref, small_ref, near_ref, far_ref,
        expand_total, merge_total, merge_ref, expand_ref, reduce_ref,
    ) = refs[count:]
    step = pl.program_id(0)

    @pl.when(step == 0)
    def _():
        assemble(place_ref, feed_layout(expand_ref.shape[1]), piece_refs, refs[-3:])
        expand_total[...] = jnp.zeros_like(expand_total)
        merge_total[...] = jnp.zeros_like(merge_total)
        small_ref[...] = jnp.zeros_like(small_ref)

    grad = grad_ref[...]
    low = grad.astype(BF16)
    add_rows(small_ref, 2, rows_sum(low.astype(F32)))
    pre_grad = (nt(low, reduce_ref[...]) * slope_ref[...].astype(F32)).astype(BF16)
    add_rows(small_ref, 3, rows_sum(pre_grad.astype(F32)))
    hat_value, rstd_value = norm(after_ref[...])
    gain = vec_ref[2:3, :D]
    normed = (hat_value * gain + vec_ref[3:4, :D]).astype(BF16)
    expand_total[...] += tn(normed, pre_grad)
    normed_grad = nt(pre_grad, expand_ref[...])
    add_rows(small_ref, 0, rows_sum(normed_grad * hat_value))
    add_rows(small_ref, 1, rows_sum(normed_grad))
    after_grad = grad + norm_back(normed_grad, hat_value, rstd_value, gain)
    after_grad_ref[...] = after_grad
    merge_grad = after_grad.astype(BF16)
    merge_total[...] += tn(att_ref[...], merge_grad)
    att_grad_ref[...] = nt(merge_grad, merge_ref[...]).astype(BF16)

    @pl.when(step == pl.num_programs(0) - 1)
    def _():
        start = scatter_rows(place_ref, expand_total, near_ref, far_ref, 0, 1)
        scatter_rows(place_ref, merge_total, near_ref, far_ref, start, 1)


def feed_back(place, grad, after_attn, slope, attended, vec, pieces):
    count = grad.shape[0]
    ff = vec.shape[1]
    devices = len(pieces)

    def rows(width):
        return pl.BlockSpec((ROWS, width), lambda i: (i, 0))

    packed = (devices // 2, D // devices, ff + D)
    return pl.pallas_call(
        functools.partial(feed_back_kernel, devices),
        grid=(count // ROWS,),
        in_specs=[scalars(), rows(D), rows(D), rows(ff), rows(D), whole(vec.shape)]
        + [whole(piece.shape) for piece in pieces],
        out_specs=[rows(D), rows(D), whole((8, ff)), whole(packed), whole(packed)],
        out_shape=[
            shape((count, D), F32),
            shape((count, D), BF16),
            shape((8, ff), F32),
            shape(packed, BF16),
            shape(packed, BF16),
        ],
        scratch_shapes=[
            pltpu.VMEM((D, ff), F32),
            pltpu.VMEM((D, D), F32),
        ]
        + feed_scratch(ff),
        compiler_params=params(1),
        cost_estimate=cost(6 * count * D * (ff + D // 2), 12 * count * ff),
        name="feed_back",
    )(place, grad, after_attn, slope, attended, vec, *pieces)


def chosen_rows(ids, slot, rows):
    place = lax.broadcasted_iota(jnp.int32, (ids.shape[0], SEG), 1)
    return nn(jnp.where(ids[:, slot : slot + 1] == place, 1.0, 0.0).astype(BF16), rows)


def ids_down(ids):
    return jnp.concatenate([ids] * 2, axis=0).T


def take_kernel(place_ref, ids_ref, rows_ref, out_ref):
    ids = ids_down(ids_ref[0] - place_ref[1] * SEG)
    rows = rows_ref[0]
    for slot in range(K):
        out_ref[0, slot] = chosen_rows(ids, slot, rows).astype(BF16)


def take(place, ids, rows):
    batch = ids.shape[0]
    return pl.pallas_call(
        take_kernel,
        grid=(batch,),
        in_specs=[
            scalars(),
            pl.BlockSpec((1, K, SEG), lambda b: (b, 0, 0)),
            pl.BlockSpec((1, SEG, D), lambda b: (b, 0, 0)),
        ],
        out_specs=pl.BlockSpec((1, K, SEG, D), lambda b: (b, 0, 0, 0)),
        out_shape=shape((batch, K, SEG, D), BF16),
        compiler_params=params(1),
        cost_estimate=cost(2 * batch * K * SEG * SEG * D, 4 * batch * K * SEG * D),
        name="take",
    )(place, ids, rows)


def give_kernel(distances, started, place_ref, ids_ref, grad_ref, *refs):
    out_refs = refs[started:]
    place = lax.broadcasted_iota(jnp.int32, (SEG, SEG), 0)
    for index, distance in enumerate(distances):
        ids = ids_ref[0] - (place_ref[1] - distance) * SEG
        total = None
        for slot in range(K):
            chosen = jnp.where(ids[slot : slot + 1, :] == place, 1.0, 0.0).astype(BF16)
            part = nn(chosen, grad_ref[0, slot])
            total = part if total is None else total + part
        if started and index == 0:
            total = total + refs[0][0].astype(F32)
        out_refs[index][0] = total.astype(out_refs[index].dtype)


def give(place, ids, grads, arrived, distances):
    batch = ids.shape[0]
    block = pl.BlockSpec((1, SEG, D), lambda b: (b, 0, 0))
    started = arrived is not None
    work = len(distances) * batch * K * SEG * D
    return pl.pallas_call(
        functools.partial(give_kernel, distances, started),
        grid=(batch,),
        in_specs=[
            scalars(),
            pl.BlockSpec((1, K, SEG), lambda b: (b, 0, 0)),
            pl.BlockSpec((1, K, SEG, D), lambda b: (b, 0, 0, 0)),
        ]
        + [block] * started,
        out_specs=[block] * len(distances),
        out_shape=[shape((batch, SEG, D), BF16 if d else F32) for d in distances],
        compiler_params=params(1),
        cost_estimate=cost(2 * work * SEG, 2 * work),
        name="give",
    )(place, ids, grads, *([arrived] if started else []))


def near_kernel(
    hops, count, place_ref, ids_ref, rows_ref, after_ref, grad_ref, vec_ref, *refs
):
    state_refs = refs[:hops]
    piece_refs = refs[hops : hops + count]
    (
        out_ref, row_grad_ref, after_grad_ref, small_ref, near_ref, far_ref,
        keys_total, merge_total, query_total, nq_ref, keys_ref, merge_ref,
    ) = refs[hops + count :]
    first = (pl.program_id(0) == 0) & (pl.program_id(1) == 0)
    last = (pl.program_id(0) == pl.num_programs(0) - 1) & (
        pl.program_id(1) == pl.num_programs(1) - 1
    )

    @pl.when(first)
    def _():
        keys_total[...] = jnp.zeros_like(keys_total)
        merge_total[...] = jnp.zeros_like(merge_total)
        query_total[...] = jnp.zeros_like(query_total)
        assemble(place_ref, ((1, D), (1, 2 * D), (1, D)), piece_refs, refs[-3:])
        small_ref[...] = jnp.zeros_like(small_ref)

    row = lax.broadcasted_iota(jnp.int32, (D, D), 0)
    column = lax.broadcasted_iota(jnp.int32, (D, D), 1)
    same_head = jnp.where(
        lax.shift_right_logical(row, 6) == lax.shift_right_logical(column, 6), 1.0, 0.0
    ).astype(BF16)
    scale = HD**-0.5
    after_ffn = after_ref[0]
    hidden_low = after_ffn.astype(BF16)
    query_float = nn(hidden_low, nq_ref[...]).astype(BF16).astype(F32)
    taken = []
    for slot in range(K):
        total = rows_ref[0, slot].astype(F32)
        for hop in range(hops):
            ids = ids_down(ids_ref[0] - (place_ref[1] - hop - 1) * SEG)
            total = total + chosen_rows(ids, slot, state_refs[hop][0])
        taken.append(total.astype(BF16))
    pairs = [nn(rows, keys_ref[...]).astype(BF16) for rows in taken]
    near_key = [pair[:, :D].astype(F32) for pair in pairs]
    near_value = [pair[:, D:].astype(F32) for pair in pairs]
    scores = [nn((query_float * key).astype(BF16), same_head) * scale for key in near_key]
    top = functools.reduce(jnp.maximum, scores)
    weights = [jnp.exp(score - top) for score in scores]
    inverse = 1.0 / functools.reduce(jnp.add, weights)
    probs = [weight * inverse for weight in weights]
    mixed = functools.reduce(jnp.add, [p * v for p, v in zip(probs, near_value)]).astype(BF16)
    near_out = nn(mixed, merge_ref[...])
    gate_vector = vec_ref[5:6, :D]
    gate = jax.nn.sigmoid(jnp.sum(after_ffn * gate_vector, axis=-1, keepdims=True))
    out_ref[0] = (gate * after_ffn + (1.0 - gate) * near_out).astype(BF16)
    grad = grad_ref[0].astype(F32)
    gate_grad = (
        jnp.sum(grad * (after_ffn - near_out), axis=-1, keepdims=True) * gate * (1.0 - gate)
    )
    add_rows(small_ref, 0, rows_sum(gate_grad * after_ffn))
    near_grad = ((1.0 - gate) * grad).astype(BF16)
    merge_total[...] += tn(mixed, near_grad)
    mixed_grad = nt(near_grad, merge_ref[...]).astype(BF16).astype(F32)
    prob_grads = [nn((mixed_grad * value).astype(BF16), same_head) for value in near_value]
    inner = functools.reduce(jnp.add, [p * g for p, g in zip(probs, prob_grads)])
    query_grad = None
    for slot in range(K):
        score_grad = probs[slot] * (prob_grads[slot] - inner) * scale
        part = score_grad * near_key[slot]
        query_grad = part if query_grad is None else query_grad + part
        pair_grad = jnp.concatenate(
            [(score_grad * query_float).astype(BF16), (probs[slot] * mixed_grad).astype(BF16)],
            axis=1,
        )
        keys_total[...] += tn(taken[slot], pair_grad)
        row_grad_ref[0, slot] = nt(pair_grad, keys_ref[...]).astype(BF16)
    query_grad = query_grad.astype(BF16)
    query_total[...] += tn(hidden_low, query_grad)
    after_grad_ref[0] = gate * grad + gate_grad * gate_vector + nt(query_grad, nq_ref[...])

    @pl.when(last)
    def _():
        start = scatter_rows(place_ref, query_total, near_ref, far_ref, 0, 1)
        start = scatter_rows(place_ref, keys_total, near_ref, far_ref, start, 1)
        scatter_rows(place_ref, merge_total, near_ref, far_ref, start, 1)


def near(place, ids, rows, states, after_ffn, grad, vec, pieces):
    batch = rows.shape[0]
    devices = len(pieces)
    row_block = pl.BlockSpec((1, K, ROWS, D), lambda b, i: (b, 0, i, 0))
    block = pl.BlockSpec((1, ROWS, D), lambda b, i: (b, i, 0))
    packed = (devices // 2, D // devices, 4 * D)
    count = batch * SEG
    return pl.pallas_call(
        functools.partial(near_kernel, len(states), devices),
        grid=(batch, SEG // ROWS),
        in_specs=[scalars(), pl.BlockSpec((1, K, ROWS), lambda b, i: (b, 0, i))]
        + [row_block, block, block, whole(vec.shape)]
        + [pl.BlockSpec((1, SEG, D), lambda b, i: (b, 0, 0))] * len(states)
        + [whole(piece.shape) for piece in pieces],
        out_specs=[block, row_block, block, whole((8, D)), whole(packed), whole(packed)],
        out_shape=[
            shape((batch, SEG, D), BF16),
            shape((batch, K, SEG, D), BF16),
            shape((batch, SEG, D), F32),
            shape((8, D), F32),
            shape(packed, BF16),
            shape(packed, BF16),
        ],
        scratch_shapes=[
            pltpu.VMEM((D, 2 * D), F32),
            pltpu.VMEM((D, D), F32),
            pltpu.VMEM((D, D), F32),
            pltpu.VMEM((D, D), BF16),
            pltpu.VMEM((D, 2 * D), BF16),
            pltpu.VMEM((D, D), BF16),
        ],
        compiler_params=params(2),
        cost_estimate=cost(
            2 * count * D * D * (11 * K + 6), count * D * (4 * K + 12), count * K * D
        ),
        name="near",
    )(place, ids, rows, after_ffn, grad, vec, *states, *pieces)


def reduce_grad_kernel(place_ref, active_ref, grad_ref, near_ref, far_ref, total):
    step = pl.program_id(0)

    @pl.when(step == 0)
    def _():
        total[...] = jnp.zeros_like(total)

    total[...] += tn(active_ref[...], grad_ref[...].astype(BF16))

    @pl.when(step == pl.num_programs(0) - 1)
    def _():
        scatter_rows(place_ref, total, near_ref, far_ref, 0, total.shape[0] // D)


def reduce_grad(place, devices, active, grad):
    count, ff = active.shape
    packed = (devices // 2, D // devices, ff)
    return pl.pallas_call(
        reduce_grad_kernel,
        grid=(count // ROWS,),
        in_specs=[
            scalars(),
            pl.BlockSpec((ROWS, ff), lambda i: (i, 0)),
            pl.BlockSpec((ROWS, D), lambda i: (i, 0)),
        ],
        out_specs=[whole(packed), whole(packed)],
        out_shape=[shape(packed, BF16), shape(packed, BF16)],
        scratch_shapes=[pltpu.VMEM((ff, D), F32)],
        compiler_params=params(1),
        cost_estimate=cost(2 * count * ff * D, 2 * count * ff),
        name="reduce_grad",
    )(place, active, grad)


def finish_kernel(
    parts, place_ref, x_ref, before_ref, dq_ref, dk_ref, dv_ref, dkm_ref, dvm_ref, grad_ref,
    own_ref, sent_ref, arrived_ref, vec_ref, w_ref, gate_ref, feed_ref, diag_ref, select_ref,
    part_ref, send_ref, near_ref, far_ref,
    w_total, norm_total, small_total,
):
    step = pl.program_id(0)

    @pl.when(step == 0)
    def _():
        w_total[...] = jnp.zeros_like(w_total)
        norm_total[...] = jnp.zeros_like(norm_total)

    gain = vec_ref[0:1, :D]
    shift = vec_ref[1:2, :D]
    hat_value, rstd_value = norm(x_ref[0].astype(F32))
    normed = (hat_value * gain + shift).astype(BF16)
    hat_before, rstd_before = norm(before_ref[0].astype(F32))
    normed_before = (hat_before * gain + shift).astype(BF16)
    w_total[:, :D] += tn(normed, dq_ref[0])
    w_total[:, D : 2 * D] += tn(normed, dk_ref[0]) + tn(normed_before, dkm_ref[0])
    w_total[:, 2 * D :] += tn(normed, dv_ref[0]) + tn(normed_before, dvm_ref[0])
    normed_grad = (
        nt(dq_ref[0], w_ref[:, :D])
        + nt(dk_ref[0], w_ref[:, D : 2 * D])
        + nt(dv_ref[0], w_ref[:, 2 * D :])
    )
    before_grad = nt(dkm_ref[0], w_ref[:, D : 2 * D]) + nt(dvm_ref[0], w_ref[:, 2 * D :])
    add_rows(norm_total, 0, rows_sum(normed_grad * hat_value) + rows_sum(before_grad * hat_before))
    add_rows(norm_total, 1, rows_sum(normed_grad) + rows_sum(before_grad))
    send_ref[0] = (
        sent_ref[0].astype(F32)
        + arrived_ref[0].astype(F32)
        + norm_back(before_grad, hat_before, rstd_before, gain)
    ).astype(BF16)
    part_ref[0] = (
        grad_ref[0] + own_ref[0] + norm_back(normed_grad, hat_value, rstd_value, gain)
    )

    @pl.when(step == pl.num_programs(0) - 1)
    def _():
        devices = small_total.shape[0] // 16
        rows = w_total.shape[0] // devices
        small_total[...] = jnp.zeros_like(small_total)
        lines = [
            norm_total[0:1, :],
            norm_total[1:2, :],
            feed_ref[0:1, :D],
            feed_ref[1:2, :D],
            feed_ref[2:3, :D],
            gate_ref[0:1, :],
            feed_ref[3:4, :],
        ]
        for index, (line, width) in enumerate(zip(lines, parts)):
            for d in range(devices):
                row = 16 * d + index
                small_total[row : row + 1, :width] = line[:, d * width : (d + 1) * width]
        table = lax.dot_general(
            diag_ref[...],
            select_ref[...],
            (((1,), (0,)), ((), ())),
            precision=HIGH,
            preferred_element_type=F32,
        )
        own_buckets = NB // devices
        bucket = lax.broadcasted_iota(jnp.int32, (devices, NB), 1)
        owner = lax.broadcasted_iota(jnp.int32, (devices, NB), 0)
        pieces = []
        for place in range(own_buckets):
            chosen = jnp.where(bucket == owner * own_buckets + place, 1.0, 0.0)
            pieces.append(
                lax.dot_general(
                    chosen,
                    table,
                    (((1,), (1,)), ((), ())),
                    precision=HIGH,
                    preferred_element_type=F32,
                )
            )
        buckets = jnp.concatenate(pieces, axis=1)
        for d in range(devices):
            row = 16 * d + len(parts)
            small_total[row : row + 1, : buckets.shape[1]] = buckets[d : d + 1, :]
        width = small_total.shape[1]
        for core_step, ref in ((0, near_ref), (1, far_ref)):
            for chip_step in range(ref.shape[0]):
                target = device_of(place_ref, chip_step, core_step)
                source = pl.multiple_of(target * rows, rows)
                ref[chip_step, :rows, :] = w_total[pl.ds(source, rows), :].astype(BF16)
                ref[chip_step, rows:, :] = jnp.zeros((16, ref.shape[2]), BF16)
                lines = small_total[pl.ds(pl.multiple_of(target * 16, 16), 16), :]
                ref[chip_step, rows:, :width] = lines.astype(BF16)


def finish(
    place, devices, parts, x, before, pieces, grad, own, sent, arrived, vec, weight, gate,
    feed_small, diag,
):
    batch = x.shape[0]
    block = pl.BlockSpec((1, SEG, D), lambda b: (b, 0, 0))
    packed = (devices // 2, D // devices + 16, 3 * D)
    select = jnp.asarray(backward_selector())
    small_width = -(-max(parts) // 128) * 128
    return pl.pallas_call(
        functools.partial(finish_kernel, parts),
        grid=(batch,),
        in_specs=[scalars()]
        + [block] * 11
        + [whole(w.shape) for w in (vec, weight, gate, feed_small, diag, select)],
        out_specs=[block, block, whole(packed), whole(packed)],
        out_shape=[
            shape((batch, SEG, D), F32),
            shape((batch, SEG, D), BF16),
            shape(packed, BF16),
            shape(packed, BF16),
        ],
        scratch_shapes=[
            pltpu.VMEM((D, 3 * D), F32),
            pltpu.VMEM((8, D), F32),
            pltpu.VMEM((16 * devices, small_width), F32),
        ],
        compiler_params=params(1),
        cost_estimate=cost(20 * batch * SEG * D * D, 30 * batch * SEG * D),
        name="finish",
    )(
        place, x, before, *pieces, grad, own, sent, arrived, vec, weight, gate, feed_small, diag,
        select,
    )


def shift(block, distance):
    count = lax.axis_size("seq")
    return lax.ppermute(block, "seq", [(i, (i + distance) % count) for i in range(count)])


def swap(block, axis, bits):
    count = lax.axis_size(axis)
    return lax.ppermute(block, axis, [(i, i ^ bits) for i in range(count)])


def together(*values):
    return lax.optimization_barrier(values)


def chip_steps():
    steps = list(range(1, lax.axis_size("fsdp") // 2))
    cut = (2 * len(steps) + 2) // 3
    return steps[:cut], steps[cut:]


def from_chips(shard, steps):
    return [swap(shard, "fsdp", 2 * step) for step in steps]


def from_core(pieces):
    return [swap(piece, "fsdp", 1) for piece in pieces]


def core_sums(near_half, arrived):
    return [
        (near_half[step].astype(F32) + arrived[step].astype(F32)).astype(BF16)
        for step in range(near_half.shape[0])
    ]


def to_chips(pieces, steps):
    return [swap(pieces[step], "fsdp", 2 * step) for step in steps]


def chip_sum(pieces):
    return functools.reduce(jnp.add, [piece.astype(F32) for piece in pieces]).astype(BF16)


def segment_steps():
    return [1 << bit for bit in range(lax.axis_size("seq").bit_length() - 1)]


def pair_sum(left, right):
    return (left.astype(F32) + right.astype(F32)).astype(BF16)


def on_device(
    layer_input,
    neighbour_ids,
    out_grad,
    attn_norm_gain,
    attn_norm_bias,
    attn_project,
    attn_merge,
    position_bias,
    ffn_norm_gain,
    ffn_norm_bias,
    ffn_expand,
    expand_bias,
    ffn_reduce,
    reduce_bias,
    near_query,
    near_keys,
    near_merge,
    gate_vector,
):
    batch = layer_input.shape[0]
    count = batch * SEG
    devices = lax.axis_size("fsdp")
    segments = lax.axis_size("seq")
    rows = attn_project.shape[0]
    ff = ffn_expand.shape[1]
    ratio = ff // D

    place = jnp.stack([lax.axis_index("fsdp"), lax.axis_index("seq")]).astype(jnp.int32)
    vectors = [
        attn_norm_gain, attn_norm_bias, ffn_norm_gain, ffn_norm_bias, reduce_bias, gate_vector,
        expand_bias, position_bias,
    ]
    parts = [v.shape[0] for v in vectors[:-1]]
    steps = segment_steps()
    near_steps, far_steps = chip_steps()
    chips = near_steps + far_steps

    attn_shard = pack_first(attn_project, vectors)
    attn_pieces = [attn_shard] + from_chips(attn_shard, chips)
    before = shift(layer_input, 1)
    ids = jnp.swapaxes(neighbour_ids, 1, 2)
    feed_shard = pack(rows, [attn_merge, ffn_expand, ffn_reduce])
    near_shard = pack(rows, [near_query, near_keys, near_merge])
    near_rows = take(place, ids, layer_input)
    near_rows, feed_shard, near_shard, attn_pieces = together(
        near_rows, feed_shard, near_shard, attn_pieces
    )
    feed_pieces = [feed_shard] + from_chips(feed_shard, near_steps)
    attn_w, vec, line, joined, memory = first(
        place, layer_input, before, attn_pieces + from_core(attn_pieces), parts, ff
    )
    joined, memory, before, feed_pieces = together(joined, memory, before, feed_pieces)
    feed_pieces += from_chips(feed_shard, far_steps)
    states = [before]
    if segments > 2:
        states.append(shift(before, 1))
    attended = None
    probs = []
    for part in range(2):
        attended, part_probs = attend(place, joined, memory, line, part * PAIRS, attended)
        probs.append(part_probs)
        if part == 0:
            attended, memory, near_shard, feed_pieces, states = together(
                attended, memory, near_shard, feed_pieces, states
            )
            feed_far = from_core(feed_pieces)
            near_pieces = [near_shard] + from_chips(near_shard, chips)
            if len(states) < segments - 1:
                states.append(shift(states[-1], 1))
    attended, feed_far = together(attended, feed_far)
    feed_pieces += feed_far
    flat_attended = attended.reshape(count, D)
    after_attn, active, slope, after_ffn = feed(
        place, layer_input.reshape(count, D), flat_attended, vec, feed_pieces
    )
    after_ffn, near_pieces = together(after_ffn, near_pieces)
    while len(states) < segments - 1:
        states.append(shift(states[-1], 1))
    near_pieces += from_core(near_pieces)
    output, row_grads, after_grad, gate_small, near_half, far_half = near(
        place, ids, near_rows, states, after_ffn.reshape(batch, SEG, D), out_grad, vec,
        near_pieces,
    )

    near_arrived = swap(far_half, "fsdp", 1)
    (message,) = give(place, ids, row_grads, None, (segments - 1,))
    message, after_grad, row_grads = together(message, after_grad, row_grads)
    arrived = shift(message, -1)
    after_grad = after_grad.reshape(count, D)
    reduce_half, reduce_far = reduce_grad(place, devices, active, after_grad)
    reduce_arrived = swap(reduce_far, "fsdp", 1)
    reduce_half, after_grad, near_arrived = together(reduce_half, after_grad, near_arrived)
    grad_after, att_grad, feed_small, feed_half, feed_far = feed_back(
        place, after_grad, after_attn, slope, flat_attended, vec, feed_pieces
    )
    feed_half, feed_far, att_grad, row_grads, arrived, reduce_arrived = together(
        feed_half, feed_far, att_grad, row_grads, arrived, reduce_arrived
    )
    feed_arrived = swap(feed_far, "fsdp", 1)
    near_sums = core_sums(
        jnp.concatenate([near_half, reduce_half], axis=2),
        jnp.concatenate([near_arrived, reduce_arrived], axis=2),
    )
    near_sums, row_grads = together(near_sums, row_grads)
    near_total = [near_sums[0]] + to_chips(near_sums, chips)
    for distance in range(segments - 2, 1, -1):
        (message,) = give(place, ids, row_grads, arrived, (distance,))
        row_grads, message = together(row_grads, message)
        arrived = shift(message, -1)
    row_grads, feed_arrived = together(row_grads, feed_arrived)
    feed_sums = core_sums(feed_half, feed_arrived)
    sent, own = give(place, ids, row_grads, None, (1, 0))
    att_grad, sent, feed_sums = together(att_grad, sent, feed_sums)
    *pieces, first_diag = attend_back(joined, memory, att_grad.reshape(batch, SEG, D), attended, probs[0], 0, [])
    pieces, near_total = together(pieces, near_total)
    near_low = chip_sum(near_total)
    feed_total = [feed_sums[0]] + to_chips(feed_sums, chips)
    near_pair = (near_low, swap(near_low, "seq", steps[0]))
    *pieces, last_diag = attend_back(
        joined, memory, att_grad.reshape(batch, SEG, D), attended, probs[1], PAIRS, pieces
    )
    pieces, arrived, feed_total, near_pair = together(pieces, arrived, feed_total, near_pair)
    for step in steps[1:]:
        near_low = pair_sum(*near_pair)
        near_pair = (near_low, swap(near_low, "seq", step))
    feed_low = chip_sum(feed_total)
    diag = jnp.concatenate([first_diag.reshape(-1, SPAN), last_diag.reshape(-1, SPAN)], axis=0)
    partial, message, attn_half, attn_far = finish(
        place, devices, parts, layer_input, before, pieces, grad_after.reshape(batch, SEG, D),
        own, sent, arrived, vec, attn_w, gate_small, feed_small, diag,
    )
    partial, message, attn_half, attn_far, near_pair, feed_low = together(
        partial, message, attn_half, attn_far, near_pair, feed_low
    )
    attn_arrived = swap(attn_far, "fsdp", 1)
    last = shift(message, -1)
    feed_pair = (feed_low, swap(feed_low, "seq", steps[0]))
    attn_sums = core_sums(attn_half, attn_arrived)
    attn_total = [attn_sums[0]] + to_chips(attn_sums, chips)
    near_grads = unpack(near_pair, ((1, D), (1, 2 * D), (1, D), (ratio, D)))
    near_grads, attn_total, feed_pair = together(near_grads, attn_total, feed_pair)
    attn_low = chip_sum(attn_total)
    for step in steps[1:]:
        feed_low = pair_sum(*feed_pair)
        feed_pair = (feed_low, swap(feed_low, "seq", step))
    for step in steps[:-1]:
        attn_low = pair_sum(attn_low, swap(attn_low, "seq", step))
    attn_low, last = together(attn_low, last)
    attn_pair = (attn_low, swap(attn_low, "seq", steps[-1]))
    input_grad = partial + last.astype(F32)
    feed_grads = unpack(feed_pair, ((1, ff), (1, D)))
    input_grad, feed_grads, attn_pair = together(input_grad, feed_grads, attn_pair)
    project_grad, *smalls = unpack(attn_pair, ((1, 3 * D),), parts + [position_bias.shape[0]])
    return (
        output,
        input_grad,
        smalls[0],
        smalls[1],
        project_grad,
        feed_grads[1],
        smalls[7],
        smalls[2],
        smalls[3],
        feed_grads[0],
        smalls[6],
        near_grads[3],
        smalls[4],
        *near_grads[:3],
        smalls[5],
    )


def solution(mesh):
    in_specs = (
        P("fsdp", "seq", None),
        P("fsdp", "seq", None),
        P("fsdp", "seq", None),
        P("fsdp"),
        P("fsdp"),
        P("fsdp", None),
        P("fsdp", None),
        P("fsdp"),
        P("fsdp"),
        P("fsdp"),
        P("fsdp", None),
        P("fsdp"),
        P("fsdp", None),
        P("fsdp"),
        P("fsdp", None),
        P("fsdp", None),
        P("fsdp", None),
        P("fsdp"),
    )
    out_specs = (
        P("fsdp", "seq", None),
        P("fsdp", "seq", None),
        P("fsdp"),
        P("fsdp"),
        P("fsdp", None),
        P("fsdp", None),
        P("fsdp"),
        P("fsdp"),
        P("fsdp"),
        P("fsdp", None),
        P("fsdp"),
        P("fsdp", None),
        P("fsdp"),
        P("fsdp", None),
        P("fsdp", None),
        P("fsdp", None),
        P("fsdp"),
    )
    return jax.shard_map(
        on_device, mesh=mesh, in_specs=in_specs, out_specs=out_specs, check_vma=False
    )
```

time: 406 us -> 325 us (0.80)
  blocking collectives: 23.9 us -> 0 us
  local copies, waits for them, and re-layouts: 24.7 us -> 7.21 us
  waiting for transfers between devices: 86.4 us -> 70 us
  starting transfers between devices: 49.7 us -> 35.9 us
  Pallas kernels: 201 us -> 196 us
    ppermute x30 -> x40, waiting for transfers between devices: 86.4 us -> 55.4 us  [swap(): return lax.ppermute(block, axis, [(i, i ^ bits) for i in range(count)])]
    all_gather x1 -> x0, blocking collectives: 23.9 us -> none  [on_device(): small = lax.all_gather(small, 'fsdp', axis=0, tiled=True)]
    ppermute x6, waiting for transfers between devices: 0.02 us -> 14.7 us  [shift(): lax.ppermute(block, 'seq', [(i, (i + distance) % count) for i in range(co...]
    ppermute x6, starting transfers between devices: 15.9 us -> 7.15 us  [shift(): lax.ppermute(block, 'seq', [(i, (i + distance) % count) for i in range(co...]
    pallas_call x19, Pallas kernels: 186 us -> 180 us  [the longest x1 41.4 us: near(): pl.pallas_call(functools.partial(near_kernel, len(states), devices), grid...]
    slice x8 -> x0, local copies, waits for them, and re-layouts: 5.4 us -> none  [the longest x3 1.67 us: on_device(): smalls.append(line[start:start + width])]
    ppermute x30 -> x40, starting transfers between devices: 33.7 us -> 28.7 us  [swap(): return lax.ppermute(block, axis, [(i, i ^ bits) for i in range(count)])]
    concatenate x3 -> x2, local copies, waits for them, and re-layouts: 4.96 us -> 0.25 us  [the longest x1 0.18 us: on_device(): jnp.concatenate([near_half, reduce_half], axis=2)]
  transfers between devices with their start and end apart: 36 -> 46, of which waited for: 15 -> 21; matrix products, arithmetic and copies ran while one was open for 6% -> 3% of each run, Pallas kernels for 41% -> 48%
where the time goes in v2:
time: 325 us; the launch traced here: 320 us
  Pallas kernels  196 us (60%)
  waiting for transfers between devices  70 us (22%)
  starting transfers between devices  35.9 us (11%)
  other arithmetic  9.04 us (3%)
  local copies, waits for them, and re-layouts  7.21 us (2%)
    ppermute x40, waiting for transfers between devices, swap(): return lax.ppermute(block, axis, [(i, i ^ bits) for i in range(count)])  55.4 us
    pallas_call x1, Pallas kernels, near(): pl.pallas_call(functools.partial(near_kernel, len(states), devices), grid...  41.4 us
    ppermute x40, starting transfers between devices, swap(): return lax.ppermute(block, axis, [(i, i ^ bits) for i in range(count)])  28.7 us
    pallas_call x2, Pallas kernels, attend_back(): pl.pallas_call(attend_back_kernel, grid=(PAIRS, batch), in_specs=[lanes(0...  27.3 us
    pallas_call x1, Pallas kernels, feed_back(): pl.pallas_call(functools.partial(feed_back_kernel, devices), grid=(count...  26.3 us
    pallas_call x2, Pallas kernels, attend(): pl.pallas_call(functools.partial(attend_kernel, first), grid=(PAIRS, batc...  24.2 us
    pallas_call x3, Pallas kernels, give(): pl.pallas_call(functools.partial(give_kernel, distances, started), grid=(...  17.3 us
    pallas_call x1, Pallas kernels, finish(): pl.pallas_call(functools.partial(finish_kernel, parts), grid=(batch,), in...  16 us
  transfers between devices with their start and end apart: 46, of which 21 were waited for; matrix products, arithmetic and copies ran while one was open for 3% of the time, Pallas kernels for 48%

profile of v2, /device:TPU:0, one launch (start us, length us, event | category | flops | bytes accessed | tf_op | source)
XLA Modules:
  0.0 319.6 jit_solution(16643323761108861351)
XLA Ops:
  0.7 3.1 collective-permute-start.3
  3.7 1.7 pack_first.1.refs_0_
  5.5 2.4 collective-permute-start.2
  8.9 1.7 pack.3.refs_3_
  10.6 1.9 pack.2.refs_0_
  13.1 5.7 %take.1.rows_ref = bf16[2,4,512,512]{3,2,1,0:T(8,128)(2,1)} custom-call(s32[2]{0:T(128)} %pad_add_fusion.place_ref, s32[2,4,512]{2,1,0:T(4,128)} %bitcast.42, bf16[2,512,512]{2,1,0:T(8,128)(2,1)} %x_ref.3), custom_call_target="tpu_custom_call" | custom-call | flops 71582784 | bytes 279620 | tf_op jit(solution)/shard_map/take/pallas_call | solution.py:632
  19.4 1.5 collective-permute-start.9
  20.9 1.1 collective-permute-start.8
  22.5 1.0 collective-permute-done.4.refs_4_
  24.0 1.0 collective-permute-done.6.refs_6_
  25.3 3.8 %collective-permute-done.3.before_ref.refs_0_ = bf16[2,512,512]{2,1,0:T(8,128)(2,1)S(1)} collective-permute-done((bf16[2,512,512]{2,1,0:T(8,128)(2,1)}, bf16[2,512,512]{2,1,0:T(8,128)(2,1)S(1)}, u32[]{:S(2)}, u32[]{:S(2)}) %collective-permute-start.3) | collective-permute-done | bytes 1048608 | tf_op jit(solution)/shard_map/ppermute | solution.py:973
  29.2 1.0 copy-done
  30.2 7.1 %first.1 = (bf16[512,1536]{1,0:T(8,128)(2,1)}, f32[8,2048]{1,0:T(8,128)}, f32[8,1152]{1,0:T(8,128)}, bf16[2,512,1536]{2,1,0:T(8,128)(2,1)}, bf16[2,512,1024]{2,1,0:T(8,128)(2,1)}) custom-call(s32[2]{0:T(128)} %pad_add_fusion.place_ref, bf16[2,512,512]{2,1,0:T(8,128)(2,1)} %x_ref.3, bf16[2,512,512]{2,1,0:T(8,128)(2,1)} %copy-done, ...), custom_call_target="tpu_custom_call" | custom-call | flops 89478488 | bytes 139810 | tf_op jit(solution)/shard_map/first/pallas_call | solution.py:258
  37.4 2.5 collective-permute-start.10
  39.9 12.1 %attend.2 = (bf16[2,512,512]{2,1,0:T(8,128)(2,1)}, bf16[2,4,1024,512]{3,2,1,0:T(8,128)(2,1)}) custom-call(s32[2]{0:T(128)} %pad_add_fusion.place_ref, bf16[2,512,1536]{2,1,0:T(8,128)(2,1)} %get-tuple-element.188.q_ref.k_ref.v_ref, bf16[2,512,1536]{2,1,0:T(8,128)(2,1)} %get-tuple-element.188.q_ref.k_ref.v_ref, ...), custom_call_target="tpu_custom_call" | custom-call | flops 143165568 | bytes 419430 | tf_op jit(solution)/shard_map/attend/pallas_call | solution.py:348
  51.9 0.9 collective-permute-done.10.refs_3_
  52.8 10.9 %collective-permute-done.11.refs_1_ = bf16[2,512,512]{2,1,0:T(8,128)(2,1)S(1)} collective-permute-done((bf16[2,512,512]{2,1,0:T(8,128)(2,1)}, bf16[2,512,512]{2,1,0:T(8,128)(2,1)S(1)}, u32[]{:S(2)}, u32[]{:S(2)}) %collective-permute-start.11) | collective-permute-done | bytes 1048608 | tf_op jit(solution)/shard_map/ppermute | solution.py:973
  65.0 0.7 collective-permute-done.12.refs_4_
  65.7 2.2 collective-permute-start.18
  68.4 0.9 collective-permute-start.16
  69.3 12.1 %attend.3 = (bf16[2,512,512]{2,1,0:T(8,128)(2,1)}, bf16[2,4,1024,512]{3,2,1,0:T(8,128)(2,1)}) custom-call(s32[2]{0:T(128)} %pad_add_fusion.place_ref, bf16[2,512,1536]{2,1,0:T(8,128)(2,1)} %get-tuple-element.188.q_ref.k_ref.v_ref, bf16[2,512,1536]{2,1,0:T(8,128)(2,1)} %get-tuple-element.188.q_ref.k_ref.v_ref, ...), custom_call_target="tpu_custom_call", output_to_operand_aliasing={{0}: (7, {})} | custom-call | flops 143165568 | bytes 419430 | tf_op jit(solution)/shard_map/attend/pallas_call | solution.py:348
  81.5 0.8 copy-done.8
  82.3 12.4 %feed.1 = (f32[1024,512]{1,0:T(8,128)}, bf16[1024,2048]{1,0:T(8,128)(2,1)}, bf16[1024,2048]{1,0:T(8,128)(2,1)}, f32[1024,512]{1,0:T(8,128)}) custom-call(s32[2]{0:T(128)} %pad_add_fusion.place_ref, bf16[1024,512]{1,0:T(8,128)(2,1)} %bitcast.35, bf16[1024,512]{1,0:T(8,128)(2,1)} %bitcast.33, f32[8,2048]{1,0:T(8,128)} %get-tuple-element.205.vec_ref, ...), custom_call_target="tpu_custom_call" | custom-call | flops 178956976 | bytes 838860 | tf_op jit(solution)/shard_map/feed/pallas_call | solution.py:502
  98.6 41.4 %near.1 = (bf16[2,512,512]{2,1,0:T(8,128)(2,1)}, bf16[2,4,512,512]{3,2,1,0:T(8,128)(2,1)}, f32[2,512,512]{2,1,0:T(8,128)}, f32[8,512]{1,0:T(8,128)}, bf16[4,64,2...) custom-call(s32[2]{0:T(128)} %pad_add_fusion.place_ref, s32[2,4,512]{2,1,0:T(4,128)} %bitcast.43, ...), custom_call_target="tpu_custom_call" | custom-call | flops 894784832 | bytes 489335 | tf_op jit(solution)/shard_map/near/pallas_call | solution.py:775
  140.2 4.9 %give.3 = bf16[2,512,512]{2,1,0:T(8,128)(2,1)} custom-call(s32[2]{0:T(128)} %pad_add_fusion.place_ref, s32[2,4,512]{2,1,0:T(4,128)} %bitcast.44, bf16[2,4,512,512]{3,2,1,0:T(8,128)(2,1)} %get-tuple-element.245.grad_ref), custom_call_target="tpu_custom_call" | custom-call | flops 71582784 | bytes 139810 | tf_op jit(solution)/shard_map/give/pallas_call | solution.py:668
  145.2 7.0 %reduce_grad.1 = (bf16[4,64,2048]{2,1,0:T(8,128)(2,1)}, bf16[4,64,2048]{2,1,0:T(8,128)(2,1)}) custom-call(s32[2]{0:T(128)} %pad_add_fusion.place_ref, bf16[1024,2048]{1,0:T(8,128)(2,1)} %get-tuple-element.220.active_ref, f32[1024,512]{1,0:T(8,128)} %bitcast.36), custom_call_target="tpu_custom_call" | custom-call | flops 71582784 | bytes 139810 | tf_op jit(solution)/shard_map/reduce_grad/pallas_call | solution.py:824
  152.5 2.7 collective-permute-start.25
  155.4 26.3 %feed_back.1 = (f32[1024,512]{1,0:T(8,128)}, bf16[1024,512]{1,0:T(8,128)(2,1)}, f32[8,2048]{1,0:T(8,128)}, bf16[4,64,2560]{2,1,0:T(8,128)(2,1)}, bf16[4,64,2560]{2,1,0:T(8,128)(2,1)}) custom-call(s32[2]{0:T(128)} %pad_add_fusion.place_ref, f32[1024,512]{1,0:T(8,128)} %bitcast.37, f32[1024,512]{1,0:T(8,128)} %get-tuple-element.227.after_ref, ...), custom_call_target="tpu_custom_call" | custom-call | flops 241591904 | bytes 838860 | tf_op jit(solution)/shard_map/feed_back/pallas_call | solution.py:590
  182.0 0.7 copy-done.16
  182.8 0.8 fusion.3
  183.6 5.0 %give.4 = bf16[2,512,512]{2,1,0:T(8,128)(2,1)} custom-call(s32[2]{0:T(128)} %pad_add_fusion.place_ref, s32[2,4,512]{2,1,0:T(4,128)} %bitcast.45, bf16[2,4,512,512]{3,2,1,0:T(8,128)(2,1)} %get-tuple-element.245.grad_ref, bf16[2,512,512]{2,1,0:T(8,128)(2,1)} %copy-done.16), custom_call_target="tpu_custom_call" | custom-call | flops 71582784 | bytes 139810 | tf_op jit(solution)/shard_map/give/pallas_call | solution.py:668
  188.6 1.2 collective-permute-start.28
  189.9 1.5 collective-permute-start.29
  191.4 0.7 collective-permute-start.30
  192.1 0.8 collective-permute-start.31
  192.9 7.3 %give.5 = (bf16[2,512,512]{2,1,0:T(8,128)(2,1)}, f32[2,512,512]{2,1,0:T(8,128)}) custom-call(s32[2]{0:T(128)} %pad_add_fusion.place_ref, s32[2,4,512]{2,1,0:T(4,128)} %bitcast.46, bf16[2,4,512,512]{3,2,1,0:T(8,128)(2,1)} %get-tuple-element.245.grad_ref), custom_call_target="tpu_custom_call" | custom-call | flops 143165568 | bytes 279620 | tf_op jit(solution)/shard_map/give/pallas_call | solution.py:668
  200.2 1.1 fusion.7
  201.3 13.7 %attend_back.2 = (bf16[2,512,512]{2,1,0:T(8,128)(2,1)}, bf16[2,512,512]{2,1,0:T(8,128)(2,1)}, bf16[2,512,512]{2,1,0:T(8,128)(2,1)}, bf16[2,512,512]{2,1,0:T(8,12...) custom-call(bf16[2,512,1536]{2,1,0:T(8,128)(2,1)} %get-tuple-element.188.q_ref.k_ref.v_ref, ...), custom_call_target="tpu_custom_call" | custom-call | flops 286331168 | bytes 419430 | tf_op jit(solution)/shard_map/attend_back/pallas_call | solution.py:446
  215.3 1.3 collective-permute-start.35
  216.6 1.2 collective-permute-start.32
  217.8 1.5 collective-permute-start.33
  219.4 0.7 collective-permute-start.34
  220.1 13.7 %attend_back.3 = (bf16[2,512,512]{2,1,0:T(8,128)(2,1)}, bf16[2,512,512]{2,1,0:T(8,128)(2,1)}, bf16[2,512,512]{2,1,0:T(8,128)(2,1)}, bf16[2,512,512]{2,1,0:T(8,12...) custom-call(bf16[2,512,1536]{2,1,0:T(8,128)(2,1)} %get-tuple-element, ...), custom_call_target="tpu_custom_call", output_to_operand_aliasing={{0}: (8, {}), {1}: (9, {}), {2}: (10, {}), {3}: (11, {}), {... | custom-call | flops 286331168 | bytes 419430 | tf_op jit(solution)/shard_map/attend_back/pallas_call | solution.py:446
  233.8 0.7 reshape.114
  235.2 0.7 copy-done.25
  236.4 16.0 %finish.1 = (f32[2,512,512]{2,1,0:T(8,128)}, bf16[2,512,512]{2,1,0:T(8,128)(2,1)}, bf16[4,80,1536]{2,1,0:T(8,128)(2,1)}, bf16[4,80,1536]{2,1,0:T(8,128)(2,1)}) custom-call(s32[2]{0:T(128)} %pad_add_fusion.place_ref, bf16[2,512,512]{2,1,0:T(8,128)(2,1)} %x_ref.3, bf16[2,512,512]{2,1,0:T(8,128)(2,1)} %copy-done, ...), custom_call_target="tpu_custom_call" | custom-call | flops 178956976 | bytes 524288 | tf_op jit(solution)/shard_map/finish/pallas_call | solution.py:944
  252.6 7.3 %collective-permute-done.36.refs_1_ = bf16[64,4096]{1,0:T(8,128)(2,1)S(1)} collective-permute-done((bf16[64,4096]{1,0:T(8,128)(2,1)S(1)}, bf16[64,4096]{1,0:T(8,128)(2,1)S(1)}, u32[]{:S(2)}, u32[]{:S(2)}) %collective-permute-start.36) | collective-permute-done | bytes 524320 | tf_op jit(solution)/shard_map/ppermute | solution.py:978
  259.9 2.8 collective-permute-done.37
  262.7 1.0 fusion.11
  263.7 2.2 collective-permute-start.40
  266.4 0.8 collective-permute-start.38
  267.5 2.2 unpack.3
  269.7 0.7 collective-permute-done.41
  270.4 3.3 %collective-permute-done.40 = bf16[80,1536]{1,0:T(8,128)(2,1)} collective-permute-done((bf16[80,1536]{1,0:T(8,128)(2,1)}, bf16[80,1536]{1,0:T(8,128)(2,1)}, u32[]{:S(2)}, u32[]{:S(2)}) %collective-permute-start.40) | collective-permute-done | bytes 245792 | tf_op jit(solution)/shard_map/ppermute | solution.py:978
  273.7 4.4 %collective-permute-done.39 = bf16[80,1536]{1,0:T(8,128)(2,1)} collective-permute-done((bf16[80,1536]{1,0:T(8,128)(2,1)}, bf16[80,1536]{1,0:T(8,128)(2,1)}, u32[]{:S(2)}, u32[]{:S(2)}) %collective-permute-start.39) | collective-permute-done | bytes 245792 | tf_op jit(solution)/shard_map/ppermute | solution.py:978
  278.2 1.3 add_convert_fusion.13
  279.7 0.9 collective-permute-start.44
  280.6 24.2 %collective-permute-done.42 = bf16[80,1536]{1,0:T(8,128)(2,1)S(1)} collective-permute-done((bf16[80,1536]{1,0:T(8,128)(2,1)S(1)}, bf16[80,1536]{1,0:T(8,128)(2,1)S(1)}, u32[]{:S(2)}, u32[]{:S(2)}) %collective-permute-start.42) | collective-permute-done | bytes 245792 | tf_op jit(solution)/shard_map/ppermute | solution.py:978
  305.0 2.9 convert_add_fusion
  307.9 0.7 copy-done.24
  308.6 2.0 unpack.4
  310.6 6.2 %collective-permute-done.45.refs_1_ = bf16[80,1536]{1,0:T(8,128)(2,1)S(1)} collective-permute-done((bf16[80,1536]{1,0:T(8,128)(2,1)S(1)}, bf16[80,1536]{1,0:T(8,128)(2,1)S(1)}, u32[]{:S(2)}, u32[]{:S(2)}) %collective-permute-start.45) | collective-permute-done | bytes 245792 | tf_op jit(solution)/shard_map/ppermute | solution.py:978
  316.8 0.7 copy-done.42
  317.5 1.9 unpack.5
  (155 shorter events, 13.0 us)
Async XLA Ops:
  0.7 28.5 %collective-permute-start.3 = (bf16[2,512,512]{2,1,0:T(8,128)(2,1)}, bf16[2,512,512]{2,1,0:T(8,128)(2,1)S(1)}, u32[]{:S(2)}, u32[]{:S(2)}) collective-permute-start(bf16[2,512,512]{2,1,0:T(8,128)(2,1)} %x_ref.3), channel_id=1, source_target_pairs={{0,1},{1,2},{2,3},{3,0},{4,5},{5,6},{6,7},{7,4},{8,9},{9,10},{10,1... | collective-permute-start | bytes 3145736 | tf_op jit(solution)/shard_map/ppermute | solution.py:973
  5.5 13.4 %collective-permute-start.2 = (bf16[80,1536]{1,0:T(8,128)(2,1)}, bf16[80,1536]{1,0:T(8,128)(2,1)S(1)}, u32[]{:S(2)}, u32[]{:S(2)}) collective-permute-start(bf16[80,1536]{1,0:T(8,128)(2,1)} %pack_first.1.refs_0_), channel_id=1, source_target_pairs={{0,24},{4,28},{8,16},{12,20},{16,8},{20,12},{24,0},{28,4},{1,25},{... | collective-permute-start | bytes 737288 | tf_op jit(solution)/shard_map/ppermute | solution.py:978
  7.9 11.3 %collective-permute-start.1 = (bf16[80,1536]{1,0:T(8,128)(2,1)}, bf16[80,1536]{1,0:T(8,128)(2,1)S(1)}, u32[]{:S(2)}, u32[]{:S(2)}) collective-permute-start(bf16[80,1536]{1,0:T(8,128)(2,1)} %pack_first.1.refs_0_), channel_id=1, source_target_pairs={{0,16},{4,20},{8,24},{12,28},{16,0},{20,4},{24,8},{28,12},{1,17},{... | collective-permute-start | bytes 737288 | tf_op jit(solution)/shard_map/ppermute | solution.py:978
  8.4 10.9 %collective-permute-start = (bf16[80,1536]{1,0:T(8,128)(2,1)}, bf16[80,1536]{1,0:T(8,128)(2,1)S(1)}, u32[]{:S(2)}, u32[]{:S(2)}) collective-permute-start(bf16[80,1536]{1,0:T(8,128)(2,1)} %pack_first.1.refs_0_), channel_id=1, source_target_pairs={{0,8},{4,12},{8,0},{12,4},{16,24},{20,28},{24,16},{28,20},{1,9},{5... | collective-permute-start | bytes 737288 | tf_op jit(solution)/shard_map/ppermute | solution.py:978
  18.8 10.3 %copy-start.36 = (bf16[80,1536]{1,0:T(8,128)(2,1)}, bf16[80,1536]{1,0:T(8,128)(2,1)S(1)}, u32[]{:S(2)}) copy-start(bf16[80,1536]{1,0:T(8,128)(2,1)S(1)} %collective-permute-done.2.refs_3_) | copy-start | bytes 737284
  19.4 17.9 %collective-permute-start.9 = (bf16[64,4608]{1,0:T(8,128)(2,1)S(1)}, bf16[64,4608]{1,0:T(8,128)(2,1)S(1)}, u32[]{:S(2)}, u32[]{:S(2)}) collective-permute-start(bf16[64,4608]{1,0:T(8,128)(2,1)S(1)} %copy-done.1), channel_id=1, source_target_pairs={{0,16},{4,20},{8,24},{12,28},{16,0},{20,4},{24,8},{28,12},{1,17},{... | collective-permute-start | bytes 1769480 | tf_op jit(solution)/shard_map/ppermute | solution.py:978
  20.9 16.4 %collective-permute-start.8 = (bf16[64,4608]{1,0:T(8,128)(2,1)S(1)}, bf16[64,4608]{1,0:T(8,128)(2,1)S(1)}, u32[]{:S(2)}, u32[]{:S(2)}) collective-permute-start(bf16[64,4608]{1,0:T(8,128)(2,1)S(1)} %copy-done.1), channel_id=1, source_target_pairs={{0,8},{4,12},{8,0},{12,4},{16,24},{20,28},{24,16},{28,20},{1,9},{5... | collective-permute-start | bytes 1769480 | tf_op jit(solution)/shard_map/ppermute | solution.py:978
  22.0 1.5 collective-permute-start.4
  22.0 1.9 collective-permute-start.5
  23.5 1.5 collective-permute-start.6
  23.8 1.5 collective-permute-start.7
  37.3 27.0 %copy-start.2 = (bf16[64,4608]{1,0:T(8,128)(2,1)}, bf16[64,4608]{1,0:T(8,128)(2,1)S(1)}, u32[]{:S(2)}) copy-start(bf16[64,4608]{1,0:T(8,128)(2,1)S(1)} %collective-permute-done.9.refs_2_) | copy-start | bytes 1769476
  37.3 26.4 %copy-start.3 = (bf16[64,4608]{1,0:T(8,128)(2,1)}, bf16[64,4608]{1,0:T(8,128)(2,1)S(1)}, u32[]{:S(2)}) copy-start(bf16[64,4608]{1,0:T(8,128)(2,1)S(1)} %collective-permute-done.8.refs_1_) | copy-start | bytes 1769476
  37.3 26.4 %collective-permute-start.11 = (bf16[2,512,512]{2,1,0:T(8,128)(2,1)}, bf16[2,512,512]{2,1,0:T(8,128)(2,1)S(1)}, u32[]{:S(2)}, u32[]{:S(2)}) collective-permute-start(bf16[2,512,512]{2,1,0:T(8,128)(2,1)} %copy-done), channel_id=1, source_target_pairs={{0,1},{1,2},{2,3},{3,0},{4,5},{5,6},{6,7},{7,4},{8,9},{9,10},{10,1... | collective-permute-start | bytes 3145736 | tf_op jit(solution)/shard_map/ppermute | solution.py:973
  37.4 15.4 %collective-permute-start.10 = (bf16[64,4608]{1,0:T(8,128)(2,1)S(1)}, bf16[64,4608]{1,0:T(8,128)(2,1)S(1)}, u32[]{:S(2)}, u32[]{:S(2)}) collective-permute-start(bf16[64,4608]{1,0:T(8,128)(2,1)S(1)} %copy-done.1), channel_id=1, source_target_pairs={{0,24},{4,28},{8,16},{12,20},{16,8},{20,12},{24,0},{28,4},{1,25},{... | collective-permute-start | bytes 1769480 | tf_op jit(solution)/shard_map/ppermute | solution.py:978
  39.9 25.8 %copy-start.17 = (bf16[64,2048]{1,0:T(8,128)(2,1)S(1)}, bf16[64,2048]{1,0:T(8,128)(2,1)}, u32[]{:S(2)}) copy-start(bf16[64,2048]{1,0:T(8,128)(2,1)} %pack.3.refs_3_) | copy-start | bytes 786436
  52.8 28.6 %copy-start.4 = (bf16[64,4608]{1,0:T(8,128)(2,1)}, bf16[64,4608]{1,0:T(8,128)(2,1)S(1)}, u32[]{:S(2)}) copy-start(bf16[64,4608]{1,0:T(8,128)(2,1)S(1)} %collective-permute-done.10.refs_3_) | copy-start | bytes 1769476
  63.7 17.7 %copy-start.14 = (bf16[2,512,512]{2,1,0:T(8,128)(2,1)}, bf16[2,512,512]{2,1,0:T(8,128)(2,1)S(1)}, u32[]{:S(2)}) copy-start(bf16[2,512,512]{2,1,0:T(8,128)(2,1)S(1)} %collective-permute-done.11.refs_1_) | copy-start | bytes 3145732
  63.7 2.0 collective-permute-start.12
  63.7 4.2 %collective-permute-start.13 = (bf16[64,4608]{1,0:T(8,128)(2,1)S(1)}, bf16[64,4608]{1,0:T(8,128)(2,1)S(1)}, u32[]{:S(2)}, u32[]{:S(2)}) collective-permute-start(bf16[64,4608]{1,0:T(8,128)(2,1)S(1)} %collective-permute-done.8.refs_1_), channel_id=1, source_target_pairs={{0,4},{4,0},{8,12},{12,8},{16,20},{20,16},{24,28},{28,24},{1,5},{5... | collective-permute-start | bytes 1769480 | tf_op jit(solution)/shard_map/ppermute | solution.py:978
  64.2 4.2 %collective-permute-start.14 = (bf16[64,4608]{1,0:T(8,128)(2,1)S(1)}, bf16[64,4608]{1,0:T(8,128)(2,1)S(1)}, u32[]{:S(2)}, u32[]{:S(2)}) collective-permute-start(bf16[64,4608]{1,0:T(8,128)(2,1)S(1)} %collective-permute-done.9.refs_2_), channel_id=1, source_target_pairs={{0,4},{4,0},{8,12},{12,8},{16,20},{20,16},{24,28},{28,24},{1,5},{5... | collective-permute-start | bytes 1769480 | tf_op jit(solution)/shard_map/ppermute | solution.py:978
  64.3 33.2 %collective-permute-start.19 = (bf16[2,512,512]{2,1,0:T(8,128)(2,1)S(1)}, bf16[2,512,512]{2,1,0:T(8,128)(2,1)S(1)}, u32[]{:S(2)}, u32[]{:S(2)}) collective-permute-start(bf16[2,512,512]{2,1,0:T(8,128)(2,1)S(1)} %collective-permute-done.11.refs_1_), channel_id=1, source_target_pairs={{0,1},{1,2},{2,3},{3,0},{4,5},{5,6},{6,7},{7,4},{8,9},{9,10},{10,1... | collective-permute-start | bytes 3145736 | tf_op jit(solution)/shard_map/ppermute | solution.py:973
  64.5 17.0 %collective-permute-start.15 = (bf16[64,4608]{1,0:T(8,128)(2,1)S(1)}, bf16[64,4608]{1,0:T(8,128)(2,1)S(1)}, u32[]{:S(2)}, u32[]{:S(2)}) collective-permute-start(bf16[64,4608]{1,0:T(8,128)(2,1)S(1)} %collective-permute-done.10.refs_3_), channel_id=1, source_target_pairs={{0,4},{4,0},{8,12},{12,8},{16,20},{20,16},{24,28},{28,24},{1,5},{5... | collective-permute-start | bytes 1769480 | tf_op jit(solution)/shard_map/ppermute | solution.py:978
  65.7 15.7 %copy-start.5 = (bf16[64,4608]{1,0:T(8,128)(2,1)}, bf16[64,4608]{1,0:T(8,128)(2,1)S(1)}, u32[]{:S(2)}) copy-start(bf16[64,4608]{1,0:T(8,128)(2,1)S(1)} %collective-permute-done.12.refs_4_) | copy-start | bytes 1769476
  65.7 29.0 %collective-permute-start.18 = (bf16[64,2048]{1,0:T(8,128)(2,1)S(1)}, bf16[64,2048]{1,0:T(8,128)(2,1)S(1)}, u32[]{:S(2)}, u32[]{:S(2)}) collective-permute-start(bf16[64,2048]{1,0:T(8,128)(2,1)S(1)} %copy-done.17), channel_id=1, source_target_pairs={{0,24},{4,28},{8,16},{12,20},{16,8},{20,12},{24,0},{28,4},{1,25},{... | collective-permute-start | bytes 786440 | tf_op jit(solution)/shard_map/ppermute | solution.py:978
  67.9 13.5 %copy-start.6 = (bf16[64,4608]{1,0:T(8,128)(2,1)}, bf16[64,4608]{1,0:T(8,128)(2,1)S(1)}, u32[]{:S(2)}) copy-start(bf16[64,4608]{1,0:T(8,128)(2,1)S(1)} %collective-permute-done.13.refs_5_) | copy-start | bytes 1769476
  67.9 26.8 %collective-permute-start.17 = (bf16[64,2048]{1,0:T(8,128)(2,1)S(1)}, bf16[64,2048]{1,0:T(8,128)(2,1)S(1)}, u32[]{:S(2)}, u32[]{:S(2)}) collective-permute-start(bf16[64,2048]{1,0:T(8,128)(2,1)S(1)} %copy-done.17), channel_id=1, source_target_pairs={{0,16},{4,20},{8,24},{12,28},{16,0},{20,4},{24,8},{28,12},{1,17},{... | collective-permute-start | bytes 786440 | tf_op jit(solution)/shard_map/ppermute | solution.py:978
  68.4 13.0 %copy-start.7 = (bf16[64,4608]{1,0:T(8,128)(2,1)}, bf16[64,4608]{1,0:T(8,128)(2,1)S(1)}, u32[]{:S(2)}) copy-start(bf16[64,4608]{1,0:T(8,128)(2,1)S(1)} %collective-permute-done.14.refs_6_) | copy-start | bytes 1769476
  68.4 26.3 %collective-permute-start.16 = (bf16[64,2048]{1,0:T(8,128)(2,1)S(1)}, bf16[64,2048]{1,0:T(8,128)(2,1)S(1)}, u32[]{:S(2)}, u32[]{:S(2)}) collective-permute-start(bf16[64,2048]{1,0:T(8,128)(2,1)S(1)} %copy-done.17), channel_id=1, source_target_pairs={{0,8},{4,12},{8,0},{12,4},{16,24},{20,28},{24,16},{28,20},{1,9},{5... | collective-permute-start | bytes 786440 | tf_op jit(solution)/shard_map/ppermute | solution.py:978
  94.8 1.6 collective-permute-start.20
  94.8 1.9 collective-permute-start.21
  95.3 1.8 collective-permute-start.22
  95.4 2.1 collective-permute-start.23
  140.0 15.4 %collective-permute-start.24 = (bf16[4,64,2048]{2,1,0:T(8,128)(2,1)}, bf16[4,64,2048]{2,1,0:T(8,128)(2,1)S(1)}, u32[]{:S(2)}, u32[]{:S(2)}) collective-permute-start(bf16[4,64,2048]{2,1,0:T(8,128)(2,1)} %get-tuple-element.225), channel_id=1, source_target_pairs={{0,4},{4,0},{8,12},{12,8},{16,20},{20,16},{24,28},{28,24},{1,5},{5... | collective-permute-start | bytes 3145736 | tf_op jit(solution)/shard_map/ppermute | solution.py:978
  145.2 10.1 %copy-start.18 = (bf16[4,64,2048]{2,1,0:T(8,128)(2,1)S(1)}, bf16[4,64,2048]{2,1,0:T(8,128)(2,1)}, u32[]{:S(2)}) copy-start(bf16[4,64,2048]{2,1,0:T(8,128)(2,1)} %get-tuple-element.236) | copy-start | bytes 3145732
  152.2 29.5 %collective-permute-start.26 = (bf16[4,64,2048]{2,1,0:T(8,128)(2,1)}, bf16[4,64,2048]{2,1,0:T(8,128)(2,1)S(1)}, u32[]{:S(2)}, u32[]{:S(2)}) collective-permute-start(bf16[4,64,2048]{2,1,0:T(8,128)(2,1)} %get-tuple-element.234), channel_id=1, source_target_pairs={{0,4},{4,0},{8,12},{12,8},{16,20},{20,16},{24,28},{28,24},{1,5},{5... | collective-permute-start | bytes 3145736 | tf_op jit(solution)/shard_map/ppermute | solution.py:978
  152.5 29.2 %collective-permute-start.25 = (bf16[2,512,512]{2,1,0:T(8,128)(2,1)}, bf16[2,512,512]{2,1,0:T(8,128)(2,1)S(1)}, u32[]{:S(2)}, u32[]{:S(2)}) collective-permute-start(bf16[2,512,512]{2,1,0:T(8,128)(2,1)} %give.3), channel_id=1, source_target_pairs={{0,3},{1,0},{2,1},{3,2},{4,7},{5,4},{6,5},{7,6},{8,11},{9,8},{10,9... | collective-permute-start | bytes 3145736 | tf_op jit(solution)/shard_map/ppermute | solution.py:973
  155.4 26.4 %copy-start.19 = (bf16[4,64,2048]{2,1,0:T(8,128)(2,1)S(1)}, bf16[4,64,2048]{2,1,0:T(8,128)(2,1)}, u32[]{:S(2)}) copy-start(bf16[4,64,2048]{2,1,0:T(8,128)(2,1)} %get-tuple-element.237) | copy-start | bytes 3145732
  181.7 11.1 %collective-permute-start.27 = (bf16[4,64,2560]{2,1,0:T(8,128)(2,1)}, bf16[4,64,2560]{2,1,0:T(8,128)(2,1)S(1)}, u32[]{:S(2)}, u32[]{:S(2)}) collective-permute-start(bf16[4,64,2560]{2,1,0:T(8,128)(2,1)} %get-tuple-element.244), channel_id=1, source_target_pairs={{0,4},{4,0},{8,12},{12,8},{16,20},{20,16},{24,28},{28,24},{1,5},{5... | collective-permute-start | bytes 3932168 | tf_op jit(solution)/shard_map/ppermute | solution.py:978
  188.6 11.5 %copy-start.12 = (bf16[4,64,2560]{2,1,0:T(8,128)(2,1)S(1)}, bf16[4,64,2560]{2,1,0:T(8,128)(2,1)}, u32[]{:S(2)}) copy-start(bf16[4,64,2560]{2,1,0:T(8,128)(2,1)} %get-tuple-element.247) | copy-start | bytes 3932164
  188.6 26.4 %collective-permute-start.28 = (bf16[64,4096]{1,0:T(8,128)(2,1)S(1)}, bf16[64,4096]{1,0:T(8,128)(2,1)S(1)}, u32[]{:S(2)}, u32[]{:S(2)}) collective-permute-start(bf16[64,4096]{1,0:T(8,128)(2,1)S(1)} %get-tuple-element.258), channel_id=1, source_target_pairs={{0,8},{4,12},{8,0},{12,4},{16,24},{20,28},{24,16},{28,20},{1,9},{5... | collective-permute-start | bytes 1572872 | tf_op jit(solution)/shard_map/ppermute | solution.py:978
  189.9 25.1 %collective-permute-start.29 = (bf16[64,4096]{1,0:T(8,128)(2,1)S(1)}, bf16[64,4096]{1,0:T(8,128)(2,1)S(1)}, u32[]{:S(2)}, u32[]{:S(2)}) collective-permute-start(bf16[64,4096]{1,0:T(8,128)(2,1)S(1)} %get-tuple-element.259), channel_id=1, source_target_pairs={{0,16},{4,20},{8,24},{12,28},{16,0},{20,4},{24,8},{28,12},{1,17},{... | collective-permute-start | bytes 1572872 | tf_op jit(solution)/shard_map/ppermute | solution.py:978
  191.4 23.6 %collective-permute-start.30 = (bf16[64,4096]{1,0:T(8,128)(2,1)S(1)}, bf16[64,4096]{1,0:T(8,128)(2,1)S(1)}, u32[]{:S(2)}, u32[]{:S(2)}) collective-permute-start(bf16[64,4096]{1,0:T(8,128)(2,1)S(1)} %get-tuple-element.260), channel_id=1, source_target_pairs={{0,24},{4,28},{8,16},{12,20},{16,8},{20,12},{24,0},{28,4},{1,25},{... | collective-permute-start | bytes 1572872 | tf_op jit(solution)/shard_map/ppermute | solution.py:978
  192.1 43.1 %collective-permute-start.31 = (bf16[2,512,512]{2,1,0:T(8,128)(2,1)}, bf16[2,512,512]{2,1,0:T(8,128)(2,1)S(1)}, u32[]{:S(2)}, u32[]{:S(2)}) collective-permute-start(bf16[2,512,512]{2,1,0:T(8,128)(2,1)} %give.4), channel_id=1, source_target_pairs={{0,3},{1,0},{2,1},{3,2},{4,7},{5,4},{6,5},{7,6},{8,11},{9,8},{10,9... | collective-permute-start | bytes 3145736 | tf_op jit(solution)/shard_map/ppermute | solution.py:973
  215.3 20.0 %collective-permute-start.35 = (bf16[64,4096]{1,0:T(8,128)(2,1)S(1)}, bf16[64,4096]{1,0:T(8,128)(2,1)S(1)}, u32[]{:S(2)}, u32[]{:S(2)}) collective-permute-start(bf16[64,4096]{1,0:T(8,128)(2,1)S(1)} %add_convert_fusion.1), channel_id=1, source_target_pairs={{0,1},{1,0},{2,3},{3,2},{4,5},{5,4},{6,7},{7,6},{8,9},{9,8},{10,11... | collective-permute-start | bytes 1572872 | tf_op jit(solution)/shard_map/ppermute | solution.py:978
  216.6 18.6 %collective-permute-start.32 = (bf16[64,2560]{1,0:T(8,128)(2,1)}, bf16[64,2560]{1,0:T(8,128)(2,1)S(1)}, u32[]{:S(2)}, u32[]{:S(2)}) collective-permute-start(bf16[64,2560]{1,0:T(8,128)(2,1)} %get-tuple-element.273), channel_id=1, source_target_pairs={{0,8},{4,12},{8,0},{12,4},{16,24},{20,28},{24,16},{28,20},{1,9},{5... | collective-permute-start | bytes 983048 | tf_op jit(solution)/shard_map/ppermute | solution.py:978
  217.8 17.3 %collective-permute-start.33 = (bf16[64,2560]{1,0:T(8,128)(2,1)}, bf16[64,2560]{1,0:T(8,128)(2,1)S(1)}, u32[]{:S(2)}, u32[]{:S(2)}) collective-permute-start(bf16[64,2560]{1,0:T(8,128)(2,1)} %get-tuple-element.274), channel_id=1, source_target_pairs={{0,16},{4,20},{8,24},{12,28},{16,0},{20,4},{24,8},{28,12},{1,17},{... | collective-permute-start | bytes 983048 | tf_op jit(solution)/shard_map/ppermute | solution.py:978
  219.4 15.8 %collective-permute-start.34 = (bf16[64,2560]{1,0:T(8,128)(2,1)}, bf16[64,2560]{1,0:T(8,128)(2,1)S(1)}, u32[]{:S(2)}, u32[]{:S(2)}) collective-permute-start(bf16[64,2560]{1,0:T(8,128)(2,1)} %get-tuple-element.275), channel_id=1, source_target_pairs={{0,24},{4,28},{8,16},{12,20},{16,8},{20,12},{24,0},{28,4},{1,25},{... | collective-permute-start | bytes 983048 | tf_op jit(solution)/shard_map/ppermute | solution.py:978
  236.2 16.2 %copy-start.9 = (bf16[64,4096]{1,0:T(8,128)(2,1)}, bf16[64,4096]{1,0:T(8,128)(2,1)S(1)}, u32[]{:S(2)}) copy-start(bf16[64,4096]{1,0:T(8,128)(2,1)S(1)} %add_convert_fusion.refs_0_) | copy-start | bytes 1572868
  236.2 23.7 %collective-permute-start.36 = (bf16[64,4096]{1,0:T(8,128)(2,1)S(1)}, bf16[64,4096]{1,0:T(8,128)(2,1)S(1)}, u32[]{:S(2)}, u32[]{:S(2)}) collective-permute-start(bf16[64,4096]{1,0:T(8,128)(2,1)S(1)} %add_convert_fusion.refs_0_), channel_id=1, source_target_pairs={{0,2},{1,3},{2,0},{3,1},{4,6},{5,7},{6,4},{7,5},{8,10},{9,11},{10,... | collective-permute-start | bytes 1572872 | tf_op jit(solution)/shard_map/ppermute | solution.py:978
  236.4 16.0 %copy-start.26 = (bf16[64,2560]{1,0:T(8,128)(2,1)S(1)}, bf16[64,2560]{1,0:T(8,128)(2,1)}, u32[]{:S(2)}) copy-start(bf16[64,2560]{1,0:T(8,128)(2,1)} %copy-done.25) | copy-start | bytes 983044
  236.4 16.0 %copy-start.28 = (bf16[64,2560]{1,0:T(8,128)(2,1)S(1)}, bf16[64,2560]{1,0:T(8,128)(2,1)}, u32[]{:S(2)}) copy-start(bf16[64,2560]{1,0:T(8,128)(2,1)} %copy-done.27) | copy-start | bytes 983044
  252.4 10.3 %copy-start.21 = (bf16[4,80,1536]{2,1,0:T(8,128)(2,1)S(1)}, bf16[4,80,1536]{2,1,0:T(8,128)(2,1)}, u32[]{:S(2)}) copy-start(bf16[4,80,1536]{2,1,0:T(8,128)(2,1)} %get-tuple-element.311) | copy-start | bytes 2949124
  259.9 2.8 collective-permute-start.37
  259.9 10.5 %collective-permute-start.41 = (bf16[64,2560]{1,0:T(8,128)(2,1)S(1)}, bf16[64,2560]{1,0:T(8,128)(2,1)S(1)}, u32[]{:S(2)}, u32[]{:S(2)}) collective-permute-start(bf16[64,2560]{1,0:T(8,128)(2,1)S(1)} %add_convert_fusion.7), channel_id=1, source_target_pairs={{0,1},{1,0},{2,3},{3,2},{4,5},{5,4},{6,7},{7,6},{8,9},{9,8},{10,11... | collective-permute-start | bytes 983048 | tf_op jit(solution)/shard_map/ppermute | solution.py:978
  263.7 41.3 %copy-start.10 = (f32[2,512,512]{2,1,0:T(8,128)S(1)}, f32[2,512,512]{2,1,0:T(8,128)}, u32[]{:S(2)}) copy-start(f32[2,512,512]{2,1,0:T(8,128)} %get-tuple-element.304) | copy-start | bytes 6291460
  263.7 10.1 %collective-permute-start.40 = (bf16[80,1536]{1,0:T(8,128)(2,1)}, bf16[80,1536]{1,0:T(8,128)(2,1)}, u32[]{:S(2)}, u32[]{:S(2)}) collective-permute-start(bf16[80,1536]{1,0:T(8,128)(2,1)} %get-tuple-element.351), channel_id=1, source_target_pairs={{0,24},{4,28},{8,16},{12,20},{16,8},{20,12},{24,0},{28,4},{1,25},{... | collective-permute-start | bytes 737288 | tf_op jit(solution)/shard_map/ppermute | solution.py:978
  265.9 12.3 %collective-permute-start.39 = (bf16[80,1536]{1,0:T(8,128)(2,1)}, bf16[80,1536]{1,0:T(8,128)(2,1)}, u32[]{:S(2)}, u32[]{:S(2)}) collective-permute-start(bf16[80,1536]{1,0:T(8,128)(2,1)} %get-tuple-element.352), channel_id=1, source_target_pairs={{0,16},{4,20},{8,24},{12,28},{16,0},{20,4},{24,8},{28,12},{1,17},{... | collective-permute-start | bytes 737288 | tf_op jit(solution)/shard_map/ppermute | solution.py:978
  266.4 11.8 %collective-permute-start.38 = (bf16[80,1536]{1,0:T(8,128)(2,1)}, bf16[80,1536]{1,0:T(8,128)(2,1)}, u32[]{:S(2)}, u32[]{:S(2)}) collective-permute-start(bf16[80,1536]{1,0:T(8,128)(2,1)} %get-tuple-element.353), channel_id=1, source_target_pairs={{0,8},{4,12},{8,0},{12,4},{16,24},{20,28},{24,16},{28,20},{1,9},{5... | collective-permute-start | bytes 737288 | tf_op jit(solution)/shard_map/ppermute | solution.py:978
  267.2 37.7 %collective-permute-start.43 = (bf16[2,512,512]{2,1,0:T(8,128)(2,1)}, bf16[2,512,512]{2,1,0:T(8,128)(2,1)}, u32[]{:S(2)}, u32[]{:S(2)}) collective-permute-start(bf16[2,512,512]{2,1,0:T(8,128)(2,1)} %get-tuple-element.318), channel_id=1, source_target_pairs={{0,3},{1,0},{2,1},{3,2},{4,7},{5,4},{6,5},{7,6},{8,11},{9,8},{10,9... | collective-permute-start | bytes 3145736 | tf_op jit(solution)/shard_map/ppermute | solution.py:973
  279.5 25.3 %collective-permute-start.42 = (bf16[80,1536]{1,0:T(8,128)(2,1)S(1)}, bf16[80,1536]{1,0:T(8,128)(2,1)S(1)}, u32[]{:S(2)}, u32[]{:S(2)}) collective-permute-start(bf16[80,1536]{1,0:T(8,128)(2,1)S(1)} %add_convert_fusion.13), channel_id=1, source_target_pairs={{0,1},{1,0},{2,3},{3,2},{4,5},{5,4},{6,7},{7,6},{8,9},{9,8},{10,11... | collective-permute-start | bytes 737288 | tf_op jit(solution)/shard_map/ppermute | solution.py:978
  279.6 28.2 %copy-start.11 = (bf16[64,2560]{1,0:T(8,128)(2,1)}, bf16[64,2560]{1,0:T(8,128)(2,1)S(1)}, u32[]{:S(2)}) copy-start(bf16[64,2560]{1,0:T(8,128)(2,1)S(1)} %add_convert_fusion.6.refs_0_) | copy-start | bytes 983044
  279.7 28.2 %collective-permute-start.44 = (bf16[64,2560]{1,0:T(8,128)(2,1)S(1)}, bf16[64,2560]{1,0:T(8,128)(2,1)S(1)}, u32[]{:S(2)}, u32[]{:S(2)}) collective-permute-start(bf16[64,2560]{1,0:T(8,128)(2,1)S(1)} %add_convert_fusion.6.refs_0_), channel_id=1, source_target_pairs={{0,2},{1,3},{2,0},{3,1},{4,6},{5,7},{6,4},{7,5},{8,10},{9,11},{10,... | collective-permute-start | bytes 983048 | tf_op jit(solution)/shard_map/ppermute | solution.py:978
  304.9 11.9 %collective-permute-start.45 = (bf16[80,1536]{1,0:T(8,128)(2,1)S(1)}, bf16[80,1536]{1,0:T(8,128)(2,1)S(1)}, u32[]{:S(2)}, u32[]{:S(2)}) collective-permute-start(bf16[80,1536]{1,0:T(8,128)(2,1)S(1)} %add_convert_fusion.12.refs_0_), channel_id=1, source_target_pairs={{0,2},{1,3},{2,0},{3,1},{4,6},{5,7},{6,4},{7,5},{8,10},{9,11},{10,... | collective-permute-start | bytes 737288 | tf_op jit(solution)/shard_map/ppermute | solution.py:978
  (27 other events, 89.4 us)
